TPU v7x, 32 devices: a whole 2x2x4 slice. The times are simulated.
32 devices in a mesh: dp: 2 (over y), expert: 16 (over z, x, core).
Axes of the slice: x: 2, y: 2, z: 4, core: 2. Of those that a mesh axis runs over, the one named last changes fastest.
Arguments:
- hidden_in: bfloat16 [4096, 2, 512], P(('dp', 'expert')), may hold values from -6 to 6
- out_grad: bfloat16 [4096, 4096], P(('dp', 'expert')), may hold values from -3 to 3
- expert_ids: int32 [4096, 2], P(('dp', 'expert')), may hold values from 0 to 15, as said below
- gate_num: int32 [4096, 2], P(('dp', 'expert')), may hold values from 1 to 16
- down_weight: bfloat16 [16, 512, 4096], P('expert', 'dp'), may hold values from -0.25 to 0.25
Outputs:
- layer_out: bfloat16 [4096, 4096], P(('dp', 'expert'))
- hidden_grad: bfloat16 [4096, 2, 512], P(('dp', 'expert'))
- down_grad: bfloat16 [16, 512, 4096], P('expert', 'dp')
Inputs may be any that keep to these rules, and one draw needn't show every extreme that they name: `expert_ids`: the 2 experts of a token differ. The 128 tokens of one device name any one expert at most 32 times.
All inputs are finite; a program needn't handle non-finite values.
Results may differ from a plain program's by a relative error of at most 0.0059.
Values may be sent and summed in bfloat16 or wider, within the bound.
No kernel may reach another device: no remote copies, remote signals or barrier semaphores. Data moves between devices by JAX's collectives and lax.ppermute only.
A program may use at most 64 MiB of HBM per device.

v0:
```python
import jax
import jax.numpy as jnp
from jax import lax
from jax.sharding import PartitionSpec as P


def on_device(hidden_in, out_grad, expert_ids, gate_num, down_weight):
    tok_rows = hidden_in.shape[0]
    units = hidden_in.shape[2]
    width = out_grad.shape[1]
    experts = lax.axis_size("expert")
    replicas = lax.axis_size("dp")
    capacity = 4 * tok_rows // experts
    buffer_rows = experts * capacity
    slot_count = 2 * tok_rows
    numerators = gate_num.astype(jnp.float32)
    denominator = jnp.sum(numerators, axis=1, keepdims=True)
    gate_share = numerators / denominator
    scaled = (
        (gate_share[:, :, None] * hidden_in.astype(jnp.float32))
        .astype(jnp.bfloat16)
        .reshape(slot_count, units)
    )
    routed = expert_ids.reshape(slot_count)
    one_hot = (routed[:, None] == jnp.arange(experts, dtype=jnp.int32)[None, :]).astype(jnp.int32)
    ordinal = jnp.sum((jnp.cumsum(one_hot, axis=0) - 1) * one_hot, axis=1)
    target_row = routed * capacity + ordinal
    grad_copies = jnp.broadcast_to(out_grad[:, None, :], (tok_rows, 2, width)).reshape(
        slot_count, width
    )
    gate_pair = jnp.stack([numerators, jnp.broadcast_to(denominator, numerators.shape)], axis=2)
    gate_pair = gate_pair.reshape(slot_count, 2).astype(jnp.bfloat16)
    send_hidden = jnp.zeros((buffer_rows, units), jnp.bfloat16).at[target_row].set(scaled)
    send_grad = jnp.zeros((buffer_rows, width), jnp.bfloat16).at[target_row].set(grad_copies)
    send_gate = jnp.zeros((buffer_rows, 2), jnp.bfloat16).at[target_row].set(gate_pair)
    weight_local = down_weight[0]
    gathered = lax.all_gather(weight_local, "dp", axis=0, tiled=True)
    recv_hidden, recv_gate = (
        lax.all_to_all(send_hidden, "expert", split_axis=0, concat_axis=0, tiled=True),
        lax.all_to_all(send_gate, "expert", split_axis=0, concat_axis=0, tiled=True),
    )
    slot_out = jnp.dot(recv_hidden, gathered, preferred_element_type=jnp.float32).astype(
        jnp.bfloat16
    )
    recv_grad = lax.all_to_all(send_grad, "expert", split_axis=0, concat_axis=0, tiled=True)
    share = recv_gate[:, 0].astype(jnp.float32) / jnp.maximum(
        recv_gate[:, 1].astype(jnp.float32), 1.0
    )
    back_proj = lax.dot_general(
        recv_grad, gathered, (((1,), (1,)), ((), ())), preferred_element_type=jnp.float32
    )
    slot_grad = (share[:, None] * back_proj).astype(jnp.bfloat16)
    grad_part = lax.psum_scatter(
        lax.dot_general(
            recv_hidden, recv_grad, (((0,), (0,)), ((), ())), preferred_element_type=jnp.float32
        ).astype(jnp.bfloat16),
        "dp",
        scatter_dimension=0,
        tiled=True,
    ).astype(jnp.float32)
    back_out, back_grad = (
        lax.all_to_all(slot_out, "expert", split_axis=0, concat_axis=0, tiled=True),
        lax.all_to_all(slot_grad, "expert", split_axis=0, concat_axis=0, tiled=True),
    )
    out_slots = back_out[target_row].reshape(tok_rows, 2, width)
    layer_out = jnp.sum(out_slots.astype(jnp.float32), axis=1).astype(jnp.bfloat16)
    hidden_grad = back_grad[target_row].reshape(tok_rows, 2, units)
    down_grad = (grad_part / replicas).astype(jnp.bfloat16)[None]
    return (layer_out, hidden_grad, down_grad)


def solution(mesh):
    return jax.shard_map(
        on_device,
        mesh=mesh,
        in_specs=(
            P(("dp", "expert"), None, None),
            P(("dp", "expert"), None),
            P(("dp", "expert"), None),
            P(("dp", "expert"), None),
            P("expert", "dp", None),
        ),
        out_specs=(
            P(("dp", "expert"), None),
            P(("dp", "expert"), None, None),
            P("expert", "dp", None),
        ),
        check_vma=False,
    )
```

profile of v0, /device:TPU:11, one launch (start us, length us, event | category | flops | bytes accessed | tf_op | source)
XLA Modules:
  0.0 294.1 jit_solution(7476292417636293528)
XLA Ops:
  7.2 0.8 copy.32
  8.2 0.7 broadcast_multiply_fusion
  8.9 0.7 convert_reduce_fusion
  9.6 0.7 convert_convert_fusion
  10.3 0.6 reduce-window.6
  10.9 0.2 slice_reduce_fusion
  12.2 1.2 scatter_custom_fusion.1
  13.4 0.8 copy.38
  14.2 6.6 %all-to-all-start.2 = ((bf16[16,32,2]{1,2,0:T(2,128)(2,1)}), bf16[16,32,2]{1,2,0:T(2,128)(2,1)S(1)}, u32[]{:S(2)}, u32[]{:S(2)}) async-start(bf16[16,32,2]{1,2,0:T(2,128)(2,1)} %copy.38), calls=%async_computation.2 | async-start | bytes 16384 | tf_op jit(solution)/shard_map/all_to_all | solution.py:40
  20.7 3.3 %broadcast_in_dim.13 = bf16[128,2,4096]{2,1,0:T(2,128)(2,1)S(1)} broadcast(bf16[128,4096]{1,0:T(8,128)(2,1)} %param.6), dimensions={0,2} | broadcast | bytes 3145728 | tf_op jit(solution)/shard_map/broadcast_in_dim | solution.py:28
  24.0 2.2 reshape.129
  26.2 7.0 %scatter_custom_fusion.2 = bf16[512,4096]{1,0:T(8,128)(2,1)} fusion(s32[256]{0:T(256)S(1)} %bitcast.52, bf16[256,4096]{1,0:T(8,128)(2,1)} %reshape.129, bf16[]{:T(256)} %constant.8.clone.1), kind=kCustom, calls=%fused_computation.12 | custom fusion | bytes 4194816 | tf_op jit(solution)/shard_map/scatter | solution.py:34
  33.3 6.2 %all-to-all-start.3 = ((bf16[16,32,4096]{2,1,0:T(8,128)(2,1)}), bf16[16,32,4096]{2,1,0:T(8,128)(2,1)}, u32[]{:S(2)}, u32[]{:S(2)}) async-start(bf16[16,32,4096]{2,1,0:T(8,128)(2,1)} %bitcast.46), calls=%async_computation.3 | async-start | bytes 8388608 | tf_op jit(solution)/shard_map/all_to_all | solution.py:45
  39.5 0.7 all-gather.3.cloned.1.call-update
  40.3 0.3 multiply_convert_fusion.1
  40.7 2.3 scatter_custom_fusion
  43.0 88.9 %all-to-all-done.3 = bf16[16,32,4096]{2,1,0:T(8,128)(2,1)} async-done(((bf16[16,32,4096]{2,1,0:T(8,128)(2,1)}), bf16[16,32,4096]{2,1,0:T(8,128)(2,1)}, u32[]{:S(2)}, u32[]{:S(2)}) %all-to-all-start.3) | async-done | bytes 4194336 | tf_op jit(solution)/shard_map/all_to_all | solution.py:45
  131.9 4.9 %all-to-all-start = ((bf16[16,32,512]{2,1,0:T(8,128)(2,1)}), bf16[16,32,512]{2,1,0:T(8,128)(2,1)S(1)}, u32[]{:S(2)}, u32[]{:S(2)}) async-start(bf16[16,32,512]{2,1,0:T(8,128)(2,1)} %bitcast.3), calls=%async_computation | async-start | bytes 1048576 | tf_op jit(solution)/shard_map/all_to_all | solution.py:39
  137.0 6.6 %fusion.9 = bf16[512,512]{1,0:T(8,128)(2,1)} fusion(bf16[512,4096]{1,0:T(8,128)(2,1)} %bitcast.11, bf16[1,512,4096]{2,1,0:T(8,128)(2,1)} %all-gather.3.cloned.1.call-done, f32[512]{0:T(512)S(1)} %bitcast.56), kind=kOutput, calls=%fused_computation.15 | convolution fusion | flops 2148007936 | bytes 8914944 | tf_op jit(solution)/shard_map/dot_general | solution.py:49
  143.6 6.8 %all-to-all-done = bf16[16,32,512]{2,1,0:T(8,128)(2,1)S(1)} async-done(((bf16[16,32,512]{2,1,0:T(8,128)(2,1)}), bf16[16,32,512]{2,1,0:T(8,128)(2,1)S(1)}, u32[]{:S(2)}, u32[]{:S(2)}) %all-to-all-start) | async-done | bytes 524320 | tf_op jit(solution)/shard_map/all_to_all | solution.py:39
  150.4 5.0 %all-to-all-start.4 = ((bf16[16,32,512]{2,1,0:T(8,128)(2,1)}), bf16[16,32,512]{2,1,0:T(8,128)(2,1)S(1)}, u32[]{:S(2)}, u32[]{:S(2)}) async-start(bf16[16,32,512]{2,1,0:T(8,128)(2,1)} %bitcast.12), calls=%async_computation.4 | async-start | bytes 1048576 | tf_op jit(solution)/shard_map/all_to_all | solution.py:63
  155.4 6.5 %bitcast_convert_fusion = bf16[512,4096]{1,0:T(8,128)(2,1)} fusion(bf16[16,32,512]{2,1,0:T(8,128)(2,1)S(1)} %all-to-all-done, bf16[16,32,4096]{2,1,0:T(8,128)(2,1)} %all-to-all-done.3), kind=kOutput, calls=%fused_computation.5 | convolution fusion | flops 2149580800 | bytes 8912896 | tf_op jit(solution)/shard_map/dot_general | solution.py:54
  161.9 6.5 %convolution_convert_fusion = bf16[512,4096]{1,0:T(8,128)(2,1)} fusion(bf16[512,512]{1,0:T(8,128)(2,1)S(1)} %bitcast.49, bf16[1,512,4096]{2,1,0:T(8,128)(2,1)} %all-gather.3.cloned.1.call-done), kind=kOutput, calls=%fused_computation.6 | convolution fusion | flops 2149580800 | bytes 8912896 | tf_op jit(solution)/shard_map/dot_general | solution.py:42
  168.5 0.5 all-to-all-done.4
  169.0 5.5 %all-to-all-start.1 = ((bf16[16,32,4096]{2,1,0:T(8,128)(2,1)}), bf16[16,32,4096]{2,1,0:T(8,128)(2,1)}, u32[]{:S(2)}, u32[]{:S(2)}) async-start(bf16[16,32,4096]{2,1,0:T(8,128)(2,1)} %bitcast.48), calls=%async_computation.1 | async-start | bytes 8388608 | tf_op jit(solution)/shard_map/all_to_all | solution.py:62
  174.5 1.2 gather_fusion.1
  175.6 0.8 reshape.92
  176.5 90.5 %all-to-all-done.1 = bf16[16,32,4096]{2,1,0:T(8,128)(2,1)} async-done(((bf16[16,32,4096]{2,1,0:T(8,128)(2,1)}), bf16[16,32,4096]{2,1,0:T(8,128)(2,1)}, u32[]{:S(2)}, u32[]{:S(2)}) %all-to-all-start.1) | async-done | bytes 4194336 | tf_op jit(solution)/shard_map/all_to_all | solution.py:62
  266.9 6.6 %gather_fusion = bf16[256,4096]{1,0:T(8,128)(2,1)S(1)} fusion(bf16[512,4096]{1,0:T(8,128)(2,1)} %bitcast.7, s32[1024]{0:T(1024)S(1)} %pad_clamp_fusion), kind=kCustom, calls=%fused_computation | custom fusion | bytes 4195328 | tf_op jit(solution)/shard_map/gather | solution.py:65
  273.6 2.6 reshape.90
  276.2 7.7 %reduce_sum.35 = bf16[128,4096]{1,0:T(8,128)(2,1)} reduce(bf16[128,2,4096]{2,1,0:T(2,128)(2,1)} %reshape.90, bf16[]{:T(256)} %constant.8.clone.1), dimensions={1}, to_apply=%region_5.6 | reduce | flops 524288 | bytes 3145730 | tf_op jit(solution)/shard_map/reduce_sum | solution.py:66
  283.9 3.3 %fusion.3 = bf16[1,256,4096]{2,1,0:T(8,128)(2,1)} fusion(bf16[256,4096]{1,0:T(8,128)(2,1)} %reduce-scatter.2.cloned.1.call-done), kind=kLoop, calls=%fused_computation.11 | loop fusion | flops 3145728 | bytes 4194304 | tf_op jit(solution)/shard_map/broadcast_in_dim | solution.py:68
  (33 shorter events, 1.8 us)
Async XLA Ops:
  14.2 19.1 %all-to-all-start.2 = ((bf16[16,32,2]{1,2,0:T(2,128)(2,1)}), bf16[16,32,2]{1,2,0:T(2,128)(2,1)S(1)}, u32[]{:S(2)}, u32[]{:S(2)}) async-start(bf16[16,32,2]{1,2,0:T(2,128)(2,1)} %copy.38), calls=%async_computation.2 | async-start | bytes 16384 | tf_op jit(solution)/shard_map/all_to_all | solution.py:40
  33.3 6.9 %copy-start.1 = (s32[128,2]{0,1:T(2,128)S(1)}, s32[128,2]{0,1:T(2,128)}, u32[]{:S(2)}) copy-start(s32[128,2]{0,1:T(2,128)} %param.8) | copy-start | bytes 3076
  33.3 7.0 %copy-start = (bf16[128,2,512]{2,1,0:T(2,128)(2,1)S(1)}, bf16[128,2,512]{2,1,0:T(2,128)(2,1)}, u32[]{:S(2)}) copy-start(bf16[128,2,512]{2,1,0:T(2,128)(2,1)} %param.5) | copy-start | bytes 786436
  33.3 98.6 %all-to-all-start.3 = ((bf16[16,32,4096]{2,1,0:T(8,128)(2,1)}), bf16[16,32,4096]{2,1,0:T(8,128)(2,1)}, u32[]{:S(2)}, u32[]{:S(2)}) async-start(bf16[16,32,4096]{2,1,0:T(8,128)(2,1)} %bitcast.46), calls=%async_computation.3 | async-start | bytes 8388608 | tf_op jit(solution)/shard_map/all_to_all | solution.py:45
  39.4 97.5 %all-gather.3.cloned.1.call-start = ((), (), s32[]{:S(2)}) async-start(), calls=%async_computation.7 | async-start | bytes 6291456 | tf_op jit(solution)/shard_map/all_gather | solution.py:37
  131.9 18.5 %all-to-all-start = ((bf16[16,32,512]{2,1,0:T(8,128)(2,1)}), bf16[16,32,512]{2,1,0:T(8,128)(2,1)S(1)}, u32[]{:S(2)}, u32[]{:S(2)}) async-start(bf16[16,32,512]{2,1,0:T(8,128)(2,1)} %bitcast.3), calls=%async_computation | async-start | bytes 1048576 | tf_op jit(solution)/shard_map/all_to_all | solution.py:39
  150.4 18.6 %all-to-all-start.4 = ((bf16[16,32,512]{2,1,0:T(8,128)(2,1)}), bf16[16,32,512]{2,1,0:T(8,128)(2,1)S(1)}, u32[]{:S(2)}, u32[]{:S(2)}) async-start(bf16[16,32,512]{2,1,0:T(8,128)(2,1)} %bitcast.12), calls=%async_computation.4 | async-start | bytes 1048576 | tf_op jit(solution)/shard_map/all_to_all | solution.py:63
  155.4 128.5 %reduce-scatter.2.cloned.1.call-start = ((), (), s32[]{:S(2)}) async-start(), calls=%async_computation.6 | async-start | bytes 6291456 | tf_op jit(solution)/shard_map/reduce_scatter | solution.py:53
  169.0 98.0 %all-to-all-start.1 = ((bf16[16,32,4096]{2,1,0:T(8,128)(2,1)}), bf16[16,32,4096]{2,1,0:T(8,128)(2,1)}, u32[]{:S(2)}, u32[]{:S(2)}) async-start(bf16[16,32,4096]{2,1,0:T(8,128)(2,1)} %bitcast.48), calls=%async_computation.1 | async-start | bytes 8388608 | tf_op jit(solution)/shard_map/all_to_all | solution.py:62
Sparse Core Ops, SparseCore 0:
  41.8 57.3 all-gather.2
  162.1 54.8 reduce-scatter.1
where the time goes:
time: 295 us; the launch traced here: 294 us
  waiting for transfers between devices  187 us (63%)
  local copies, waits for them, and re-layouts  30.5 us (10%)
  starting transfers between devices  28.2 us (10%)
  matrix products  19.6 us (7%)
  between operations  14.2 us (5%)
  other arithmetic  14.1 us (5%)
    all_to_all x1, waiting for transfers between devices, on_device(): lax.all_to_all(slot_out, 'expert', split_axis=0, concat_axis=0, tiled=True)  90.5 us
    all_to_all x1, waiting for transfers between devices, on_device(): lax.all_to_all(send_grad, 'expert', split_axis=0, concat_axis=0, tiled=True)  88.9 us
    reduce_sum x1, other arithmetic, on_device(): jnp.sum(out_slots.astype(jnp.float32), axis=1).astype(jnp.bfloat16)  7.69 us
    scatter x1, local copies, waits for them, and re-layouts, on_device(): jnp.zeros((buffer_rows, width), jnp.bfloat16).at[target_row]  7.04 us
    all_to_all x1, waiting for transfers between devices, on_device(): lax.all_to_all(send_hidden, 'expert', split_axis=0, concat_axis=0, tiled=...  6.83 us
    dot_general x1, matrix products, on_device(): lax.dot_general(recv_grad, gathered, (((1,), (1,)), ((), ())), preferred_...  6.62 us
    gather x1, local copies, waits for them, and re-layouts, on_device(): out_slots = back_out[target_row].reshape(tok_rows, 2, width)  6.61 us
    all_to_all x1, starting transfers between devices, on_device(): lax.all_to_all(send_gate, 'expert', split_axis=0, concat_axis=0, tiled=True)  6.55 us
  transfers between devices with their start and end apart: 7, of which 4 were waited for; matrix products, arithmetic and copies ran while one was open for 18% of the time, Pallas kernels for 0%

commit v1 on v0

v1 whole, which is shorter than its diff:
```python
import jax
import jax.numpy as jnp
from jax import lax
from jax.sharding import Mesh
from jax.sharding import PartitionSpec as P

F32 = jnp.float32
BF16 = jnp.bfloat16
SWAP = [(0, 1), (1, 0)]


def dot(a, b, ca=1, cb=0):
    return lax.dot_general(a, b, (((ca,), (cb,)), ((), ())), preferred_element_type=F32)


def one_hot_rows(rows, index):
    return (jnp.arange(rows, dtype=jnp.int32)[:, None] == index[None, :]).astype(BF16)


def target_rows(expert_ids, experts, capacity):
    routed = expert_ids.reshape(-1)
    slots = routed.shape[0]
    one_hot = (routed[:, None] == jnp.arange(experts, dtype=jnp.int32)[None, :]).astype(BF16)
    order = jnp.arange(slots, dtype=jnp.int32)
    earlier = (order[:, None] > order[None, :]).astype(BF16)
    ordinal = jnp.sum(dot(earlier, one_hot) * one_hot.astype(F32), axis=1).astype(jnp.int32)
    return (routed * capacity + ordinal).reshape(expert_ids.shape)


def exchange(x, axes):
    return lax.all_to_all(x, axes, split_axis=0, concat_axis=0, tiled=True)


def swap_if(flag, x):
    n = x.shape[0] // 2
    low, high = x[:n], x[n:]
    return jnp.where(flag, jnp.concatenate([high, low], 0), x)


def on_device(hidden_in, out_grad, expert_ids, gate_num, down_weight):
    tok_rows, top, units = hidden_in.shape
    half_experts = lax.axis_size("e")
    experts = 2 * half_experts
    replicas = lax.axis_size("dp")
    capacity = 4 * tok_rows // experts
    half_rows = half_experts * capacity
    slots = top * tok_rows
    side = lax.axis_index("h")
    dp = lax.axis_index("dp")
    share_units = units // replicas

    ids_other = lax.ppermute(expert_ids, "h", SWAP)
    grad_other = lax.ppermute(out_grad, "h", SWAP)
    weight_own = down_weight[0]
    if replicas == 2:
        weights = [weight_own, lax.ppermute(weight_own, "dp", SWAP)]
    else:
        weights = [lax.all_gather(weight_own, "dp", axis=0, tiled=True)]

    rows_own = target_rows(expert_ids, experts, capacity)
    rows_other = target_rows(ids_other, experts, capacity)
    numerators = gate_num.astype(F32)
    gate = numerators / jnp.sum(numerators, axis=1, keepdims=True)
    scaled = (gate[:, :, None] * hidden_in.astype(F32)).astype(BF16).reshape(slots, units)
    if replicas == 2:
        scaled = jnp.where(
            dp == 1,
            jnp.concatenate([scaled[:, share_units:], scaled[:, :share_units]], 1),
            scaled,
        )
    send_hidden = dot(one_hot_rows(2 * half_rows, rows_own.reshape(slots)), scaled).astype(BF16)
    recv_hidden = exchange(send_hidden, ("h", "e"))
    recv_hidden = swap_if(side == 1, recv_hidden)
    hid = [recv_hidden[:half_rows], recv_hidden[half_rows:]]

    def pick(rows):
        local = rows - side * half_rows
        return one_hot_rows(half_rows, local[:, 0]) + one_hot_rows(half_rows, local[:, 1])

    pick_own = pick(rows_own)
    pick_other = pick(rows_other)
    recv_own = exchange(dot(pick_own, out_grad).astype(BF16), "e")
    recv_other = exchange(dot(pick_other, grad_other).astype(BF16), "e")

    def forward(h):
        if replicas == 2:
            a = dot(h[:, :share_units], weights[0]) + dot(h[:, share_units:], weights[1])
        else:
            a = dot(h, weights[0])
        return a.astype(BF16)

    back_other = exchange(forward(hid[1]), "e")
    part_other = dot(pick_other, back_other, 0, 0).astype(BF16)
    part_mine = lax.ppermute(part_other, "h", SWAP)
    back_own = exchange(forward(hid[0]), "e")
    layer_out = (dot(pick_own, back_own, 0, 0) + part_mine.astype(F32)).astype(BF16)

    def backward(g):
        return jnp.concatenate([dot(g, w, 1, 1).astype(BF16) for w in weights], 1)

    grad_rows = swap_if(
        side == 1, jnp.concatenate([backward(recv_own), backward(recv_other)], 0)
    )
    back_rows = exchange(grad_rows, ("h", "e"))
    slot_back = dot(one_hot_rows(2 * half_rows, rows_own.reshape(slots)), back_rows, 0, 0)
    if replicas == 2:
        slot_back = jnp.where(
            dp == 1,
            jnp.concatenate([slot_back[:, share_units:], slot_back[:, :share_units]], 1),
            slot_back,
        )
    hidden_grad = (gate[:, :, None] * slot_back.reshape(tok_rows, top, units)).astype(BF16)

    def weight_grad(lo, hi):
        return (
            dot(hid[0][:, lo:hi], recv_own, 0, 0) + dot(hid[1][:, lo:hi], recv_other, 0, 0)
        ).astype(BF16)

    if replicas == 2:
        theirs = lax.ppermute(weight_grad(share_units, units), "dp", SWAP)
        total = weight_grad(0, share_units).astype(F32) + theirs.astype(F32)
    else:
        total = lax.psum_scatter(
            weight_grad(0, units), "dp", scatter_dimension=0, tiled=True
        ).astype(F32)
    down_grad = (total / replicas).astype(BF16)[None]
    return (layer_out, hidden_grad, down_grad)


def solution(mesh):
    replicas, experts = mesh.devices.shape
    halves = Mesh(mesh.devices.reshape(replicas, 2, experts // 2), ("dp", "h", "e"))
    tokens = ("dp", "h", "e")
    return jax.shard_map(
        on_device,
        mesh=halves,
        in_specs=(
            P(tokens, None, None),
            P(tokens, None),
            P(tokens, None),
            P(tokens, None),
            P(("h", "e"), "dp", None),
        ),
        out_specs=(
            P(tokens, None),
            P(tokens, None, None),
            P(("h", "e"), "dp", None),
        ),
        check_vma=False,
    )
```

time: 295 us -> 275 us (0.932); the launches traced: 294 us -> 271 us
  local copies, waits for them, and re-layouts: 30.5 us -> 5.12 us
  waiting for transfers between devices: 187 us -> 162 us
  matrix products: 19.6 us -> 43.2 us
  blocking collectives: 0 us -> 18.4 us
  between operations: 14.2 us -> 0.87 us
  other arithmetic: 14.1 us -> 3.17 us
  starting transfers between devices: 28.2 us -> 38.3 us
    all_to_all x5, waiting for transfers between devices: 187 us -> 31.2 us  [exchange(): return lax.all_to_all(x, axes, split_axis=0, concat_axis=0, tiled=True)]
    ppermute x0 -> x5, waiting for transfers between devices: none -> 130 us  [the longest x1 45.7 us: on_device(): grad_other = lax.ppermute(out_grad, 'h', SWAP)]
    dot_general x3 -> x20, matrix products: 19.6 us -> 43.2 us  [dot(): lax.dot_general(a, b, (((ca,), (cb,)), ((), ())), preferred_element_type=...]
    all_to_all x0 -> x1, blocking collectives: none -> 18.4 us  [exchange(): return lax.all_to_all(x, axes, split_axis=0, concat_axis=0, tiled=True)]
    scatter x3 -> x0, local copies, waits for them, and re-layouts: 10.6 us -> none  [the longest x1 7.04 us: on_device(): jnp.zeros((buffer_rows, width), jnp.bfloat16).at[target_row]]
    ppermute x0 -> x5, starting transfers between devices: none -> 9.22 us  [the longest x1 2.37 us: on_device(): ids_other = lax.ppermute(expert_ids, 'h', SWAP)]
    reduce_sum x3 -> x1, other arithmetic: 8.47 us -> 0.02 us  [on_device(): gate = numerators / jnp.sum(numerators, axis=1, keepdims=True)]
    gather x2 -> x0, local copies, waits for them, and re-layouts: 7.76 us -> none  [the longest x1 6.61 us: on_device(): out_slots = back_out[target_row].reshape(tok_rows, 2, width)]
  transfers between devices with their start and end apart: 7 -> 10, of which waited for: 4 -> 7; matrix products, arithmetic and copies ran while one was open for 18% -> 9% of each run, Pallas kernels for 0% -> 0%
where the time goes in v1:
time: 275 us; the launch traced here: 271 us
  waiting for transfers between devices  162 us (59%)
  matrix products  43.2 us (16%)
  starting transfers between devices  38.3 us (14%)
  blocking collectives  18.4 us (7%)
  local copies, waits for them, and re-layouts  5.12 us (2%)
  other arithmetic  3.17 us (1%)
    ppermute x1, waiting for transfers between devices, on_device(): grad_other = lax.ppermute(out_grad, 'h', SWAP)  45.7 us
    ppermute x1, waiting for transfers between devices, on_device(): weights = [weight_own, lax.ppermute(weight_own, 'dp', SWAP)]  43.4 us
    dot_general x20, matrix products, dot(): lax.dot_general(a, b, (((ca,), (cb,)), ((), ())), preferred_element_type=...  43.2 us
    ppermute x1, waiting for transfers between devices, on_device(): theirs = lax.ppermute(weight_grad(share_units, units), 'dp', SWAP)  39.9 us
    all_to_all x5, waiting for transfers between devices, exchange(): return lax.all_to_all(x, axes, split_axis=0, concat_axis=0, tiled=True)  31.2 us
    all_to_all x5, starting transfers between devices, exchange(): return lax.all_to_all(x, axes, split_axis=0, concat_axis=0, tiled=True)  29.1 us
    all_to_all x1, blocking collectives, exchange(): return lax.all_to_all(x, axes, split_axis=0, concat_axis=0, tiled=True)  18.4 us
  transfers between devices with their start and end apart: 10, of which 7 were waited for; matrix products, arithmetic and copies ran while one was open for 9% of the time, Pallas kernels for 0%

profile of v1, /device:TPU:11, one launch (start us, length us, event | category | flops | bytes accessed | tf_op | source)
XLA Modules:
  0.0 270.7 jit_solution(12595555170194003273)
XLA Ops:
  1.4 2.4 collective-permute-start.1
  5.1 1.3 collective-permute-done.1
  7.1 3.2 %convolution_convert_fusion = bf16[256,4096]{1,0:T(8,128)(2,1)} fusion(bf16[128,4096]{1,0:T(8,128)(2,1)} %param.6, s32[128]{0:T(128)S(1)} %get-tuple-element.4, s32[128]{0:T(128)S(1)} %get-tuple-element.3), kind=kOutput, calls=%fused_computation.4 | convolution fusion | flops 269746176 | bytes 3146752 | tf_op jit(solution)/shard_map/dot_general | solution.py:13
  10.4 5.7 %all-to-all-start.4 = ((bf16[8,32,4096]{2,1,0:T(8,128)(2,1)}), bf16[8,32,4096]{2,1,0:T(8,128)(2,1)S(1)}, u32[]{:S(2)}, u32[]{:S(2)}) async-start(bf16[8,32,4096]{2,1,0:T(8,128)(2,1)} %bitcast.48), calls=%async_computation.4 | async-start | bytes 4194304 | tf_op jit(solution)/shard_map/all_to_all | solution.py:31
  16.1 2.3 collective-permute-start.3
  18.6 45.7 %collective-permute-done.3 = bf16[128,4096]{1,0:T(8,128)(2,1)S(1)} collective-permute-done((bf16[128,4096]{1,0:T(8,128)(2,1)S(1)}, bf16[128,4096]{1,0:T(8,128)(2,1)S(1)}, u32[]{:S(2)}, u32[]{:S(2)}) %collective-permute-start.3) | collective-permute-done | bytes 1048608 | tf_op jit(solution)/shard_map/ppermute | solution.py:53
  64.3 2.0 convolution_convert_fusion.1
  66.3 4.7 %all-to-all-start.3 = ((bf16[8,32,4096]{2,1,0:T(8,128)(2,1)}), bf16[8,32,4096]{2,1,0:T(8,128)(2,1)}, u32[]{:S(2)}, u32[]{:S(2)}) async-start(bf16[8,32,4096]{2,1,0:T(8,128)(2,1)} %bitcast.47), calls=%async_computation.3 | async-start | bytes 4194304 | tf_op jit(solution)/shard_map/all_to_all | solution.py:31
  71.0 1.2 collective-permute-start
  72.3 2.4 convolution_convert_fusion.5
  74.7 43.4 %collective-permute-done = bf16[256,4096]{1,0:T(8,128)(2,1)} collective-permute-done((bf16[256,4096]{1,0:T(8,128)(2,1)}, bf16[256,4096]{1,0:T(8,128)(2,1)}, u32[]{:S(2)}, u32[]{:S(2)}) %collective-permute-start) | collective-permute-done | bytes 2097184 | tf_op jit(solution)/shard_map/ppermute | solution.py:56
  118.0 2.3 convolution_convert_fusion.4
  120.4 3.0 %convolution_convert_fusion.7 = bf16[256,256]{0,1:T(8,128)(2,1)S(1)} fusion(bf16[256,4096]{1,0:T(8,128)(2,1)} %bitcast.10, bf16[1,256,4096]{2,1,0:T(8,128)(2,1)} %param.9), kind=kOutput, calls=%fused_computation.19 | convolution fusion | flops 536936448 | bytes 4325376 | tf_op jit(solution)/shard_map/dot_general | solution.py:13
  123.3 3.0 %convolution_convert_fusion.6 = bf16[256,256]{0,1:T(8,128)(2,1)S(1)} fusion(bf16[256,4096]{1,0:T(8,128)(2,1)} %bitcast.10, bf16[256,4096]{1,0:T(8,128)(2,1)} %collective-permute-done), kind=kOutput, calls=%fused_computation.18 | convolution fusion | flops 536936448 | bytes 4325376 | tf_op jit(solution)/shard_map/dot_general | solution.py:13
  127.5 7.2 %all-to-all-start.5 = ((bf16[16,32,512]{2,1,0:T(8,128)(2,1)}), bf16[16,32,512]{2,1,0:T(8,128)(2,1)S(1)}, u32[]{:S(2)}, u32[]{:S(2)}) async-start(bf16[16,32,512]{2,1,0:T(8,128)(2,1)} %bitcast.13), calls=%async_computation.5 | async-start | bytes 1048576 | tf_op jit(solution)/shard_map/all_to_all | solution.py:31
  134.8 13.4 %all-to-all-done.5 = bf16[16,32,512]{2,1,0:T(8,128)(2,1)S(1)} async-done(((bf16[16,32,512]{2,1,0:T(8,128)(2,1)}), bf16[16,32,512]{2,1,0:T(8,128)(2,1)S(1)}, u32[]{:S(2)}, u32[]{:S(2)}) %all-to-all-start.5) | async-done | bytes 524320 | tf_op jit(solution)/shard_map/all_to_all | solution.py:31
  149.5 1.1 multiply_convert_fusion.1
  151.2 18.4 %all_to_all.69 = bf16[16,32,512]{2,1,0:T(8,128)(2,1)S(1)} all-to-all(bf16[16,32,512]{2,1,0:T(8,128)(2,1)S(1)} %bitcast.55), channel_id=1, replica_groups=mesh['dp'=2,'h'=2,'e'=8] {'h','e'}, dimensions={0} | all-to-all | bytes 1048576 | tf_op jit(solution)/shard_map/all_to_all | solution.py:31
  171.8 2.3 fusion.21
  174.2 3.7 %fusion.1 = bf16[256,4096]{1,0:T(8,128)(2,1)} fusion(f32[256,4096]{1,0:T(8,128)S(1)} %fusion.21, bf16[256,4096]{1,0:T(8,128)(2,1)} %collective-permute-done, bf16[512,512]{0,1:T(8,128)(2,1)S(1)} %maximum_select_fusion), kind=kOutput, calls=%fused_computation.7 | convolution fusion | flops 538968064 | bytes 8519680 | tf_op jit(solution)/shard_map/dot_general | solution.py:13
  177.9 5.2 %all-to-all-start.2 = ((bf16[8,32,4096]{2,1,0:T(8,128)(2,1)}), bf16[8,32,4096]{2,1,0:T(8,128)(2,1)}, u32[]{:S(2)}, u32[]{:S(2)}) async-start(bf16[8,32,4096]{2,1,0:T(8,128)(2,1)} %bitcast.50), calls=%async_computation.2 | async-start | bytes 4194304 | tf_op jit(solution)/shard_map/all_to_all | solution.py:31
  183.1 2.3 fusion.30
  185.5 3.7 %fusion = bf16[256,4096]{1,0:T(8,128)(2,1)} fusion(f32[256,4096]{1,0:T(8,128)S(1)} %fusion.30, bf16[256,4096]{1,0:T(8,128)(2,1)} %collective-permute-done, bf16[512,512]{0,1:T(8,128)(2,1)S(1)} %maximum_select_fusion), kind=kOutput, calls=%fused_computation.6 | convolution fusion | flops 538968064 | bytes 8519680 | tf_op jit(solution)/shard_map/dot_general | solution.py:13
  189.2 17.8 %all-to-all-done.2 = bf16[8,32,4096]{2,1,0:T(8,128)(2,1)} async-done(((bf16[8,32,4096]{2,1,0:T(8,128)(2,1)}), bf16[8,32,4096]{2,1,0:T(8,128)(2,1)}, u32[]{:S(2)}, u32[]{:S(2)}) %all-to-all-start.2) | async-done | bytes 2097184 | tf_op jit(solution)/shard_map/all_to_all | solution.py:31
  206.9 6.2 %all-to-all-start.1 = ((bf16[8,32,4096]{2,1,0:T(8,128)(2,1)}), bf16[8,32,4096]{2,1,0:T(8,128)(2,1)}, u32[]{:S(2)}, u32[]{:S(2)}) async-start(bf16[8,32,4096]{2,1,0:T(8,128)(2,1)} %bitcast.49), calls=%async_computation.1 | async-start | bytes 4194304 | tf_op jit(solution)/shard_map/all_to_all | solution.py:31
  213.9 2.4 fusion.4
  216.3 1.3 collective-permute-start.4
  217.6 3.1 %convolution_convert_fusion.2 = bf16[128,4096]{1,0:T(8,128)(2,1)} fusion(bf16[256,4096]{1,0:T(8,128)(2,1)} %bitcast.8, s32[128]{0:T(128)S(1)} %get-tuple-element.6, s32[128]{0:T(128)S(1)} %get-tuple-element.5), kind=kOutput, calls=%fused_computation.11 | convolution fusion | flops 269221888 | bytes 3146752 | tf_op jit(solution)/shard_map/dot_general | solution.py:13
  220.7 2.0 collective-permute-start.2
  223.4 39.9 %collective-permute-done.4 = bf16[256,4096]{1,0:T(8,128)(2,1)S(1)} collective-permute-done((bf16[256,4096]{1,0:T(8,128)(2,1)S(1)}, bf16[256,4096]{1,0:T(8,128)(2,1)S(1)}, u32[]{:S(2)}, u32[]{:S(2)}) %collective-permute-start.4) | collective-permute-done | bytes 2097184 | tf_op jit(solution)/shard_map/ppermute | solution.py:120
  263.2 4.0 %fusion.5 = bf16[1,256,4096]{2,1,0:T(8,128)(2,1)} fusion(bf16[256,4096]{1,0:T(8,128)(2,1)S(1)} %collective-permute-done.4, f32[256,4096]{1,0:T(8,128)S(1)} %fusion.28, bf16[256,4096]{1,0:T(8,128)(2,1)} %bitcast.10, bf16[512,512]{0,1:T(8,128)(2,1)S(1)} %maximum_select_fusion), kind=kOutput, calls=%fused_computation.13 | convolution fusion | flops 544210944 | bytes 10616832 | tf_op jit(solution)/shard_map/dot_general | solution.py:13
  267.4 3.3 %add_convert_fusion = bf16[128,4096]{1,0:T(8,128)(2,1)} fusion(bf16[128,4096]{1,0:T(8,128)(2,1)} %collective-permute-done.2, bf16[256,4096]{1,0:T(8,128)(2,1)} %bitcast.6, s32[128]{0:T(128)S(1)} %get-tuple-element.4, s32[128]{0:T(128)S(1)} %get-tuple-element.3), kind=kOutput, calls=%fused_computation.14 | convolution fusion | flops 270270464 | bytes 4195328 | tf_op jit(solution)/shard_map/dot_general | solution.py:13
  (44 shorter events, 9.9 us)
Async XLA Ops:
  1.4 5.0 %collective-permute-start.1 = (s32[128,2]{1,0:T(8,128)S(1)}, s32[128,2]{1,0:T(8,128)S(1)}, u32[]{:S(2)}, u32[]{:S(2)}) collective-permute-start(s32[128,2]{1,0:T(8,128)S(1)} %copy.22), channel_id=1, source_target_pairs={{0,8},{8,0},{1,9},{9,1},{2,10},{10,2},{3,11},{11,3},{4,12},{12,4},... | collective-permute-start | bytes 3080 | tf_op jit(solution)/shard_map/ppermute | solution.py:52
  10.4 5.7 %copy-start = (bf16[128,4096]{1,0:T(8,128)(2,1)S(1)}, bf16[128,4096]{1,0:T(8,128)(2,1)}, u32[]{:S(2)}) copy-start(bf16[128,4096]{1,0:T(8,128)(2,1)} %param.6) | copy-start | bytes 3145732
  10.4 56.0 %all-to-all-start.4 = ((bf16[8,32,4096]{2,1,0:T(8,128)(2,1)}), bf16[8,32,4096]{2,1,0:T(8,128)(2,1)S(1)}, u32[]{:S(2)}, u32[]{:S(2)}) async-start(bf16[8,32,4096]{2,1,0:T(8,128)(2,1)} %bitcast.48), calls=%async_computation.4 | async-start | bytes 4194304 | tf_op jit(solution)/shard_map/all_to_all | solution.py:31
  16.1 48.2 %collective-permute-start.3 = (bf16[128,4096]{1,0:T(8,128)(2,1)S(1)}, bf16[128,4096]{1,0:T(8,128)(2,1)S(1)}, u32[]{:S(2)}, u32[]{:S(2)}) collective-permute-start(bf16[128,4096]{1,0:T(8,128)(2,1)S(1)} %copy-done), channel_id=1, source_target_pairs={{0,8},{8,0},{1,9},{9,1},{2,10},{10,2},{3,11},{11,3},{4,12},{12,4},... | collective-permute-start | bytes 3145736 | tf_op jit(solution)/shard_map/ppermute | solution.py:53
  66.3 54.0 %all-to-all-start.3 = ((bf16[8,32,4096]{2,1,0:T(8,128)(2,1)}), bf16[8,32,4096]{2,1,0:T(8,128)(2,1)}, u32[]{:S(2)}, u32[]{:S(2)}) async-start(bf16[8,32,4096]{2,1,0:T(8,128)(2,1)} %bitcast.47), calls=%async_computation.3 | async-start | bytes 4194304 | tf_op jit(solution)/shard_map/all_to_all | solution.py:31
  71.0 47.0 %collective-permute-start = (bf16[256,4096]{1,0:T(8,128)(2,1)}, bf16[256,4096]{1,0:T(8,128)(2,1)}, u32[]{:S(2)}, u32[]{:S(2)}) collective-permute-start(bf16[256,4096]{1,0:T(8,128)(2,1)} %bitcast.46), channel_id=1, source_target_pairs={{0,16},{16,0},{1,17},{17,1},{2,18},{18,2},{3,19},{19,3},{4,20},{20... | collective-permute-start | bytes 6291464 | tf_op jit(solution)/shard_map/ppermute | solution.py:56
  126.3 8.3 %copy-start.2 = (s32[128,2]{0,1:T(2,128)S(1)}, s32[128,2]{0,1:T(2,128)}, u32[]{:S(2)}) copy-start(s32[128,2]{0,1:T(2,128)} %param.8) | copy-start | bytes 3076
  127.5 20.8 %all-to-all-start.5 = ((bf16[16,32,512]{2,1,0:T(8,128)(2,1)}), bf16[16,32,512]{2,1,0:T(8,128)(2,1)S(1)}, u32[]{:S(2)}, u32[]{:S(2)}) async-start(bf16[16,32,512]{2,1,0:T(8,128)(2,1)} %bitcast.13), calls=%async_computation.5 | async-start | bytes 1048576 | tf_op jit(solution)/shard_map/all_to_all | solution.py:31
  148.6 1.0 copy-start.1
  177.9 29.0 %all-to-all-start.2 = ((bf16[8,32,4096]{2,1,0:T(8,128)(2,1)}), bf16[8,32,4096]{2,1,0:T(8,128)(2,1)}, u32[]{:S(2)}, u32[]{:S(2)}) async-start(bf16[8,32,4096]{2,1,0:T(8,128)(2,1)} %bitcast.50), calls=%async_computation.2 | async-start | bytes 4194304 | tf_op jit(solution)/shard_map/all_to_all | solution.py:31
  206.9 60.3 %all-to-all-start.1 = ((bf16[8,32,4096]{2,1,0:T(8,128)(2,1)}), bf16[8,32,4096]{2,1,0:T(8,128)(2,1)}, u32[]{:S(2)}, u32[]{:S(2)}) async-start(bf16[8,32,4096]{2,1,0:T(8,128)(2,1)} %bitcast.49), calls=%async_computation.1 | async-start | bytes 4194304 | tf_op jit(solution)/shard_map/all_to_all | solution.py:31
  216.3 46.9 %collective-permute-start.4 = (bf16[256,4096]{1,0:T(8,128)(2,1)S(1)}, bf16[256,4096]{1,0:T(8,128)(2,1)S(1)}, u32[]{:S(2)}, u32[]{:S(2)}) collective-permute-start(bf16[256,4096]{1,0:T(8,128)(2,1)S(1)} %fusion.4), channel_id=1, source_target_pairs={{0,16},{16,0},{1,17},{17,1},{2,18},{18,2},{3,19},{19,3},{4,20},{20... | collective-permute-start | bytes 6291464 | tf_op jit(solution)/shard_map/ppermute | solution.py:120
  220.7 46.7 %collective-permute-start.2 = (bf16[128,4096]{1,0:T(8,128)(2,1)}, bf16[128,4096]{1,0:T(8,128)(2,1)}, u32[]{:S(2)}, u32[]{:S(2)}) collective-permute-start(bf16[128,4096]{1,0:T(8,128)(2,1)} %convolution_convert_fusion.2), channel_id=1, source_target_pairs={{0,8},{8,0},{1,9},{9,1},{2,10},{10,2},{3,11},{11,3},{4,12},{12,4},... | collective-permute-start | bytes 3145736 | tf_op jit(solution)/shard_map/ppermute | solution.py:94

commit v2 on v1

v2 whole, which is shorter than its diff:
```python
import functools

import jax
import jax.numpy as jnp
from jax import lax
from jax.experimental import pallas as pl
from jax.experimental.pallas import tpu as pltpu
from jax.sharding import Mesh
from jax.sharding import PartitionSpec as P

F32 = jnp.float32
BF16 = jnp.bfloat16
I32 = jnp.int32
SWAP = [(0, 1), (1, 0)]
VMEM = pl.BlockSpec(memory_space=pltpu.VMEM)
SMEM = pl.BlockSpec(memory_space=pltpu.SMEM)
STEP = 1024


def dot(a, b, ca=1, cb=0):
    return lax.dot_general(a, b, (((ca,), (cb,)), ((), ())), preferred_element_type=F32)


def call(body, outs, *args, specs=None):
    many = isinstance(outs, (list, tuple))
    return pl.pallas_call(
        body,
        out_shape=outs,
        in_specs=[SMEM] + [VMEM] * (len(args) - 1),
        out_specs=[VMEM] * len(outs) if many else VMEM,
        compiler_params=pltpu.CompilerParams(vmem_limit_bytes=48 * 1024 * 1024),
    )(*args)


def shaped(shape, dtype=BF16):
    return jax.ShapeDtypeStruct(tuple(shape), dtype)


def iota(shape, dim):
    return lax.broadcasted_iota(I32, shape, dim)


def slot_rows(ids, experts, capacity):
    tokens = ids.shape[0]
    lanes = iota((tokens, experts), 1)
    earlier = (iota((tokens, tokens), 0) > iota((tokens, tokens), 1)).astype(BF16)
    eye = iota((tokens, tokens), 0) == iota((tokens, tokens), 1)
    cols, rows = [], []
    base = jnp.zeros((1, experts), F32)
    for k in range(ids.shape[1]):
        chosen = ids[:, k : k + 1]
        one_hot = (chosen == lanes).astype(F32)
        before = dot(earlier, one_hot.astype(BF16)) + base
        ordinal = jnp.sum(before * one_hot, axis=1, keepdims=True)
        base = base + jnp.sum(one_hot, axis=0, keepdims=True)
        col = chosen.astype(F32) * capacity + ordinal
        row = jnp.sum(jnp.where(eye, jnp.broadcast_to(col, (tokens, tokens)), 0.0), axis=0, keepdims=True)
        cols.append(col.astype(I32))
        rows.append(row.astype(I32))
    return cols, rows


def store_rows(cols, rows, row_ref, col_ref):
    for k in range(len(cols)):
        row_ref[k : k + 1, :] = rows[k]
        col_ref[:, k : k + 1] = cols[k]


def swap_halves(x, flag):
    n = x.shape[1] // 2
    return jnp.where(flag, jnp.concatenate([x[:, n:], x[:, :n]], 1), x)


def prepare_body(experts, capacity, top, swap, place, ids_ref, num_ref, hid_ref, row_ref, col_ref, send_ref):
    tokens = ids_ref.shape[0]
    units = hid_ref.shape[1] // top
    cols, rows = slot_rows(ids_ref[...], experts, capacity)
    store_rows(cols, rows, row_ref, col_ref)
    numerators = num_ref[...].astype(F32)
    total = jnp.sum(numerators, axis=1, keepdims=True)
    target = iota((experts * capacity, tokens), 0)
    acc = None
    for k in range(top):
        share = numerators[:, k : k + 1] / total
        scaled = (share * hid_ref[:, k * units : (k + 1) * units].astype(F32)).astype(BF16)
        part = dot((target == rows[k]).astype(BF16), scaled)
        acc = part if acc is None else acc + part
    out = acc.astype(BF16)
    send_ref[...] = swap_halves(out, place[1] == 1) if swap else out


def rows_body(experts, capacity, place, ids_ref, row_ref, col_ref):
    cols, rows = slot_rows(ids_ref[...], experts, capacity)
    store_rows(cols, rows, row_ref, col_ref)


def pick_body(top, place, row_ref, *refs):
    *grads, out_ref = refs
    half = out_ref.shape[0]
    target = iota((half, row_ref.shape[1]), 0) + place[0] * half
    pick = None
    for k in range(top):
        hit = target == row_ref[k : k + 1, :]
        pick = hit if pick is None else pick | hit
    pick = pick.astype(BF16)
    c0 = 0
    for g in grads:
        width = g.shape[1]
        step = min(STEP, width)
        for c in range(0, width, step):
            out_ref[:, c0 + c : c0 + c + step] = dot(pick, g[:, c : c + step]).astype(BF16)
        c0 += width


def combine_body(top, place, col_ref, back_ref, *refs):
    *parts, out_refs = refs
    half, width = back_ref.shape
    target = iota((col_ref.shape[0], half), 1) + place[0] * half
    hit = None
    for k in range(top):
        h = target == col_ref[:, k : k + 1]
        hit = h if hit is None else hit | h
    hit = hit.astype(BF16)
    step = min(STEP, width)
    for c in range(0, width, step):
        acc = dot(hit, back_ref[:, c : c + step])
        c0 = 0
        for p in parts:
            if c0 <= c < c0 + p.shape[1]:
                acc = acc + p[:, c - c0 : c - c0 + step].astype(F32)
            c0 += p.shape[1]
        out_refs[:, c : c + step] = acc.astype(BF16)


def piece_cols(pieces, c, step):
    for r0, c0, ref in pieces:
        if c0 <= c < c0 + ref.shape[1]:
            yield r0, ref.shape[0], ref[:, c - c0 : c - c0 + step]


def forward_body(which, offsets, place, hid_ref, *refs):
    *weights, out_ref = refs
    half, width = out_ref.shape
    side = place[0]
    start = (1 - side if which else side) * half
    hid = hid_ref[pl.ds(pl.multiple_of(start, half), half), :]
    pieces = [(r, c, ref) for (r, c), ref in zip(offsets, weights)]
    step = min(STEP, width)
    for c in range(0, width, step):
        acc = None
        for r0, n, w in piece_cols(pieces, c, step):
            part = dot(hid[:, r0 : r0 + n], w)
            acc = part if acc is None else acc + part
        out_ref[:, c : c + step] = acc.astype(BF16)


def backward_body(offsets, place, own_ref, other_ref, *refs):
    *weights, out_ref = refs
    half, width = own_ref.shape
    side = place[0]
    pieces = [(r, c, ref) for (r, c), ref in zip(offsets, weights)]
    starts = sorted({r for r, _ in offsets})
    for which, g in ((0, own_ref), (1, other_ref)):
        start = pl.multiple_of((1 - side if which else side) * half, half)
        for r in starts:
            acc, n = None, 0
            for r0, c0, ref in pieces:
                if r0 == r:
                    part = dot(g[:, c0 : c0 + ref.shape[1]], ref[...], 1, 1)
                    acc = part if acc is None else acc + part
                    n = ref.shape[0]
            out_ref[pl.ds(start, half), r : r + n] = acc.astype(BF16)


def weight_grad_body(lo, hi, place, hid_ref, own_ref, other_ref, *out_refs):
    half, _ = own_ref.shape
    side = place[0]
    h_own = hid_ref[pl.ds(pl.multiple_of(side * half, half), half), :][:, lo:hi]
    h_other = hid_ref[pl.ds(pl.multiple_of((1 - side) * half, half), half), :][:, lo:hi]
    c0 = 0
    for out_ref in out_refs:
        width = out_ref.shape[1]
        step = min(STEP, width)
        for c in range(0, width, step):
            at = slice(c0 + c, c0 + c + step)
            acc = dot(h_own, own_ref[:, at], 0, 0) + dot(h_other, other_ref[:, at], 0, 0)
            out_ref[:, c : c + step] = acc.astype(BF16)
        c0 += width


def average_body(lo, hi, replicas, place, hid_ref, own_ref, other_ref, *refs):
    *theirs, out_ref = refs
    half, _ = own_ref.shape
    side = place[0]
    h_own = hid_ref[pl.ds(pl.multiple_of(side * half, half), half), :][:, lo:hi]
    h_other = hid_ref[pl.ds(pl.multiple_of((1 - side) * half, half), half), :][:, lo:hi]
    c0 = 0
    for t in theirs:
        width = t.shape[1]
        step = min(STEP, width)
        for c in range(0, width, step):
            at = slice(c0 + c, c0 + c + step)
            acc = dot(h_own, own_ref[:, at], 0, 0) + dot(h_other, other_ref[:, at], 0, 0)
            acc = acc.astype(BF16).astype(F32) + t[:, c : c + step].astype(F32)
            out_ref[:, at] = (acc / replicas).astype(BF16)
        c0 += width


def hidden_grad_body(top, swap, place, col_ref, num_ref, back_ref, out_ref):
    tokens = col_ref.shape[0]
    rows, units = back_ref.shape
    numerators = num_ref[...].astype(F32)
    total = jnp.sum(numerators, axis=1, keepdims=True)
    target = iota((tokens, rows), 1)
    for k in range(top):
        hit = (target == col_ref[:, k : k + 1]).astype(BF16)
        got = (numerators[:, k : k + 1] / total * dot(hit, back_ref[...])).astype(BF16)
        out_ref[:, k * units : (k + 1) * units] = swap_halves(got, place[1] == 1) if swap else got


def after(x, *others):
    return lax.optimization_barrier((x, *others))[0]


def exchange(x, axes):
    return lax.all_to_all(x, axes, split_axis=0, concat_axis=0, tiled=True)


def cut(x, *shares):
    total, at, out = sum(shares), 0, []
    for s in shares:
        n = x.shape[1] * s // total
        out.append(x[:, at : at + n])
        at += n
    return out


def on_device(hidden_in, out_grad, expert_ids, gate_num, down_weight):
    tokens, top, units = hidden_in.shape
    width = out_grad.shape[1]
    half_experts = lax.axis_size("e")
    experts = 2 * half_experts
    replicas = lax.axis_size("dp")
    capacity = 4 * tokens // experts
    half = half_experts * capacity
    share = units // replicas
    pair = replicas == 2
    place = jnp.stack([lax.axis_index("h"), lax.axis_index("dp")]).astype(I32)
    part = functools.partial
    row_shape, col_shape = shaped((top, tokens), I32), shaped((tokens, top), I32)

    def to_other(x):
        return lax.ppermute(x, "h", SWAP)

    def to_replica(x):
        return lax.ppermute(x, "dp", SWAP)

    weight = down_weight[0]
    ids_other = to_other(expert_ids)
    row_own, col_own, send_hidden = call(
        part(prepare_body, experts, capacity, top, pair),
        [row_shape, col_shape, shaped((2 * half, units))],
        place, expert_ids, gate_num, hidden_in.reshape(tokens, top * units),
    )
    row_other, col_other = call(
        part(rows_body, experts, capacity), [row_shape, col_shape], place, ids_other
    )
    send_own = call(part(pick_body, top), shaped((half, width)), place, row_own, out_grad)

    if pair:
        w_a, w_b, w_c = cut(weight, 1, 1, 2)
        w_a = to_replica(w_a)
        hid = exchange(after(send_hidden, w_a), ("h", "e"))
        w_b = to_replica(w_b)
    else:
        hid = exchange(send_hidden, ("h", "e"))
    g_a, g_b, g_c = cut(out_grad, 1, 2, 1)
    g_a = to_other(g_a)
    if pair:
        recv_own = exchange(after(send_own, hid, w_b, g_a), "e")
        w_c = to_replica(w_c)
        q = width // 4
        weights = [weight, w_a, w_b, w_c]
        offsets = [(0, 0), (share, 0), (share, q), (share, 2 * q)]
    else:
        recv_own = exchange(after(send_own, hid, g_a), "e")
        weights = [lax.all_gather(weight, "dp", axis=0, tiled=True)]
        offsets = [(0, 0)]
    g_b = to_other(g_b)
    out_other = call(part(forward_body, 1, offsets), shaped((half, width)), place, hid, *weights)
    back_other = exchange(after(out_other, recv_own, g_b), "e")
    g_c = to_other(g_c)
    send_other = call(part(pick_body, top), shaped((half, width)), place, row_other, g_a, g_b, g_c)
    recv_other = exchange(after(send_other, back_other), "e")
    part_other = call(part(combine_body, top), shaped((tokens, width)), place, col_other, back_other)
    p_a, p_b = cut(part_other, 1, 1)
    p_a = to_other(p_a)
    out_own = call(part(forward_body, 0, offsets), shaped((half, width)), place, hid, *weights)
    back_own = exchange(after(out_own, recv_other, p_a), "e")
    p_b = to_other(p_b)
    if pair:
        d_a, d_b = call(
            part(weight_grad_body, share, units),
            [shaped((share, width // 2))] * 2,
            place, hid, recv_own, recv_other,
        )
        d_a = to_replica(d_a)
    grad_rows = call(
        part(backward_body, offsets), shaped((2 * half, units)),
        place, recv_own, recv_other, *weights,
    )
    gate_on = (back_own, p_b, d_a) if pair else (back_own, p_b)
    back_rows = exchange(after(grad_rows, *gate_on), ("h", "e"))
    layer_out = call(
        part(combine_body, top), shaped((tokens, width)), place, col_own, back_own, p_a, p_b
    )
    if pair:
        d_b = to_replica(d_b)
        down_grad = call(
            part(average_body, 0, share, replicas), shaped((share, width)),
            place, hid, recv_own, recv_other, d_a, d_b,
        )
    else:
        whole = call(
            part(weight_grad_body, 0, units), [shaped((units, width))],
            place, hid, recv_own, recv_other,
        )[0]
        total = lax.psum_scatter(whole, "dp", scatter_dimension=0, tiled=True)
        down_grad = (total.astype(F32) / replicas).astype(BF16)
    hidden_grad = call(
        part(hidden_grad_body, top, pair), shaped((tokens, top * units)),
        place, col_own, gate_num, back_rows,
    )
    return (layer_out, hidden_grad.reshape(tokens, top, units), down_grad[None])


def solution(mesh):
    replicas, experts = mesh.devices.shape
    halves = Mesh(mesh.devices.reshape(replicas, 2, experts // 2), ("dp", "h", "e"))
    tokens = ("dp", "h", "e")
    return jax.shard_map(
        on_device,
        mesh=halves,
        in_specs=(
            P(tokens, None, None),
            P(tokens, None),
            P(tokens, None),
            P(tokens, None),
            P(("h", "e"), "dp", None),
        ),
        out_specs=(
            P(tokens, None),
            P(tokens, None, None),
            P(("h", "e"), "dp", None),
        ),
        check_vma=False,
    )
```

time: 275 us -> 244 us (0.89)
  matrix products: 43.2 us -> 0 us
  Pallas kernels: 0 us -> 31.3 us
  waiting for transfers between devices: 162 us -> 141 us
  blocking collectives: 18.4 us -> 0 us
  local copies, waits for them, and re-layouts: 5.12 us -> 19.7 us
  starting transfers between devices: 38.3 us -> 47.4 us
  other arithmetic: 3.17 us -> 0.08 us
    dot_general x20 -> x0, matrix products: 43.2 us -> none  [dot(): lax.dot_general(a, b, (((ca,), (cb,)), ((), ())), preferred_element_type=...]
    pallas_call x0 -> x12, Pallas kernels: none -> 31.3 us  [call(): pl.pallas_call(body, out_shape=outs, in_specs=[SMEM] + [VMEM] * (len(args...]
    all_to_all x5 -> x6, waiting for transfers between devices: 31.2 us -> 0.02 us  [exchange(): return lax.all_to_all(x, axes, split_axis=0, concat_axis=0, tiled=True)]
    all_to_all x1 -> x0, blocking collectives: 18.4 us -> none  [exchange(): return lax.all_to_all(x, axes, split_axis=0, concat_axis=0, tiled=True)]
    unnamed x7 -> x61, local copies, waits for them, and re-layouts: 1.31 us -> 13.5 us
    ppermute x5 -> x11, waiting for transfers between devices: 130 us -> 141 us  [the longest x6 102 us: to_other(): return lax.ppermute(x, 'h', SWAP)]
    all_to_all x5 -> x6, starting transfers between devices: 29.1 us -> 34.6 us  [exchange(): return lax.all_to_all(x, axes, split_axis=0, concat_axis=0, tiled=True)]
    slice x7 -> x5, local copies, waits for them, and re-layouts: 1.42 us -> 5.35 us  [cut(): out.append(x[:, at:at + n])]
  transfers between devices with their start and end apart: 10 -> 17, of which waited for: 7 -> 8; matrix products, arithmetic and copies ran while one was open for 9% -> 1% of each run, Pallas kernels for 0% -> 13%
where the time goes in v2:
time: 244 us; the launch traced here: 241 us
  waiting for transfers between devices  141 us (58%)
  starting transfers between devices  47.4 us (19%)
  Pallas kernels  31.3 us (13%)
  local copies, waits for them, and re-layouts  19.7 us (8%)
    ppermute x6, waiting for transfers between devices, to_other(): return lax.ppermute(x, 'h', SWAP)  102 us
    ppermute x5, waiting for transfers between devices, to_replica(): return lax.ppermute(x, 'dp', SWAP)  39.8 us
    all_to_all x6, starting transfers between devices, exchange(): return lax.all_to_all(x, axes, split_axis=0, concat_axis=0, tiled=True)  34.6 us
    pallas_call x12, Pallas kernels, call(): pl.pallas_call(body, out_shape=outs, in_specs=[SMEM] + [VMEM] * (len(args...  31.3 us
    unnamed x61, local copies, waits for them, and re-layouts  13.5 us
    ppermute x6, starting transfers between devices, to_other(): return lax.ppermute(x, 'h', SWAP)  7.55 us
    slice x5, local copies, waits for them, and re-layouts, cut(): out.append(x[:, at:at + n])  5.35 us
    ppermute x5, starting transfers between devices, to_replica(): return lax.ppermute(x, 'dp', SWAP)  5.25 us
  transfers between devices with their start and end apart: 17, of which 8 were waited for; matrix products, arithmetic and copies ran while one was open for 1% of the time, Pallas kernels for 13%

profile of v2, /device:TPU:11, one launch (start us, length us, event | category | flops | bytes accessed | tf_op | source)
XLA Modules:
  0.0 240.8 jit_solution(6423369467537860695)
XLA Ops:
  0.7 2.2 fusion
  4.4 2.2 shard_map.76
  6.6 9.0 %collective-permute-done.refs_1_ = bf16[256,1024]{1,0:T(8,128)(2,1)S(1)} collective-permute-done((bf16[256,1024]{1,0:T(8,128)(2,1)S(1)}, bf16[256,1024]{1,0:T(8,128)(2,1)S(1)}, u32[]{:S(2)}, u32[]{:S(2)}) %collective-permute-start) | collective-permute-done | bytes 524320 | tf_op jit(solution)/shard_map/ppermute | solution.py:256
  15.6 7.4 %all-to-all-start = ((bf16[16,32,512]{2,1,0:T(8,128)(2,1)}), bf16[16,32,512]{2,1,0:T(8,128)(2,1)S(1)}, u32[]{:S(2)}, u32[]{:S(2)}) async-start(bf16[16,32,512]{2,1,0:T(8,128)(2,1)} %bitcast.3), calls=%async_computation | async-start | bytes 1048576 | tf_op jit(solution)/shard_map/all_to_all | solution.py:226
  25.0 2.1 collective-permute-start.4
  28.4 1.3 copy-done.5
  29.7 16.1 %collective-permute-done.4.refs_0_ = bf16[128,1024]{1,0:T(8,128)(2,1)S(1)} collective-permute-done((bf16[128,1024]{1,0:T(8,128)(2,1)S(1)}, bf16[128,1024]{1,0:T(8,128)(2,1)S(1)}, u32[]{:S(2)}, u32[]{:S(2)}) %collective-permute-start.4) | collective-permute-done | bytes 262176 | tf_op jit(solution)/shard_map/ppermute | solution.py:253
  46.7 7.4 %all-to-all-start.1 = ((bf16[8,32,4096]{2,1,0:T(8,128)(2,1)}), bf16[8,32,4096]{2,1,0:T(8,128)(2,1)S(1)}, u32[]{:S(2)}, u32[]{:S(2)}) async-start(bf16[8,32,4096]{2,1,0:T(8,128)(2,1)} %bitcast.27), calls=%async_computation.1 | async-start | bytes 4194304 | tf_op jit(solution)/shard_map/all_to_all | solution.py:226
  54.0 1.4 slice.34
  55.5 1.3 collective-permute-start.2
  57.2 22.7 %collective-permute-done.2.refs_3_ = bf16[256,2048]{1,0:T(8,128)(2,1)S(1)} collective-permute-done((bf16[256,2048]{1,0:T(8,128)(2,1)S(1)}, bf16[256,2048]{1,0:T(8,128)(2,1)S(1)}, u32[]{:S(2)}, u32[]{:S(2)}) %collective-permute-start.2) | collective-permute-done | bytes 1048608 | tf_op jit(solution)/shard_map/ppermute | solution.py:256
  79.9 3.2 %shard_map.80 = bf16[256,4096]{1,0:T(8,128)(2,1)S(1)} custom-call(s32[2]{0:T(128)S(1)} %pad_add_fusion.place, bf16[512,512]{1,0:T(8,128)(2,1)S(1)} %bitcast.21, bf16[256,4096]{1,0:T(8,128)(2,1)} %bitcast.34, bf16[256,1024]{1,0:T(8,128)(2,1)S(1)} %collective-permute-done.refs_1_, bf16[256,1024]{1,0:T(8,128)(2,1)S(1)} %copy-done.8, ...), custom_call_target="tpu_custom_call" | custom-call | tf_op jit(solution)/shard_map/pallas_call | solution.py:26
  83.2 1.3 copy-done.4
  84.5 4.6 %collective-permute-done.5.refs_1_ = bf16[128,2048]{1,0:T(8,128)(2,1)S(1)} collective-permute-done((bf16[128,2048]{1,0:T(8,128)(2,1)S(1)}, bf16[128,2048]{1,0:T(8,128)(2,1)S(1)}, u32[]{:S(2)}, u32[]{:S(2)}) %collective-permute-start.5) | collective-permute-done | bytes 524320 | tf_op jit(solution)/shard_map/ppermute | solution.py:253
  89.9 5.4 %all-to-all-start.2 = ((bf16[8,32,4096]{2,1,0:T(8,128)(2,1)}), bf16[8,32,4096]{2,1,0:T(8,128)(2,1)}, u32[]{:S(2)}, u32[]{:S(2)}) async-start(bf16[8,32,4096]{2,1,0:T(8,128)(2,1)} %bitcast.26), calls=%async_computation.2 | async-start | bytes 4194304 | tf_op jit(solution)/shard_map/all_to_all | solution.py:226
  95.2 1.8 collective-permute-start.6
  97.6 29.9 %collective-permute-done.3.ids_ref = s32[128,2]{1,0:T(8,128)S(1)} collective-permute-done((s32[128,2]{1,0:T(8,128)}, s32[128,2]{1,0:T(8,128)S(1)}, u32[]{:S(2)}, u32[]{:S(2)}) %collective-permute-start.3) | collective-permute-done | bytes 1056 | tf_op jit(solution)/shard_map/ppermute | solution.py:253
  131.4 1.3 copy-done.6
  132.7 4.8 %all-to-all-start.3 = ((bf16[8,32,4096]{2,1,0:T(8,128)(2,1)}), bf16[8,32,4096]{2,1,0:T(8,128)(2,1)}, u32[]{:S(2)}, u32[]{:S(2)}) async-start(bf16[8,32,4096]{2,1,0:T(8,128)(2,1)} %bitcast.28), calls=%async_computation.3 | async-start | bytes 4194304 | tf_op jit(solution)/shard_map/all_to_all | solution.py:226
  137.6 2.2 shard_map.82
  141.8 2.9 %shard_map.77 = bf16[256,4096]{1,0:T(8,128)(2,1)S(1)} custom-call(s32[2]{0:T(128)S(1)} %pad_add_fusion.place, bf16[512,512]{1,0:T(8,128)(2,1)S(1)} %bitcast.22, bf16[256,4096]{1,0:T(8,128)(2,1)} %bitcast.35, bf16[256,1024]{1,0:T(8,128)(2,1)S(1)} %collective-permute-done.refs_1_, bf16[256,1024]{1,0:T(8,128)(2,1)S(1)} %copy-done.9, bf16[256,2048]{1,0:T(8,128)(2,1)S(1)} %copy-done.1), custom_call_target="tpu_custom_call" | custom-call | tf_op jit(solution)/shard_map/pallas_call | solution.py:26
  144.6 1.3 copy-done.3
  145.9 27.3 %collective-permute-done.7.refs_0_ = bf16[128,2048]{1,0:T(8,128)(2,1)S(1)} collective-permute-done((bf16[128,2048]{1,0:T(8,128)(2,1)S(1)}, bf16[128,2048]{1,0:T(8,128)(2,1)S(1)}, u32[]{:S(2)}, u32[]{:S(2)}) %collective-permute-start.7) | collective-permute-done | bytes 524320 | tf_op jit(solution)/shard_map/ppermute | solution.py:253
  174.0 4.9 %all-to-all-start.4 = ((bf16[8,32,4096]{2,1,0:T(8,128)(2,1)}), bf16[8,32,4096]{2,1,0:T(8,128)(2,1)}, u32[]{:S(2)}, u32[]{:S(2)}) async-start(bf16[8,32,4096]{2,1,0:T(8,128)(2,1)} %bitcast.25), calls=%async_computation.4 | async-start | bytes 4194304 | tf_op jit(solution)/shard_map/all_to_all | solution.py:226
  178.9 4.0 %shard_map.85 = (bf16[256,2048]{1,0:T(8,128)(2,1)S(1)}, bf16[256,2048]{1,0:T(8,128)(2,1)}) custom-call(s32[2]{0:T(128)S(1)} %pad_add_fusion.place, bf16[512,512]{1,0:T(8,128)(2,1)S(1)} %bitcast.23, bf16[256,4096]{1,0:T(8,128)(2,1)S(1)} %bitcast.18, bf16[256,4096]{1,0:T(8,128)(2,1)} %bitcast.10.other_ref), custom_call_target="tpu_custom_call" | custom-call | tf_op jit(solution)/shard_map/pallas_call | solution.py:26
  184.2 1.7 collective-permute-start.8
  186.1 4.6 %shard_map.84 = bf16[512,512]{1,0:T(8,128)(2,1)S(1)} custom-call(s32[2]{0:T(128)S(1)} %pad_add_fusion.place, bf16[256,4096]{1,0:T(8,128)(2,1)S(1)} %bitcast.19, bf16[256,4096]{1,0:T(8,128)(2,1)} %bitcast.10.other_ref, bf16[256,4096]{1,0:T(8,128)(2,1)} %bitcast.36, bf16[256,1024]{1,0:T(8,128)(2,1)S(1)} %collective-permute-done.refs_1_, ...), custom_call_target="tpu_custom_call" | custom-call | tf_op jit(solution)/shard_map/pallas_call | solution.py:26
  191.5 23.8 %collective-permute-done.8.refs_1_ = bf16[128,2048]{1,0:T(8,128)(2,1)S(1)} collective-permute-done((bf16[128,2048]{1,0:T(8,128)(2,1)S(1)}, bf16[128,2048]{1,0:T(8,128)(2,1)S(1)}, u32[]{:S(2)}, u32[]{:S(2)}) %collective-permute-start.8) | collective-permute-done | bytes 524320 | tf_op jit(solution)/shard_map/ppermute | solution.py:253
  217.1 4.7 %all-to-all-start.5 = ((bf16[16,32,512]{2,1,0:T(8,128)(2,1)}), bf16[16,32,512]{2,1,0:T(8,128)(2,1)S(1)}, u32[]{:S(2)}, u32[]{:S(2)}) async-start(bf16[16,32,512]{2,1,0:T(8,128)(2,1)} %bitcast.29), calls=%async_computation.5 | async-start | bytes 1048576 | tf_op jit(solution)/shard_map/all_to_all | solution.py:226
  221.8 8.0 %collective-permute-done.10.refs_1_ = bf16[256,2048]{1,0:T(8,128)(2,1)} collective-permute-done((bf16[256,2048]{1,0:T(8,128)(2,1)}, bf16[256,2048]{1,0:T(8,128)(2,1)}, u32[]{:S(2)}, u32[]{:S(2)}) %collective-permute-start.10) | collective-permute-done | bytes 1048608 | tf_op jit(solution)/shard_map/ppermute | solution.py:256
  231.1 4.8 %shard_map.87 = bf16[256,4096]{1,0:T(8,128)(2,1)} custom-call(s32[2]{0:T(128)S(1)} %pad_add_fusion.place, bf16[512,512]{1,0:T(8,128)(2,1)S(1)} %bitcast.24, bf16[256,4096]{1,0:T(8,128)(2,1)S(1)} %bitcast.20, bf16[256,4096]{1,0:T(8,128)(2,1)} %bitcast.10.other_ref, bf16[256,2048]{1,0:T(8,128)(2,1)S(1)} %copy-done.15, ...), custom_call_target="tpu_custom_call" | custom-call | tf_op jit(solution)/shard_map/pallas_call | solution.py:26
  235.9 3.1 %shard_map.83 = bf16[128,4096]{1,0:T(8,128)(2,1)} custom-call(s32[2]{0:T(128)S(1)} %pad_add_fusion.place, s32[128,2]{1,0:T(8,128)S(1)} %get-tuple-element.16.col_ref, bf16[256,4096]{1,0:T(8,128)(2,1)} %bitcast.12.back_ref, bf16[128,2048]{1,0:T(8,128)(2,1)S(1)} %copy-done.17, bf16[128,2048]{1,0:T(8,128)(2,1)S(1)} %copy-done.21), custom_call_target="tpu_custom_call" | custom-call | tf_op jit(solution)/shard_map/pallas_call | solution.py:26
  (82 shorter events, 21.1 us)
Async XLA Ops:
  0.6 3.5 %copy-start.27 = (s32[128,2]{0,1:T(2,128)S(1)}, s32[128,2]{0,1:T(2,128)}, u32[]{:S(2)}) copy-start(s32[128,2]{0,1:T(2,128)} %param.7) | copy-start | bytes 3076
  0.6 3.6 %copy-start.28 = (s32[128,2]{0,1:T(2,128)S(1)}, s32[128,2]{0,1:T(2,128)}, u32[]{:S(2)}) copy-start(s32[128,2]{0,1:T(2,128)} %param.8) | copy-start | bytes 3076
  0.7 3.7 %copy-start.26 = (bf16[128,2,512]{2,1,0:T(2,128)(2,1)S(1)}, bf16[128,2,512]{2,1,0:T(2,128)(2,1)}, u32[]{:S(2)}) copy-start(bf16[128,2,512]{2,1,0:T(2,128)(2,1)} %param.5) | copy-start | bytes 786436
  0.7 23.6 %copy-start.11 = (bf16[128,4096]{1,0:T(8,128)(2,1)S(1)}, bf16[128,4096]{1,0:T(8,128)(2,1)}, u32[]{:S(2)}) copy-start(bf16[128,4096]{1,0:T(8,128)(2,1)} %refs_0_.1) | copy-start | bytes 3145732
  2.8 12.8 %collective-permute-start = (bf16[256,1024]{1,0:T(8,128)(2,1)S(1)}, bf16[256,1024]{1,0:T(8,128)(2,1)S(1)}, u32[]{:S(2)}, u32[]{:S(2)}) collective-permute-start(bf16[256,1024]{1,0:T(8,128)(2,1)S(1)} %get-tuple-element.30), channel_id=1, source_target_pairs={{0,16},{16,0},{1,17},{17,1},{2,18},{18,2},{3,19},{19,3},{4,20},{20... | collective-permute-start | bytes 1572872 | tf_op jit(solution)/shard_map/ppermute | solution.py:256
  4.2 24.2 %copy-start.22 = (s32[128,2]{1,0:T(8,128)}, s32[128,2]{1,0:T(8,128)S(1)}, u32[]{:S(2)}) copy-start(s32[128,2]{1,0:T(8,128)S(1)} %copy.8.ids_ref) | copy-start | bytes 3076
  15.6 31.0 %all-to-all-start = ((bf16[16,32,512]{2,1,0:T(8,128)(2,1)}), bf16[16,32,512]{2,1,0:T(8,128)(2,1)S(1)}, u32[]{:S(2)}, u32[]{:S(2)}) async-start(bf16[16,32,512]{2,1,0:T(8,128)(2,1)} %bitcast.3), calls=%async_computation | async-start | bytes 1048576 | tf_op jit(solution)/shard_map/all_to_all | solution.py:226
  23.1 22.8 %collective-permute-start.1 = (bf16[256,1024]{1,0:T(8,128)(2,1)}, bf16[256,1024]{1,0:T(8,128)(2,1)S(1)}, u32[]{:S(2)}, u32[]{:S(2)}) collective-permute-start(bf16[256,1024]{1,0:T(8,128)(2,1)} %get-tuple-element.29), channel_id=1, source_target_pairs={{0,16},{16,0},{1,17},{17,1},{2,18},{18,2},{3,19},{19,3},{4,20},{20... | collective-permute-start | bytes 1572872 | tf_op jit(solution)/shard_map/ppermute | solution.py:256
  25.0 20.8 %collective-permute-start.4 = (bf16[128,1024]{1,0:T(8,128)(2,1)S(1)}, bf16[128,1024]{1,0:T(8,128)(2,1)S(1)}, u32[]{:S(2)}, u32[]{:S(2)}) collective-permute-start(bf16[128,1024]{1,0:T(8,128)(2,1)S(1)} %get-tuple-element.34), channel_id=1, source_target_pairs={{0,8},{8,0},{1,9},{9,1},{2,10},{10,2},{3,11},{11,3},{4,12},{12,4},... | collective-permute-start | bytes 786440 | tf_op jit(solution)/shard_map/ppermute | solution.py:253
  46.7 43.2 %all-to-all-start.1 = ((bf16[8,32,4096]{2,1,0:T(8,128)(2,1)}), bf16[8,32,4096]{2,1,0:T(8,128)(2,1)S(1)}, u32[]{:S(2)}, u32[]{:S(2)}) async-start(bf16[8,32,4096]{2,1,0:T(8,128)(2,1)} %bitcast.27), calls=%async_computation.1 | async-start | bytes 4194304 | tf_op jit(solution)/shard_map/all_to_all | solution.py:226
  54.0 25.9 %copy-start.8 = (bf16[256,1024]{1,0:T(8,128)(2,1)S(1)}, bf16[256,1024]{1,0:T(8,128)(2,1)}, u32[]{:S(2)}) copy-start(bf16[256,1024]{1,0:T(8,128)(2,1)} %copy-done.7) | copy-start | bytes 1572868
  55.5 24.4 %collective-permute-start.2 = (bf16[256,2048]{1,0:T(8,128)(2,1)S(1)}, bf16[256,2048]{1,0:T(8,128)(2,1)S(1)}, u32[]{:S(2)}, u32[]{:S(2)}) collective-permute-start(bf16[256,2048]{1,0:T(8,128)(2,1)S(1)} %slice.34), channel_id=1, source_target_pairs={{0,16},{16,0},{1,17},{17,1},{2,18},{18,2},{3,19},{19,3},{4,20},{20... | collective-permute-start | bytes 3145736 | tf_op jit(solution)/shard_map/ppermute | solution.py:256
  56.8 32.2 %collective-permute-start.5 = (bf16[128,2048]{1,0:T(8,128)(2,1)S(1)}, bf16[128,2048]{1,0:T(8,128)(2,1)S(1)}, u32[]{:S(2)}, u32[]{:S(2)}) collective-permute-start(bf16[128,2048]{1,0:T(8,128)(2,1)S(1)} %slice.28), channel_id=1, source_target_pairs={{0,8},{8,0},{1,9},{9,1},{2,10},{10,2},{3,11},{11,3},{4,12},{12,4},... | collective-permute-start | bytes 1572872 | tf_op jit(solution)/shard_map/ppermute | solution.py:253
  79.9 3.2 %copy-start = (bf16[256,2048]{1,0:T(8,128)(2,1)}, bf16[256,2048]{1,0:T(8,128)(2,1)S(1)}, u32[]{:S(2)}) copy-start(bf16[256,2048]{1,0:T(8,128)(2,1)S(1)} %collective-permute-done.2.refs_3_) | copy-start | bytes 3145732
  89.9 42.9 %all-to-all-start.2 = ((bf16[8,32,4096]{2,1,0:T(8,128)(2,1)}), bf16[8,32,4096]{2,1,0:T(8,128)(2,1)}, u32[]{:S(2)}, u32[]{:S(2)}) async-start(bf16[8,32,4096]{2,1,0:T(8,128)(2,1)} %bitcast.26), calls=%async_computation.2 | async-start | bytes 4194304 | tf_op jit(solution)/shard_map/all_to_all | solution.py:226
  95.2 33.9 %collective-permute-start.6 = (bf16[128,1024]{1,0:T(8,128)(2,1)}, bf16[128,1024]{1,0:T(8,128)(2,1)S(1)}, u32[]{:S(2)}, u32[]{:S(2)}) collective-permute-start(bf16[128,1024]{1,0:T(8,128)(2,1)} %get-tuple-element.33), channel_id=1, source_target_pairs={{0,8},{8,0},{1,9},{9,1},{2,10},{10,2},{3,11},{11,3},{4,12},{12,4},... | collective-permute-start | bytes 786440 | tf_op jit(solution)/shard_map/ppermute | solution.py:253
  97.0 30.5 %collective-permute-start.3 = (s32[128,2]{1,0:T(8,128)}, s32[128,2]{1,0:T(8,128)S(1)}, u32[]{:S(2)}, u32[]{:S(2)}) collective-permute-start(s32[128,2]{1,0:T(8,128)} %copy-done.22), channel_id=1, source_target_pairs={{0,8},{8,0},{1,9},{9,1},{2,10},{10,2},{3,11},{11,3},{4,12},{12,4},... | collective-permute-start | bytes 3080 | tf_op jit(solution)/shard_map/ppermute | solution.py:253
  132.7 4.9 %copy-start.24 = (s32[128,2]{1,0:T(8,128)S(1)}, s32[128,2]{1,0:T(8,128)}, u32[]{:S(2)}) copy-start(s32[128,2]{1,0:T(8,128)} %copy-done.23) | copy-start | bytes 3076
  132.7 41.3 %all-to-all-start.3 = ((bf16[8,32,4096]{2,1,0:T(8,128)(2,1)}), bf16[8,32,4096]{2,1,0:T(8,128)(2,1)}, u32[]{:S(2)}, u32[]{:S(2)}) async-start(bf16[8,32,4096]{2,1,0:T(8,128)(2,1)} %bitcast.28), calls=%async_computation.3 | async-start | bytes 4194304 | tf_op jit(solution)/shard_map/all_to_all | solution.py:226
  137.6 4.2 %copy-start.1 = (bf16[256,2048]{1,0:T(8,128)(2,1)S(1)}, bf16[256,2048]{1,0:T(8,128)(2,1)}, u32[]{:S(2)}) copy-start(bf16[256,2048]{1,0:T(8,128)(2,1)} %copy-done) | copy-start | bytes 3145732
  137.6 4.2 %copy-start.9 = (bf16[256,1024]{1,0:T(8,128)(2,1)S(1)}, bf16[256,1024]{1,0:T(8,128)(2,1)}, u32[]{:S(2)}) copy-start(bf16[256,1024]{1,0:T(8,128)(2,1)} %copy-done.7) | copy-start | bytes 1572868
  140.8 32.5 %collective-permute-start.7 = (bf16[128,2048]{1,0:T(8,128)(2,1)S(1)}, bf16[128,2048]{1,0:T(8,128)(2,1)S(1)}, u32[]{:S(2)}, u32[]{:S(2)}) collective-permute-start(bf16[128,2048]{1,0:T(8,128)(2,1)S(1)} %get-tuple-element.32), channel_id=1, source_target_pairs={{0,8},{8,0},{1,9},{9,1},{2,10},{10,2},{3,11},{11,3},{4,12},{12,4},... | collective-permute-start | bytes 1572872 | tf_op jit(solution)/shard_map/ppermute | solution.py:253
  174.0 43.1 %all-to-all-start.4 = ((bf16[8,32,4096]{2,1,0:T(8,128)(2,1)}), bf16[8,32,4096]{2,1,0:T(8,128)(2,1)}, u32[]{:S(2)}, u32[]{:S(2)}) async-start(bf16[8,32,4096]{2,1,0:T(8,128)(2,1)} %bitcast.25), calls=%async_computation.4 | async-start | bytes 4194304 | tf_op jit(solution)/shard_map/all_to_all | solution.py:226
  178.9 5.3 %copy-start.25 = (bf16[128,2048]{1,0:T(8,128)(2,1)S(1)}, bf16[128,2048]{1,0:T(8,128)(2,1)}, u32[]{:S(2)}) copy-start(bf16[128,2048]{1,0:T(8,128)(2,1)} %get-tuple-element.31) | copy-start | bytes 1572868
  178.9 7.2 %copy-start.2 = (bf16[256,2048]{1,0:T(8,128)(2,1)S(1)}, bf16[256,2048]{1,0:T(8,128)(2,1)}, u32[]{:S(2)}) copy-start(bf16[256,2048]{1,0:T(8,128)(2,1)} %copy-done) | copy-start | bytes 3145732
  178.9 7.2 %copy-start.10 = (bf16[256,1024]{1,0:T(8,128)(2,1)S(1)}, bf16[256,1024]{1,0:T(8,128)(2,1)}, u32[]{:S(2)}) copy-start(bf16[256,1024]{1,0:T(8,128)(2,1)} %copy-done.7) | copy-start | bytes 1572868
  182.9 33.2 %collective-permute-start.9 = (bf16[256,2048]{1,0:T(8,128)(2,1)S(1)}, bf16[256,2048]{1,0:T(8,128)(2,1)S(1)}, u32[]{:S(2)}, u32[]{:S(2)}) collective-permute-start(bf16[256,2048]{1,0:T(8,128)(2,1)S(1)} %get-tuple-element.26), channel_id=1, source_target_pairs={{0,16},{16,0},{1,17},{17,1},{2,18},{18,2},{3,19},{19,3},{4,20},{20... | collective-permute-start | bytes 3145736 | tf_op jit(solution)/shard_map/ppermute | solution.py:256
  184.2 31.1 %collective-permute-start.8 = (bf16[128,2048]{1,0:T(8,128)(2,1)S(1)}, bf16[128,2048]{1,0:T(8,128)(2,1)S(1)}, u32[]{:S(2)}, u32[]{:S(2)}) collective-permute-start(bf16[128,2048]{1,0:T(8,128)(2,1)S(1)} %copy-done.25), channel_id=1, source_target_pairs={{0,8},{8,0},{1,9},{9,1},{2,10},{10,2},{3,11},{11,3},{4,12},{12,4},... | collective-permute-start | bytes 1572872 | tf_op jit(solution)/shard_map/ppermute | solution.py:253
  185.9 44.0 %collective-permute-start.10 = (bf16[256,2048]{1,0:T(8,128)(2,1)}, bf16[256,2048]{1,0:T(8,128)(2,1)}, u32[]{:S(2)}, u32[]{:S(2)}) collective-permute-start(bf16[256,2048]{1,0:T(8,128)(2,1)} %get-tuple-element.28), channel_id=1, source_target_pairs={{0,16},{16,0},{1,17},{17,1},{2,18},{18,2},{3,19},{19,3},{4,20},{20... | collective-permute-start | bytes 3145736 | tf_op jit(solution)/shard_map/ppermute | solution.py:256
  217.1 21.9 %all-to-all-start.5 = ((bf16[16,32,512]{2,1,0:T(8,128)(2,1)}), bf16[16,32,512]{2,1,0:T(8,128)(2,1)S(1)}, u32[]{:S(2)}, u32[]{:S(2)}) async-start(bf16[16,32,512]{2,1,0:T(8,128)(2,1)} %bitcast.29), calls=%async_computation.5 | async-start | bytes 1048576 | tf_op jit(solution)/shard_map/all_to_all | solution.py:226
  231.1 4.8 %copy-start.17 = (bf16[128,2048]{1,0:T(8,128)(2,1)S(1)}, bf16[128,2048]{1,0:T(8,128)(2,1)}, u32[]{:S(2)}) copy-start(bf16[128,2048]{1,0:T(8,128)(2,1)} %copy-done.16) | copy-start | bytes 1572868
  231.1 4.8 %copy-start.21 = (bf16[128,2048]{1,0:T(8,128)(2,1)S(1)}, bf16[128,2048]{1,0:T(8,128)(2,1)}, u32[]{:S(2)}) copy-start(bf16[128,2048]{1,0:T(8,128)(2,1)} %copy-done.20) | copy-start | bytes 1572868
  (14 other events, 16.0 us)

commit v3 on v0

v3 whole, which is shorter than its diff:
```python
import functools

import jax
import jax.numpy as jnp
from jax import lax
from jax.experimental import pallas as pl
from jax.experimental.pallas import tpu as pltpu
from jax.sharding import Mesh
from jax.sharding import PartitionSpec as P

F32 = jnp.float32
BF16 = jnp.bfloat16
I32 = jnp.int32
VMEM = pl.BlockSpec(memory_space=pltpu.VMEM)
SMEM = pl.BlockSpec(memory_space=pltpu.SMEM)
STEP = 1024
PLANES = 4
PAIR = 2
COST = 1 << 38


def dot(a, b, ca=1, cb=0):
    return lax.dot_general(a, b, (((ca,), (cb,)), ((), ())), preferred_element_type=F32)


def call(body, outs, *args, cost=0, scratch=()):
    many = isinstance(outs, (list, tuple))
    return pl.pallas_call(
        body,
        out_shape=outs,
        in_specs=[SMEM] + [VMEM] * (len(args) - 1),
        out_specs=[VMEM] * len(outs) if many else VMEM,
        scratch_shapes=scratch,
        name=(body.func if isinstance(body, functools.partial) else body).__name__,
        cost_estimate=pl.CostEstimate(flops=cost, bytes_accessed=0, transcendentals=0),
        compiler_params=pltpu.CompilerParams(vmem_limit_bytes=16 * 1024 * 1024),
    )(*args)


def shaped(shape, dtype=BF16):
    return jax.ShapeDtypeStruct(tuple(shape), dtype)


def iota(shape, dim):
    return lax.broadcasted_iota(I32, shape, dim)


def steps(width):
    step = min(STEP, width)
    return [slice(c, c + step) for c in range(0, width, step)]


def slot_rows(ids, experts, capacity):
    tokens = ids.shape[0]
    lanes = iota((tokens, experts), 1)
    earlier = (iota((tokens, tokens), 0) > iota((tokens, tokens), 1)).astype(BF16)
    eye = iota((tokens, tokens), 0) == iota((tokens, tokens), 1)
    cols, rows = [], []
    base = jnp.zeros((1, experts), F32)
    for k in range(ids.shape[1]):
        chosen = ids[:, k : k + 1]
        one_hot = (chosen == lanes).astype(F32)
        before = dot(earlier, one_hot.astype(BF16)) + base
        ordinal = jnp.sum(before * one_hot, axis=1, keepdims=True)
        base = base + jnp.sum(one_hot, axis=0, keepdims=True)
        col = chosen.astype(F32) * capacity + ordinal
        row = jnp.sum(jnp.where(eye, jnp.broadcast_to(col, (tokens, tokens)), 0.0), axis=0, keepdims=True)
        cols.append(col.astype(I32))
        rows.append(row.astype(I32))
    return cols, rows


def swap_halves(x, flag):
    n = x.shape[1] // 2
    return jnp.where(flag, jnp.concatenate([x[:, n:], x[:, :n]], 1), x)


def prepare_body(experts, capacity, top, swap, place, ids_ref, num_ref, hid_ref, row_ref, col_ref, send_ref):
    tokens = ids_ref.shape[0]
    units = hid_ref.shape[1] // top
    cols, rows = slot_rows(ids_ref[...], experts, capacity)
    numerators = num_ref[...].astype(F32)
    total = jnp.sum(numerators, axis=1, keepdims=True)
    target = iota((experts * capacity, tokens), 0)
    acc = None
    for k in range(top):
        row_ref[k : k + 1, :] = rows[k]
        col_ref[:, k : k + 1] = cols[k]
        share = numerators[:, k : k + 1] / total
        scaled = (share * hid_ref[:, k * units : (k + 1) * units].astype(F32)).astype(BF16)
        part = dot((target == rows[k]).astype(BF16), scaled)
        acc = part if acc is None else acc + part
    out = acc.astype(BF16)
    send_ref[...] = swap_halves(out, place[1] == 1) if swap else out


def rows_body(experts, capacity, place, *refs):
    ids_refs, row_refs = refs[:PLANES], refs[PLANES:]
    found = [slot_rows(ref[...], experts, capacity)[1] for ref in ids_refs]
    for i, row_ref in enumerate(row_refs):
        for k in range(row_ref.shape[0]):
            row = found[PLANES - 1][k]
            for j in range(PLANES - 1):
                row = jnp.where((place[0] ^ i) == j, found[j][k], row)
            row_ref[k : k + 1, :] = row


def picks(place, peers, capacity, row_refs):
    r = iota((peers * PAIR * capacity, 1), 0)
    peer = r // (PAIR * capacity)
    which = (r // capacity) % PAIR
    target = (place[0] * peers + peer) * capacity + r % capacity
    blocks = []
    for j, row_ref in enumerate(row_refs):
        hit = None
        for k in range(row_ref.shape[0]):
            h = target == row_ref[k : k + 1, :]
            hit = h if hit is None else hit | h
        blocks.append((hit & (which == j)).astype(BF16))
    return jnp.concatenate(blocks, 1)


def pick_body(peers, capacity, offset, place, *refs):
    *row_refs, grad_ref, out_ref = refs
    tokens = row_refs[0].shape[1]
    n = PAIR * capacity
    groups = PLANES // PAIR
    for g in range(groups):
        pick = picks(place, peers, capacity, row_refs[g * PAIR : (g + 1) * PAIR])
        for at in steps(out_ref.shape[1]):
            cols = slice(offset + at.start, offset + at.stop)
            res = dot(pick, grad_ref[g * PAIR * tokens : (g + 1) * PAIR * tokens, cols]).astype(BF16)
            for k in range(peers):
                o = (k * groups + g) * n
                out_ref[o : o + n, at] = res[k * n : (k + 1) * n]


def combine_body(peers, capacity, place, *refs):
    *row_refs, back_ref, out_ref = refs
    tokens = row_refs[0].shape[1]
    n = PAIR * capacity
    groups = PLANES // PAIR
    for g in range(groups):
        pick = picks(place, peers, capacity, row_refs[g * PAIR : (g + 1) * PAIR])
        for at in steps(out_ref.shape[1]):
            rows = [back_ref[(k * groups + g) * n : (k * groups + g + 1) * n, at] for k in range(peers)]
            both = dot(pick, jnp.concatenate(rows, 0), 0, 0).astype(BF16)
            out_ref[g * PAIR * tokens : (g + 1) * PAIR * tokens, at] = both


def reorder(x, outer, inner, capacity):
    return jnp.concatenate(
        [
            x[(a * inner + b) * capacity : (a * inner + b + 1) * capacity]
            for b in range(inner)
            for a in range(outer)
        ],
        0,
    )


def arrange_body(peers, capacity, place, hid_ref, out_ref):
    out_ref[...] = reorder(hid_ref[...].astype(F32), PLANES, peers, capacity).astype(BF16)


def forward_body(offset, place, hid_ref, *refs):
    *weights, out_ref = refs
    hid = hid_ref[...]
    for at in steps(out_ref.shape[1]):
        acc, r = None, 0
        for i, w in enumerate(weights):
            o = offset if i == 0 else 0
            part = dot(hid[:, r : r + w.shape[0]], w[:, o + at.start : o + at.stop])
            acc = part if acc is None else acc + part
            r += w.shape[0]
        out_ref[:, at] = acc.astype(BF16)


def weight_grad_body(lo, hi, place, hid_ref, grad_ref, out_ref):
    for at in steps(out_ref.shape[1]):
        out_ref[:, at] = dot(hid_ref[:, lo:hi], grad_ref[:, at], 0, 0).astype(BF16)


def average_body(replicas, place, *refs):
    *pieces, out_ref = refs
    n = len(pieces) // 2
    c = 0
    for a, b in zip(pieces[:n], pieces[n:]):
        for at in steps(a.shape[1]):
            total = a[:, at].astype(F32) + b[:, at].astype(F32)
            out_ref[:, c + at.start : c + at.stop] = (total / replicas).astype(BF16)
        c += a.shape[1]


def back_dots(grad_ref, weights, offset):
    w = weights[0][:, offset : offset + grad_ref.shape[1]]
    return [dot(grad_ref[...], w, 1, 1)] + [dot(grad_ref[...], x[...], 1, 1) for x in weights[1:]]


def backward_first_body(offset, place, grad_ref, *refs):
    *weights, out_ref = refs
    r = 0
    for part in back_dots(grad_ref, weights, offset):
        out_ref[:, r : r + part.shape[1]] = part
        r += part.shape[1]


def backward_last_body(peers, capacity, offset, place, first_ref, grad_ref, *refs):
    *weights, out_ref = refs
    r = 0
    for part in back_dots(grad_ref, weights, offset):
        m = part.shape[1]
        total = first_ref[:, r : r + m] + part
        out_ref[:, r : r + m] = reorder(total, peers, PLANES, capacity).astype(BF16)
        r += m


def hidden_grad_body(top, swap, place, col_ref, num_ref, back_ref, out_ref):
    tokens = col_ref.shape[0]
    rows, units = back_ref.shape
    numerators = num_ref[...].astype(F32)
    total = jnp.sum(numerators, axis=1, keepdims=True)
    target = iota((tokens, rows), 1)
    for k in range(top):
        hit = (target == col_ref[:, k : k + 1]).astype(BF16)
        got = (numerators[:, k : k + 1] / total * dot(hit, back_ref[...])).astype(BF16)
        out_ref[:, k * units : (k + 1) * units] = swap_halves(got, place[1] == 1) if swap else got


def after(x, *others):
    return lax.optimization_barrier((x, *others))[0]


def exchange(x, axes):
    return lax.all_to_all(x, axes, split_axis=0, concat_axis=0, tiled=True)


def cut(x, n):
    m = x.shape[1] // n
    return [x[:, i * m : (i + 1) * m] for i in range(n)]


def on_device(hidden_in, out_grad, expert_ids, gate_num, down_weight):
    tokens, top, units = hidden_in.shape
    width = out_grad.shape[1]
    peers = lax.axis_size("p")
    experts = PLANES * peers
    replicas = lax.axis_size("dp")
    capacity = 4 * tokens // experts
    share = units // replicas
    pair = replicas == 2
    z = lax.axis_index("z")
    place = jnp.stack([lax.axis_index("z"), lax.axis_index("dp"), lax.axis_index("p")]).astype(I32)
    part = functools.partial
    row_shape, col_shape = shaped((top, tokens), I32), shaped((tokens, top), I32)
    piece = width // 2
    total_rows = experts * capacity

    def to_replica(x):
        return lax.ppermute(x, "dp", [(0, 1), (1, 0)])

    weight = down_weight[0]
    if pair:
        w_a = cut(weight, 2)[0]
        mine = weight
    else:
        theirs = []
        mine = lax.all_gather(weight, "dp", axis=0, tiled=True)

    row_own, col_own, send_hidden = call(
        part(prepare_body, experts, capacity, top, pair),
        [row_shape, col_shape, shaped((total_rows, units))],
        place, expert_ids, gate_num, hidden_in.reshape(tokens, top * units),
    )
    grads = lax.all_gather(out_grad, "z", axis=0, tiled=True)
    if pair:
        theirs = [to_replica(w_a), to_replica(cut(after(weight, send_hidden), 2)[1])]
    hid = exchange(send_hidden, ("z", "p"))
    hid = call(part(arrange_body, peers, capacity), shaped((total_rows, units)), place, hid)
    near = [expert_ids] + [
        lax.ppermute(expert_ids, "z", [(i, i ^ j) for i in range(PLANES)]) for j in range(1, PLANES)
    ]
    chunk = shaped((total_rows, piece))

    def forward(c):
        weights = [mine] + ([theirs[c]] if pair else [])
        return call(part(forward_body, c * piece), chunk, place, hid, *weights, cost=COST)

    def combine(rows, x):
        return call(
            part(combine_body, peers, capacity), shaped((PLANES * tokens, piece)), place, *rows, x
        )

    def reduce(x):
        return lax.psum_scatter(x, "z", scatter_dimension=0, tiled=True)

    def pick(rows, c):
        return call(part(pick_body, peers, capacity, c * piece), chunk, place, *rows, grads, cost=COST)

    def weight_grad(x, lo, hi, cost=0):
        return call(
            part(weight_grad_body, lo, hi), shaped((hi - lo, piece)), place, hid, x, cost=cost
        )

    out_a, out_b = forward(0), forward(1)
    done_a = after(exchange(out_a, "p"), out_b)
    done_b = exchange(after(out_b, done_a), "p")
    rows = call(
        part(rows_body, experts, capacity), [row_shape] * PLANES, after(place, done_a), *near
    )
    part_a = combine(rows, done_a)
    pick_a = pick(rows, 0)
    done_b = after(done_b, part_a)
    layer_a = reduce(after(part_a, done_b))
    sent_a = exchange(after(pick_a, done_b), "p")
    part_b = combine(rows, done_b)
    layer_b = reduce(part_b)
    pick_b = pick(rows, 1)
    sent_a = after(sent_a, part_b, pick_b)
    sent_b = exchange(after(pick_b, sent_a), "p")
    lo, hi = (share, units) if pair else (0, units)
    other_a = weight_grad(sent_a, lo, hi)
    own_a = weight_grad(sent_a, 0, share) if pair else jnp.zeros((share, piece), BF16)
    first = call(
        part(backward_first_body, 0), shaped((total_rows, units), F32), place, sent_a, mine, *theirs[:1]
    )
    sent_b = after(sent_b, other_a, own_a, first)
    other_b = weight_grad(sent_b, lo, hi)
    grad_rows = call(
        part(backward_last_body, peers, capacity, piece), shaped((total_rows, units)),
        after(place, other_b), first, sent_b, mine, *theirs[1:],
    )
    back_rows = exchange(grad_rows, ("z", "p"))
    if pair:
        own_b = weight_grad(after(sent_b, grad_rows), 0, share, cost=COST)
    else:
        own_b = jnp.zeros((share, piece), BF16)
    other_grads, own_grads, back = [other_a, other_b], [own_a, own_b], [layer_a, layer_b]
    if pair:
        other_grads = [to_replica(g) for g in other_grads]
    else:
        other_grads = [
            lax.psum_scatter(g, "dp", scatter_dimension=0, tiled=True) for g in other_grads
        ]

    layer_out = jnp.concatenate([after(x, own_b) for x in back], 1)
    down_grad = call(
        part(average_body, replicas), shaped((share, width)), after(place, layer_out), *own_grads, *other_grads
    )
    hidden_grad = call(
        part(hidden_grad_body, top, pair), shaped((tokens, top * units)), after(place, down_grad), col_own, gate_num, back_rows
    )
    return (layer_out, hidden_grad.reshape(tokens, top, units), down_grad[None])


def solution(mesh):
    replicas, experts = mesh.devices.shape
    planes = Mesh(mesh.devices.reshape(replicas, PLANES, experts // PLANES), ("dp", "z", "p"))
    tokens = ("dp", "z", "p")
    return jax.shard_map(
        on_device,
        mesh=planes,
        in_specs=(
            P(tokens, None, None),
            P(tokens, None),
            P(tokens, None),
            P(tokens, None),
            P(("z", "p"), "dp", None),
        ),
        out_specs=(
            P(tokens, None),
            P(tokens, None, None),
            P(("z", "p"), "dp", None),
        ),
        check_vma=False,
    )
```

time: 295 us -> 226 us (0.77)
  waiting for transfers between devices: 187 us -> 96.2 us
  Pallas kernels: 0 us -> 40 us
  starting transfers between devices: 28.2 us -> 48.2 us
  matrix products: 19.6 us -> 0 us
  other arithmetic: 14.1 us -> 0.08 us
  local copies, waits for them, and re-layouts: 30.5 us -> 24.1 us
    all_to_all x5 -> x6, waiting for transfers between devices: 187 us -> 52.5 us  [exchange(): return lax.all_to_all(x, axes, split_axis=0, concat_axis=0, tiled=True)]
    pallas_call x0 -> x17, Pallas kernels: none -> 40 us  [call(): pl.pallas_call(body, out_shape=outs, in_specs=[SMEM] + [VMEM] * (len(args...]
    ppermute x0 -> x7, waiting for transfers between devices: none -> 25.4 us  [the longest x3 14.3 us: on_device(): lax.ppermute(expert_ids, 'z', [(i, i ^ j) for i in range(PLANES)])]
    dot_general x3 -> x0, matrix products: 19.6 us -> none  [the longest x1 6.62 us: on_device(): lax.dot_general(recv_grad, gathered, (((1,), (1,)), ((), ())), preferred_...]
    unnamed x5 -> x48, local copies, waits for them, and re-layouts: 0.79 us -> 17.8 us
    reduce_scatter x1 -> x2, waiting for transfers between devices: 0.01 us -> 15.1 us  [reduce(): return lax.psum_scatter(x, 'z', scatter_dimension=0, tiled=True)]
    all_to_all x5 -> x6, starting transfers between devices: 28.1 us -> 41.3 us  [exchange(): return lax.all_to_all(x, axes, split_axis=0, concat_axis=0, tiled=True)]
    scatter x3 -> x0, local copies, waits for them, and re-layouts: 10.6 us -> none  [the longest x1 7.04 us: on_device(): jnp.zeros((buffer_rows, width), jnp.bfloat16).at[target_row]]
  transfers between devices with their start and end apart: 7 -> 16, of which waited for: 4 -> 11; matrix products, arithmetic and copies ran while one was open for 18% -> 2% of each run, Pallas kernels for 0% -> 17%
where the time goes in v3:
time: 226 us; the launch traced here: 223 us
  waiting for transfers between devices  96.2 us (43%)
  starting transfers between devices  48.2 us (21%)
  Pallas kernels  40 us (18%)
  local copies, waits for them, and re-layouts  24.1 us (11%)
  between operations  14 us (6%)
    all_to_all x6, waiting for transfers between devices, exchange(): return lax.all_to_all(x, axes, split_axis=0, concat_axis=0, tiled=True)  52.5 us
    all_to_all x6, starting transfers between devices, exchange(): return lax.all_to_all(x, axes, split_axis=0, concat_axis=0, tiled=True)  41.3 us
    pallas_call x17, Pallas kernels, call(): pl.pallas_call(body, out_shape=outs, in_specs=[SMEM] + [VMEM] * (len(args...  40 us
    unnamed x48, local copies, waits for them, and re-layouts  17.8 us
    reduce_scatter x2, waiting for transfers between devices, reduce(): return lax.psum_scatter(x, 'z', scatter_dimension=0, tiled=True)  15.1 us
    ppermute x3, waiting for transfers between devices, on_device(): lax.ppermute(expert_ids, 'z', [(i, i ^ j) for i in range(PLANES)])  14.3 us
    ppermute x4, waiting for transfers between devices, to_replica(): return lax.ppermute(x, 'dp', [(0, 1), (1, 0)])  11.2 us
  transfers between devices with their start and end apart: 16, of which 11 were waited for; matrix products, arithmetic and copies ran while one was open for 2% of the time, Pallas kernels for 17%

profile of v3, /device:TPU:11, one launch (start us, length us, event | category | flops | bytes accessed | tf_op | source)
XLA Modules:
  0.0 222.5 jit_solution(2002328436483646183)
XLA Ops:
  7.2 2.5 %slice.8 = bf16[256,2048]{1,0:T(8,128)(2,1)} slice(bf16[256,4096]{1,0:T(8,128)(2,1)} %bitcast.19), slice={[0:256], [0:2048]} | slice | bytes 2097152 | tf_op jit(solution)/shard_map/slice | solution.py:240
  11.3 2.2 prepare_body.1
  13.4 6.8 %all-to-all-start = ((bf16[16,32,512]{2,1,0:T(8,128)(2,1)}), bf16[16,32,512]{2,1,0:T(8,128)(2,1)S(1)}, u32[]{:S(2)}, u32[]{:S(2)}) async-start(bf16[16,32,512]{2,1,0:T(8,128)(2,1)} %bitcast.3), calls=%async_computation | async-start | bytes 1048576 | tf_op jit(solution)/shard_map/all_to_all | solution.py:235
  21.7 12.6 %all-to-all-done = bf16[16,32,512]{2,1,0:T(8,128)(2,1)S(1)} async-done(((bf16[16,32,512]{2,1,0:T(8,128)(2,1)}), bf16[16,32,512]{2,1,0:T(8,128)(2,1)S(1)}, u32[]{:S(2)}, u32[]{:S(2)}) %all-to-all-start) | async-done | bytes 524320 | tf_op jit(solution)/shard_map/all_to_all | solution.py:235
  34.9 2.5 %forward_body.2 = bf16[512,2048]{1,0:T(8,128)(2,1)S(1)} custom-call(s32[3]{0:T(128)S(1)} %pad_add_fusion.place, bf16[512,512]{1,0:T(8,128)(2,1)S(1)} %arrange_body.1.hid_ref, bf16[256,4096]{1,0:T(8,128)(2,1)S(1)} %bitcast.21, bf16[256,2048]{1,0:T(8,128)(2,1)} %collective-permute-done.refs_1_), custom_call_target="tpu_custom_call" | custom-call | flops 274877906944 | tf_op jit(solution)/shard_map/forward_body/pallas_call | solution.py:28
  38.7 6.6 %all-to-all-start.1 = ((bf16[4,128,2048]{2,1,0:T(8,128)(2,1)}), bf16[4,128,2048]{2,1,0:T(8,128)(2,1)}, u32[]{:S(2)}, u32[]{:S(2)}) async-start(bf16[4,128,2048]{2,1,0:T(8,128)(2,1)} %bitcast.28), calls=%async_computation.1 | async-start | bytes 4194304 | tf_op jit(solution)/shard_map/all_to_all | solution.py:235
  45.3 11.2 %collective-permute-done.1.refs_1_ = bf16[256,2048]{1,0:T(8,128)(2,1)} collective-permute-done((bf16[256,2048]{1,0:T(8,128)(2,1)}, bf16[256,2048]{1,0:T(8,128)(2,1)}, u32[]{:S(2)}, u32[]{:S(2)}) %collective-permute-start.1) | collective-permute-done | bytes 1048608 | tf_op jit(solution)/shard_map/ppermute | solution.py:260
  56.5 2.5 %forward_body.3 = bf16[512,2048]{1,0:T(8,128)(2,1)S(1)} custom-call(s32[3]{0:T(128)S(1)} %pad_add_fusion.place, bf16[512,512]{1,0:T(8,128)(2,1)S(1)} %arrange_body.1.hid_ref, bf16[256,4096]{1,0:T(8,128)(2,1)S(1)} %bitcast.22, bf16[256,2048]{1,0:T(8,128)(2,1)} %collective-permute-done.1.refs_1_), custom_call_target="tpu_custom_call" | custom-call | flops 274877906944 | tf_op jit(solution)/shard_map/forward_body/pallas_call | solution.py:28
  60.3 8.9 %all-to-all-done.1 = bf16[4,128,2048]{2,1,0:T(8,128)(2,1)} async-done(((bf16[4,128,2048]{2,1,0:T(8,128)(2,1)}), bf16[4,128,2048]{2,1,0:T(8,128)(2,1)}, u32[]{:S(2)}, u32[]{:S(2)}) %all-to-all-start.1) | async-done | bytes 2097184 | tf_op jit(solution)/shard_map/all_to_all | solution.py:235
  69.2 6.5 %all-to-all-start.2 = ((bf16[4,128,2048]{2,1,0:T(8,128)(2,1)}), bf16[4,128,2048]{2,1,0:T(8,128)(2,1)}, u32[]{:S(2)}, u32[]{:S(2)}) async-start(bf16[4,128,2048]{2,1,0:T(8,128)(2,1)} %bitcast.25), calls=%async_computation.2 | async-start | bytes 4194304 | tf_op jit(solution)/shard_map/all_to_all | solution.py:235
  75.7 3.5 %collective-permute-start.3 = (s32[128,2]{1,0:T(8,128)S(1)}, s32[128,2]{1,0:T(8,128)S(1)}, u32[]{:S(2)}, u32[]{:S(2)}) collective-permute-start(s32[128,2]{1,0:T(8,128)S(1)} %copy-done.16), channel_id=1, source_target_pairs={{0,8},{4,12},{8,0},{12,4},{1,9},{5,13},{9,1},{13,5},{2,10},{6,14},... | collective-permute-start | bytes 3080 | tf_op jit(solution)/shard_map/ppermute | solution.py:281
  79.2 3.5 %collective-permute-done.2.refs_1_ = s32[128,2]{1,0:T(8,128)S(1)} collective-permute-done((s32[128,2]{1,0:T(8,128)S(1)}, s32[128,2]{1,0:T(8,128)S(1)}, u32[]{:S(2)}, u32[]{:S(2)}) %collective-permute-start.2) | collective-permute-done | bytes 1056 | tf_op jit(solution)/shard_map/ppermute | solution.py:281
  82.7 3.2 %collective-permute-done.3.refs_2_ = s32[128,2]{1,0:T(8,128)S(1)} collective-permute-done((s32[128,2]{1,0:T(8,128)S(1)}, s32[128,2]{1,0:T(8,128)S(1)}, u32[]{:S(2)}, u32[]{:S(2)}) %collective-permute-start.3) | collective-permute-done | bytes 1056 | tf_op jit(solution)/shard_map/ppermute | solution.py:281
  85.9 7.5 %collective-permute-done.4.refs_3_ = s32[128,2]{1,0:T(8,128)S(1)} collective-permute-done((s32[128,2]{1,0:T(8,128)S(1)}, s32[128,2]{1,0:T(8,128)S(1)}, u32[]{:S(2)}, u32[]{:S(2)}) %collective-permute-start.4) | collective-permute-done | bytes 1056 | tf_op jit(solution)/shard_map/ppermute | solution.py:281
  95.1 2.4 %combine_body.2 = bf16[512,2048]{1,0:T(8,128)(2,1)S(1)} custom-call(s32[3]{0:T(128)S(1)} %pad_add_fusion.place, s32[2,128]{1,0:T(2,128)S(1)} %get-tuple-element.29.refs_0_, s32[2,128]{1,0:T(2,128)S(1)} %get-tuple-element.30.refs_1_, s32[2,128]{1,0:T(2,128)S(1)} %get-tuple-element.31.refs_2_, s32[2,128]{1,0:T(2,128)S(1)} %get-tuple-element.32.refs_3_, ...), custom_call_target="tpu_custom_call" | custom-call | tf_op jit(solution)/shard_map/combine_body/pallas_call | solution.py:28
  99.6 2.4 %combine_body.3 = bf16[512,2048]{1,0:T(8,128)(2,1)S(1)} custom-call(s32[3]{0:T(128)S(1)} %pad_add_fusion.place, s32[2,128]{1,0:T(2,128)S(1)} %get-tuple-element.29.refs_0_, s32[2,128]{1,0:T(2,128)S(1)} %get-tuple-element.30.refs_1_, s32[2,128]{1,0:T(2,128)S(1)} %get-tuple-element.31.refs_2_, s32[2,128]{1,0:T(2,128)S(1)} %get-tuple-element.32.refs_3_, ...), custom_call_target="tpu_custom_call" | custom-call | tf_op jit(solution)/shard_map/combine_body/pallas_call | solution.py:28
  103.3 2.4 %all-gather.2.cloned.1.call-done.refs_4_ = bf16[512,4096]{1,0:T(8,128)(2,1)} async-done(((bf16[128,4096]{1,0:T(8,128)(2,1)}), bf16[512,4096]{1,0:T(8,128)(2,1)}) %all-gather.2.cloned.1.call-update) | async-done | bytes 4194320 | tf_op jit(solution)/shard_map/all_gather | solution.py:275
  105.7 2.2 copy-done.17
  110.5 5.1 %all-to-all-start.3 = ((bf16[4,128,2048]{2,1,0:T(8,128)(2,1)}), bf16[4,128,2048]{2,1,0:T(8,128)(2,1)}, u32[]{:S(2)}, u32[]{:S(2)}) async-start(bf16[4,128,2048]{2,1,0:T(8,128)(2,1)} %bitcast.27), calls=%async_computation.4 | async-start | bytes 4194304 | tf_op jit(solution)/shard_map/all_to_all | solution.py:235
  115.6 2.6 %copy-done.18 = bf16[512,4096]{1,0:T(8,128)(2,1)S(1)} copy-done((bf16[512,4096]{1,0:T(8,128)(2,1)S(1)}, bf16[512,4096]{1,0:T(8,128)(2,1)}, u32[]{:S(2)}) %copy-start.18) | copy-done | bytes 4194328
  120.7 18.7 %all-to-all-done.3 = bf16[4,128,2048]{2,1,0:T(8,128)(2,1)} async-done(((bf16[4,128,2048]{2,1,0:T(8,128)(2,1)}), bf16[4,128,2048]{2,1,0:T(8,128)(2,1)}, u32[]{:S(2)}, u32[]{:S(2)}) %all-to-all-start.3) | async-done | bytes 2097184 | tf_op jit(solution)/shard_map/all_to_all | solution.py:235
  139.5 6.3 %all-to-all-start.4 = ((bf16[4,128,2048]{2,1,0:T(8,128)(2,1)}), bf16[4,128,2048]{2,1,0:T(8,128)(2,1)}, u32[]{:S(2)}, u32[]{:S(2)}) async-start(bf16[4,128,2048]{2,1,0:T(8,128)(2,1)} %bitcast.26), calls=%async_computation.5 | async-start | bytes 4194304 | tf_op jit(solution)/shard_map/all_to_all | solution.py:235
  146.5 3.3 %weight_grad_body.4 = bf16[256,2048]{1,0:T(8,128)(2,1)} custom-call(s32[3]{0:T(128)S(1)} %pad_add_fusion.place, bf16[512,512]{1,0:T(8,128)(2,1)S(1)} %arrange_body.1.hid_ref, bf16[512,2048]{1,0:T(8,128)(2,1)} %bitcast.11.grad_ref), custom_call_target="tpu_custom_call" | custom-call | tf_op jit(solution)/shard_map/weight_grad_body/pallas_call | solution.py:28
  149.8 2.3 %weight_grad_body.5.refs_0_ = bf16[256,2048]{1,0:T(8,128)(2,1)S(1)} custom-call(s32[3]{0:T(128)S(1)} %pad_add_fusion.place, bf16[512,512]{1,0:T(8,128)(2,1)S(1)} %arrange_body.1.hid_ref, bf16[512,2048]{1,0:T(8,128)(2,1)} %bitcast.11.grad_ref), custom_call_target="tpu_custom_call" | custom-call | tf_op jit(solution)/shard_map/weight_grad_body/pallas_call | solution.py:28
  154.1 3.1 %backward_first_body.1.first_ref = f32[512,512]{1,0:T(8,128)S(1)} custom-call(s32[3]{0:T(128)S(1)} %pad_add_fusion.place, bf16[512,2048]{1,0:T(8,128)(2,1)} %bitcast.11.grad_ref, bf16[256,4096]{1,0:T(8,128)(2,1)S(1)} %bitcast.23, bf16[256,2048]{1,0:T(8,128)(2,1)} %collective-permute-done.refs_1_), custom_call_target="tpu_custom_call" | custom-call | tf_op jit(solution)/shard_map/backward_first_body/pallas_call | solution.py:28
  158.2 11.5 %all-to-all-done.4 = bf16[4,128,2048]{2,1,0:T(8,128)(2,1)} async-done(((bf16[4,128,2048]{2,1,0:T(8,128)(2,1)}), bf16[4,128,2048]{2,1,0:T(8,128)(2,1)}, u32[]{:S(2)}, u32[]{:S(2)}) %all-to-all-start.4) | async-done | bytes 2097184 | tf_op jit(solution)/shard_map/all_to_all | solution.py:235
  169.7 3.4 %weight_grad_body.6 = bf16[256,2048]{1,0:T(8,128)(2,1)} custom-call(s32[3]{0:T(128)S(1)} %pad_add_fusion.place, bf16[512,512]{1,0:T(8,128)(2,1)S(1)} %arrange_body.1.hid_ref, bf16[512,2048]{1,0:T(8,128)(2,1)} %bitcast.13.grad_ref), custom_call_target="tpu_custom_call" | custom-call | tf_op jit(solution)/shard_map/weight_grad_body/pallas_call | solution.py:28
  174.0 3.9 %backward_last_body.1 = bf16[512,512]{1,0:T(8,128)(2,1)} custom-call(s32[3]{0:T(128)S(1)} %pad_add_fusion.place, f32[512,512]{1,0:T(8,128)S(1)} %copy-done.6, bf16[512,2048]{1,0:T(8,128)(2,1)} %bitcast.13.grad_ref, bf16[256,4096]{1,0:T(8,128)(2,1)S(1)} %bitcast.24, bf16[256,2048]{1,0:T(8,128)(2,1)} %collective-permute-done.1.refs_1_), custom_call_target="tpu_custom_call" | custom-call | tf_op jit(solution)/shard_map/backward_last_body/pallas_call | solution.py:28
  178.0 9.9 %all-to-all-start.5 = ((bf16[16,32,512]{2,1,0:T(8,128)(2,1)}), bf16[16,32,512]{2,1,0:T(8,128)(2,1)}, u32[]{:S(2)}, u32[]{:S(2)}) async-start(bf16[16,32,512]{2,1,0:T(8,128)(2,1)} %bitcast.14), calls=%async_computation.7 | async-start | bytes 1048576 | tf_op jit(solution)/shard_map/all_to_all | solution.py:235
  187.9 2.3 %weight_grad_body.7.refs_1_ = bf16[256,2048]{1,0:T(8,128)(2,1)S(1)} custom-call(s32[3]{0:T(128)S(1)} %pad_add_fusion.place, bf16[512,512]{1,0:T(8,128)(2,1)S(1)} %arrange_body.1.hid_ref, bf16[512,2048]{1,0:T(8,128)(2,1)} %bitcast.13.grad_ref), custom_call_target="tpu_custom_call" | custom-call | flops 274877906944 | tf_op jit(solution)/shard_map/weight_grad_body/pallas_call | solution.py:28
  191.3 15.1 %reduce-scatter.5.cloned.1.call-done = bf16[128,2048]{1,0:T(8,128)(2,1)} async-done(((bf16[512,2048]{1,0:T(8,128)(2,1)}), bf16[128,2048]{1,0:T(8,128)(2,1)}) %reduce-scatter.5.cloned.1.call-update) | async-done | bytes 524304 | tf_op jit(solution)/shard_map/reduce_scatter | solution.py:295
  210.2 3.5 %average_body.1 = bf16[256,4096]{1,0:T(8,128)(2,1)} custom-call(s32[3]{0:T(128)S(1)} %pad_add_fusion.place, bf16[256,2048]{1,0:T(8,128)(2,1)S(1)} %copy-done.4, bf16[256,2048]{1,0:T(8,128)(2,1)S(1)} %copy-done.12, bf16[256,2048]{1,0:T(8,128)(2,1)} %collective-permute-done.5.refs_2_, bf16[256,2048]{1,0:T(8,128)(2,1)} %collective-permute-done.6.refs_3_), custom_call_target="tpu_custom_call" | custom-call | tf_op jit(solution)/shard_map/average_body/pallas_call | solution.py:28
  (73 shorter events, 28.0 us)
Async XLA Ops:
  7.2 3.7 %copy-start.20 = (s32[128,2]{0,1:T(2,128)S(1)}, s32[128,2]{0,1:T(2,128)}, u32[]{:S(2)}) copy-start(s32[128,2]{0,1:T(2,128)} %param.7) | copy-start | bytes 3076
  7.2 3.8 %copy-start.21 = (s32[128,2]{0,1:T(2,128)S(1)}, s32[128,2]{0,1:T(2,128)}, u32[]{:S(2)}) copy-start(s32[128,2]{0,1:T(2,128)} %param.8) | copy-start | bytes 3076
  7.2 4.0 %copy-start.19 = (bf16[128,2,512]{2,1,0:T(2,128)(2,1)S(1)}, bf16[128,2,512]{2,1,0:T(2,128)(2,1)}, u32[]{:S(2)}) copy-start(bf16[128,2,512]{2,1,0:T(2,128)(2,1)} %param.5) | copy-start | bytes 786436
  7.2 13.1 %copy-start = (bf16[1,256,4096]{2,1,0:T(8,128)(2,1)S(1)}, bf16[1,256,4096]{2,1,0:T(8,128)(2,1)}, u32[]{:S(2)}) copy-start(bf16[1,256,4096]{2,1,0:T(8,128)(2,1)} %param.9) | copy-start | bytes 6291460
  9.7 25.2 %collective-permute-start = (bf16[256,2048]{1,0:T(8,128)(2,1)}, bf16[256,2048]{1,0:T(8,128)(2,1)}, u32[]{:S(2)}, u32[]{:S(2)}) collective-permute-start(bf16[256,2048]{1,0:T(8,128)(2,1)} %slice.8), channel_id=1, source_target_pairs={{0,16},{16,0},{1,17},{17,1},{2,18},{18,2},{3,19},{19,3},{4,20},{20... | collective-permute-start | bytes 3145736 | tf_op jit(solution)/shard_map/ppermute | solution.py:260
  11.0 2.4 %copy-start.15 = (s32[128,2]{1,0:T(8,128)}, s32[128,2]{1,0:T(8,128)S(1)}, u32[]{:S(2)}) copy-start(s32[128,2]{1,0:T(8,128)S(1)} %copy.8.ids_ref.refs_0_) | copy-start | bytes 3076
  11.1 2.3 %copy-start.13 = (s32[128,2]{1,0:T(8,128)}, s32[128,2]{1,0:T(8,128)S(1)}, u32[]{:S(2)}) copy-start(s32[128,2]{1,0:T(8,128)S(1)} %copy.9.num_ref) | copy-start | bytes 3076
  13.4 20.8 %all-to-all-start = ((bf16[16,32,512]{2,1,0:T(8,128)(2,1)}), bf16[16,32,512]{2,1,0:T(8,128)(2,1)S(1)}, u32[]{:S(2)}, u32[]{:S(2)}) async-start(bf16[16,32,512]{2,1,0:T(8,128)(2,1)} %bitcast.3), calls=%async_computation | async-start | bytes 1048576 | tf_op jit(solution)/shard_map/all_to_all | solution.py:235
  20.3 85.4 %all-gather.2.cloned.1.call-start = ((), (), s32[]{:S(2)}) async-start(), calls=%async_computation.9 | async-start | bytes 5242880 | tf_op jit(solution)/shard_map/all_gather | solution.py:275
  21.4 35.1 %collective-permute-start.1 = (bf16[256,2048]{1,0:T(8,128)(2,1)}, bf16[256,2048]{1,0:T(8,128)(2,1)}, u32[]{:S(2)}, u32[]{:S(2)}) collective-permute-start(bf16[256,2048]{1,0:T(8,128)(2,1)} %slice.7), channel_id=1, source_target_pairs={{0,16},{16,0},{1,17},{17,1},{2,18},{18,2},{3,19},{19,3},{4,20},{20... | collective-permute-start | bytes 3145736 | tf_op jit(solution)/shard_map/ppermute | solution.py:260
  38.7 30.5 %all-to-all-start.1 = ((bf16[4,128,2048]{2,1,0:T(8,128)(2,1)}), bf16[4,128,2048]{2,1,0:T(8,128)(2,1)}, u32[]{:S(2)}, u32[]{:S(2)}) async-start(bf16[4,128,2048]{2,1,0:T(8,128)(2,1)} %bitcast.28), calls=%async_computation.1 | async-start | bytes 4194304 | tf_op jit(solution)/shard_map/all_to_all | solution.py:235
  59.0 1.3 copy-start.7
  69.2 6.5 %copy-start.16 = (s32[128,2]{1,0:T(8,128)S(1)}, s32[128,2]{1,0:T(8,128)}, u32[]{:S(2)}) copy-start(s32[128,2]{1,0:T(8,128)} %copy-done.15) | copy-start | bytes 3076
  69.2 30.3 %all-to-all-start.2 = ((bf16[4,128,2048]{2,1,0:T(8,128)(2,1)}), bf16[4,128,2048]{2,1,0:T(8,128)(2,1)}, u32[]{:S(2)}, u32[]{:S(2)}) async-start(bf16[4,128,2048]{2,1,0:T(8,128)(2,1)} %bitcast.25), calls=%async_computation.2 | async-start | bytes 4194304 | tf_op jit(solution)/shard_map/all_to_all | solution.py:235
  75.7 115.6 %reduce-scatter.3.cloned.1.call-start = ((), (), s32[]{:S(2)}) async-start(), calls=%async_computation.8 | async-start | bytes 2621440 | tf_op jit(solution)/shard_map/reduce_scatter | solution.py:295
  75.7 7.0 %collective-permute-start.2 = (s32[128,2]{1,0:T(8,128)S(1)}, s32[128,2]{1,0:T(8,128)S(1)}, u32[]{:S(2)}, u32[]{:S(2)}) collective-permute-start(s32[128,2]{1,0:T(8,128)S(1)} %copy-done.16), channel_id=1, source_target_pairs={{0,4},{4,0},{8,12},{12,8},{1,5},{5,1},{9,13},{13,9},{2,6},{6,2},{1... | collective-permute-start | bytes 3080 | tf_op jit(solution)/shard_map/ppermute | solution.py:281
  75.7 10.2 %collective-permute-start.3 = (s32[128,2]{1,0:T(8,128)S(1)}, s32[128,2]{1,0:T(8,128)S(1)}, u32[]{:S(2)}, u32[]{:S(2)}) collective-permute-start(s32[128,2]{1,0:T(8,128)S(1)} %copy-done.16), channel_id=1, source_target_pairs={{0,8},{4,12},{8,0},{12,4},{1,9},{5,13},{9,1},{13,5},{2,10},{6,14},... | collective-permute-start | bytes 3080 | tf_op jit(solution)/shard_map/ppermute | solution.py:281
  79.2 14.3 %collective-permute-start.4 = (s32[128,2]{1,0:T(8,128)S(1)}, s32[128,2]{1,0:T(8,128)S(1)}, u32[]{:S(2)}, u32[]{:S(2)}) collective-permute-start(s32[128,2]{1,0:T(8,128)S(1)} %copy-done.16), channel_id=1, source_target_pairs={{0,12},{4,8},{8,4},{12,0},{1,13},{5,9},{9,5},{13,1},{2,14},{6,10},... | collective-permute-start | bytes 3080 | tf_op jit(solution)/shard_map/ppermute | solution.py:281
  101.9 1.4 copy-start.2
  105.7 2.2 copy-start.17
  110.5 29.0 %all-to-all-start.3 = ((bf16[4,128,2048]{2,1,0:T(8,128)(2,1)}), bf16[4,128,2048]{2,1,0:T(8,128)(2,1)}, u32[]{:S(2)}, u32[]{:S(2)}) async-start(bf16[4,128,2048]{2,1,0:T(8,128)(2,1)} %bitcast.27), calls=%async_computation.4 | async-start | bytes 4194304 | tf_op jit(solution)/shard_map/all_to_all | solution.py:235
  115.6 2.6 %copy-start.18 = (bf16[512,4096]{1,0:T(8,128)(2,1)S(1)}, bf16[512,4096]{1,0:T(8,128)(2,1)}, u32[]{:S(2)}) copy-start(bf16[512,4096]{1,0:T(8,128)(2,1)} %all-gather.2.cloned.1.call-done.refs_4_) | copy-start | bytes 12582916
  119.4 1.3 copy-start.8
  139.5 30.2 %all-to-all-start.4 = ((bf16[4,128,2048]{2,1,0:T(8,128)(2,1)}), bf16[4,128,2048]{2,1,0:T(8,128)(2,1)}, u32[]{:S(2)}, u32[]{:S(2)}) async-start(bf16[4,128,2048]{2,1,0:T(8,128)(2,1)} %bitcast.26), calls=%async_computation.5 | async-start | bytes 4194304 | tf_op jit(solution)/shard_map/all_to_all | solution.py:235
  145.8 60.6 %reduce-scatter.5.cloned.1.call-start = ((), (), s32[]{:S(2)}) async-start(), calls=%async_computation.10 | async-start | bytes 2621440 | tf_op jit(solution)/shard_map/reduce_scatter | solution.py:295
  153.1 57.0 %collective-permute-start.5 = (bf16[256,2048]{1,0:T(8,128)(2,1)}, bf16[256,2048]{1,0:T(8,128)(2,1)}, u32[]{:S(2)}, u32[]{:S(2)}) collective-permute-start(bf16[256,2048]{1,0:T(8,128)(2,1)} %weight_grad_body.4), channel_id=1, source_target_pairs={{0,16},{16,0},{1,17},{17,1},{2,18},{18,2},{3,19},{19,3},{4,20},{20... | collective-permute-start | bytes 3145736 | tf_op jit(solution)/shard_map/ppermute | solution.py:260
  169.7 4.3 %copy-start.6 = (f32[512,512]{1,0:T(8,128)S(1)}, f32[512,512]{1,0:T(8,128)}, u32[]{:S(2)}) copy-start(f32[512,512]{1,0:T(8,128)} %copy-done.5) | copy-start | bytes 3145732
  173.1 37.0 %collective-permute-start.6 = (bf16[256,2048]{1,0:T(8,128)(2,1)}, bf16[256,2048]{1,0:T(8,128)(2,1)}, u32[]{:S(2)}, u32[]{:S(2)}) collective-permute-start(bf16[256,2048]{1,0:T(8,128)(2,1)} %weight_grad_body.6), channel_id=1, source_target_pairs={{0,16},{16,0},{1,17},{17,1},{2,18},{18,2},{3,19},{19,3},{4,20},{20... | collective-permute-start | bytes 3145736 | tf_op jit(solution)/shard_map/ppermute | solution.py:260
  178.0 35.7 %all-to-all-start.5 = ((bf16[16,32,512]{2,1,0:T(8,128)(2,1)}), bf16[16,32,512]{2,1,0:T(8,128)(2,1)}, u32[]{:S(2)}, u32[]{:S(2)}) async-start(bf16[16,32,512]{2,1,0:T(8,128)(2,1)} %bitcast.14), calls=%async_computation.7 | async-start | bytes 1048576 | tf_op jit(solution)/shard_map/all_to_all | solution.py:235
  191.3 18.9 %copy-start.4 = (bf16[256,2048]{1,0:T(8,128)(2,1)S(1)}, bf16[256,2048]{1,0:T(8,128)(2,1)}, u32[]{:S(2)}) copy-start(bf16[256,2048]{1,0:T(8,128)(2,1)} %copy-done.3) | copy-start | bytes 3145732
  191.3 18.9 %copy-start.12 = (bf16[256,2048]{1,0:T(8,128)(2,1)S(1)}, bf16[256,2048]{1,0:T(8,128)(2,1)}, u32[]{:S(2)}) copy-start(bf16[256,2048]{1,0:T(8,128)(2,1)} %copy-done.11) | copy-start | bytes 3145732
  210.1 3.5 %copy-start.14 = (s32[128,2]{1,0:T(8,128)S(1)}, s32[128,2]{1,0:T(8,128)}, u32[]{:S(2)}) copy-start(s32[128,2]{1,0:T(8,128)} %copy-done.13) | copy-start | bytes 3076
  (6 other events, 6.9 us)
Sparse Core Ops, SparseCore 0:
  22.7 82.9 all-gather.1
  108.6 43.1 reduce-scatter.2
  154.2 52.1 reduce-scatter.4

commit v4 on v3

--- a/solution.py
+++ b/solution.py
@@ -297,9 +297,10 @@
     def pick(rows, c):
         return call(part(pick_body, peers, capacity, c * piece), chunk, place, *rows, grads, cost=COST)
 
-    def weight_grad(x, lo, hi, cost=0):
+    def weight_grad(x, lo, hi, cost=0, wait=()):
         return call(
-            part(weight_grad_body, lo, hi), shaped((hi - lo, piece)), place, hid, x, cost=cost
+            part(weight_grad_body, lo, hi), shaped((hi - lo, piece)),
+            after(place, *wait), hid, x, cost=cost,
         )
 
     out_a, out_b = forward(0), forward(1)
@@ -320,7 +321,7 @@
     sent_b = exchange(after(pick_b, sent_a), "p")
     lo, hi = (share, units) if pair else (0, units)
     other_a = weight_grad(sent_a, lo, hi)
-    own_a = weight_grad(sent_a, 0, share) if pair else jnp.zeros((share, piece), BF16)
+    own_a = weight_grad(sent_a, 0, share, wait=(other_a,)) if pair else jnp.zeros((share, piece), BF16)
     first = call(
         part(backward_first_body, 0), shaped((total_rows, units), F32), place, sent_a, mine, *theirs[:1]
     )
@@ -343,13 +344,13 @@
             lax.psum_scatter(g, "dp", scatter_dimension=0, tiled=True) for g in other_grads
         ]
 
-    layer_out = jnp.concatenate([after(x, own_b) for x in back], 1)
     down_grad = call(
-        part(average_body, replicas), shaped((share, width)), after(place, layer_out), *own_grads, *other_grads
+        part(average_body, replicas), shaped((share, width)), after(place, own_b, layer_a), *own_grads, *other_grads
     )
     hidden_grad = call(
         part(hidden_grad_body, top, pair), shaped((tokens, top * units)), after(place, down_grad), col_own, gate_num, back_rows
     )
+    layer_out = jnp.concatenate([layer_a, after(layer_b, down_grad)], 1)
     return (layer_out, hidden_grad.reshape(tokens, top, units), down_grad[None])
 
 

time: 226 us -> 223 us (0.987)
  waiting for transfers between devices: 96.2 us -> 92.2 us
    reduce_scatter x2, waiting for transfers between devices: 15.1 us -> 0.01 us  [reduce(): return lax.psum_scatter(x, 'z', scatter_dimension=0, tiled=True)]
    ppermute x4, waiting for transfers between devices: 11.2 us -> 17.3 us  [to_replica(): return lax.ppermute(x, 'dp', [(0, 1), (1, 0)])]
    all_to_all x6, waiting for transfers between devices: 52.5 us -> 57.6 us  [exchange(): return lax.all_to_all(x, axes, split_axis=0, concat_axis=0, tiled=True)]
    unnamed x48 -> x49, local copies, waits for them, and re-layouts: 17.8 us -> 18.5 us
  transfers between devices with their start and end apart: 16 -> 16, of which waited for: 11 -> 12; matrix products, arithmetic and copies ran while one was open for 2% -> 1% of each run, Pallas kernels for 17% -> 18%
where the time goes in v4:
time: 223 us; the launch traced here: 220 us
  waiting for transfers between devices  92.2 us (41%)
  starting transfers between devices  48.2 us (22%)
  Pallas kernels  40.1 us (18%)
  local copies, waits for them, and re-layouts  22.9 us (10%)
  between operations  14 us (6%)
    all_to_all x6, waiting for transfers between devices, exchange(): return lax.all_to_all(x, axes, split_axis=0, concat_axis=0, tiled=True)  57.6 us
    all_to_all x6, starting transfers between devices, exchange(): return lax.all_to_all(x, axes, split_axis=0, concat_axis=0, tiled=True)  41.3 us
    pallas_call x17, Pallas kernels, call(): pl.pallas_call(body, out_shape=outs, in_specs=[SMEM] + [VMEM] * (len(args...  40.1 us
    unnamed x49, local copies, waits for them, and re-layouts  18.5 us
    ppermute x4, waiting for transfers between devices, to_replica(): return lax.ppermute(x, 'dp', [(0, 1), (1, 0)])  17.3 us
    ppermute x3, waiting for transfers between devices, on_device(): lax.ppermute(expert_ids, 'z', [(i, i ^ j) for i in range(PLANES)])  14.3 us
  transfers between devices with their start and end apart: 16, of which 12 were waited for; matrix products, arithmetic and copies ran while one was open for 1% of the time, Pallas kernels for 18%

profile of v4, /device:TPU:11, one launch (start us, length us, event | category | flops | bytes accessed | tf_op | source)
XLA Modules:
  0.0 219.6 jit_solution(12622346429386907826)
XLA Ops:
  7.2 2.5 %slice.8 = bf16[256,2048]{1,0:T(8,128)(2,1)} slice(bf16[256,4096]{1,0:T(8,128)(2,1)} %bitcast.19), slice={[0:256], [0:2048]} | slice | bytes 2097152 | tf_op jit(solution)/shard_map/slice | solution.py:240
  13.4 6.8 %all-to-all-start = ((bf16[16,32,512]{2,1,0:T(8,128)(2,1)}), bf16[16,32,512]{2,1,0:T(8,128)(2,1)S(1)}, u32[]{:S(2)}, u32[]{:S(2)}) async-start(bf16[16,32,512]{2,1,0:T(8,128)(2,1)} %bitcast.3), calls=%async_computation | async-start | bytes 1048576 | tf_op jit(solution)/shard_map/all_to_all | solution.py:235
  21.7 12.6 %all-to-all-done = bf16[16,32,512]{2,1,0:T(8,128)(2,1)S(1)} async-done(((bf16[16,32,512]{2,1,0:T(8,128)(2,1)}), bf16[16,32,512]{2,1,0:T(8,128)(2,1)S(1)}, u32[]{:S(2)}, u32[]{:S(2)}) %all-to-all-start) | async-done | bytes 524320 | tf_op jit(solution)/shard_map/all_to_all | solution.py:235
  34.9 2.5 %forward_body.2 = bf16[512,2048]{1,0:T(8,128)(2,1)S(1)} custom-call(s32[3]{0:T(128)S(1)} %pad_add_fusion.place, bf16[512,512]{1,0:T(8,128)(2,1)S(1)} %arrange_body.1.hid_ref, bf16[256,4096]{1,0:T(8,128)(2,1)S(1)} %bitcast.21, bf16[256,2048]{1,0:T(8,128)(2,1)} %collective-permute-done.refs_1_), custom_call_target="tpu_custom_call" | custom-call | flops 274877906944 | tf_op jit(solution)/shard_map/forward_body/pallas_call | solution.py:28
  38.8 6.6 %all-to-all-start.1 = ((bf16[4,128,2048]{2,1,0:T(8,128)(2,1)}), bf16[4,128,2048]{2,1,0:T(8,128)(2,1)}, u32[]{:S(2)}, u32[]{:S(2)}) async-start(bf16[4,128,2048]{2,1,0:T(8,128)(2,1)} %bitcast.28), calls=%async_computation.1 | async-start | bytes 4194304 | tf_op jit(solution)/shard_map/all_to_all | solution.py:235
  45.4 11.1 %collective-permute-done.1.refs_1_ = bf16[256,2048]{1,0:T(8,128)(2,1)} collective-permute-done((bf16[256,2048]{1,0:T(8,128)(2,1)}, bf16[256,2048]{1,0:T(8,128)(2,1)}, u32[]{:S(2)}, u32[]{:S(2)}) %collective-permute-start.1) | collective-permute-done | bytes 1048608 | tf_op jit(solution)/shard_map/ppermute | solution.py:260
  56.5 2.5 %forward_body.3 = bf16[512,2048]{1,0:T(8,128)(2,1)S(1)} custom-call(s32[3]{0:T(128)S(1)} %pad_add_fusion.place, bf16[512,512]{1,0:T(8,128)(2,1)S(1)} %arrange_body.1.hid_ref, bf16[256,4096]{1,0:T(8,128)(2,1)S(1)} %bitcast.22, bf16[256,2048]{1,0:T(8,128)(2,1)} %collective-permute-done.1.refs_1_), custom_call_target="tpu_custom_call" | custom-call | flops 274877906944 | tf_op jit(solution)/shard_map/forward_body/pallas_call | solution.py:28
  60.3 9.0 %all-to-all-done.1 = bf16[4,128,2048]{2,1,0:T(8,128)(2,1)} async-done(((bf16[4,128,2048]{2,1,0:T(8,128)(2,1)}), bf16[4,128,2048]{2,1,0:T(8,128)(2,1)}, u32[]{:S(2)}, u32[]{:S(2)}) %all-to-all-start.1) | async-done | bytes 2097184 | tf_op jit(solution)/shard_map/all_to_all | solution.py:235
  69.3 6.5 %all-to-all-start.2 = ((bf16[4,128,2048]{2,1,0:T(8,128)(2,1)}), bf16[4,128,2048]{2,1,0:T(8,128)(2,1)}, u32[]{:S(2)}, u32[]{:S(2)}) async-start(bf16[4,128,2048]{2,1,0:T(8,128)(2,1)} %bitcast.25), calls=%async_computation.2 | async-start | bytes 4194304 | tf_op jit(solution)/shard_map/all_to_all | solution.py:235
  75.8 3.5 %collective-permute-start.3 = (s32[128,2]{1,0:T(8,128)S(1)}, s32[128,2]{1,0:T(8,128)S(1)}, u32[]{:S(2)}, u32[]{:S(2)}) collective-permute-start(s32[128,2]{1,0:T(8,128)S(1)} %copy-done.16), channel_id=1, source_target_pairs={{0,8},{4,12},{8,0},{12,4},{1,9},{5,13},{9,1},{13,5},{2,10},{6,14},... | collective-permute-start | bytes 3080 | tf_op jit(solution)/shard_map/ppermute | solution.py:281
  79.3 3.4 %collective-permute-done.2.refs_1_ = s32[128,2]{1,0:T(8,128)S(1)} collective-permute-done((s32[128,2]{1,0:T(8,128)S(1)}, s32[128,2]{1,0:T(8,128)S(1)}, u32[]{:S(2)}, u32[]{:S(2)}) %collective-permute-start.2) | collective-permute-done | bytes 1056 | tf_op jit(solution)/shard_map/ppermute | solution.py:281
  82.7 3.1 %collective-permute-done.3.refs_2_ = s32[128,2]{1,0:T(8,128)S(1)} collective-permute-done((s32[128,2]{1,0:T(8,128)S(1)}, s32[128,2]{1,0:T(8,128)S(1)}, u32[]{:S(2)}, u32[]{:S(2)}) %collective-permute-start.3) | collective-permute-done | bytes 1056 | tf_op jit(solution)/shard_map/ppermute | solution.py:281
  85.9 7.7 %collective-permute-done.4.refs_3_ = s32[128,2]{1,0:T(8,128)S(1)} collective-permute-done((s32[128,2]{1,0:T(8,128)S(1)}, s32[128,2]{1,0:T(8,128)S(1)}, u32[]{:S(2)}, u32[]{:S(2)}) %collective-permute-start.4) | collective-permute-done | bytes 1056 | tf_op jit(solution)/shard_map/ppermute | solution.py:281
  95.2 2.4 %combine_body.2 = bf16[512,2048]{1,0:T(8,128)(2,1)S(1)} custom-call(s32[3]{0:T(128)S(1)} %pad_add_fusion.place, s32[2,128]{1,0:T(2,128)S(1)} %get-tuple-element.29.refs_0_, s32[2,128]{1,0:T(2,128)S(1)} %get-tuple-element.30.refs_1_, s32[2,128]{1,0:T(2,128)S(1)} %get-tuple-element.31.refs_2_, s32[2,128]{1,0:T(2,128)S(1)} %get-tuple-element.32.refs_3_, ...), custom_call_target="tpu_custom_call" | custom-call | tf_op jit(solution)/shard_map/combine_body/pallas_call | solution.py:28
  99.7 2.4 %combine_body.3 = bf16[512,2048]{1,0:T(8,128)(2,1)S(1)} custom-call(s32[3]{0:T(128)S(1)} %pad_add_fusion.place, s32[2,128]{1,0:T(2,128)S(1)} %get-tuple-element.29.refs_0_, s32[2,128]{1,0:T(2,128)S(1)} %get-tuple-element.30.refs_1_, s32[2,128]{1,0:T(2,128)S(1)} %get-tuple-element.31.refs_2_, s32[2,128]{1,0:T(2,128)S(1)} %get-tuple-element.32.refs_3_, ...), custom_call_target="tpu_custom_call" | custom-call | tf_op jit(solution)/shard_map/combine_body/pallas_call | solution.py:28
  103.4 2.3 %all-gather.2.cloned.1.call-done.refs_4_ = bf16[512,4096]{1,0:T(8,128)(2,1)} async-done(((bf16[128,4096]{1,0:T(8,128)(2,1)}), bf16[512,4096]{1,0:T(8,128)(2,1)}) %all-gather.2.cloned.1.call-update) | async-done | bytes 4194320 | tf_op jit(solution)/shard_map/all_gather | solution.py:275
  105.7 2.2 copy-done.17
  110.5 5.1 %all-to-all-start.3 = ((bf16[4,128,2048]{2,1,0:T(8,128)(2,1)}), bf16[4,128,2048]{2,1,0:T(8,128)(2,1)}, u32[]{:S(2)}, u32[]{:S(2)}) async-start(bf16[4,128,2048]{2,1,0:T(8,128)(2,1)} %bitcast.27), calls=%async_computation.5 | async-start | bytes 4194304 | tf_op jit(solution)/shard_map/all_to_all | solution.py:235
  115.6 2.5 %copy-done.18 = bf16[512,4096]{1,0:T(8,128)(2,1)S(1)} copy-done((bf16[512,4096]{1,0:T(8,128)(2,1)S(1)}, bf16[512,4096]{1,0:T(8,128)(2,1)}, u32[]{:S(2)}) %copy-start.18) | copy-done | bytes 4194328
  120.7 18.8 %all-to-all-done.3 = bf16[4,128,2048]{2,1,0:T(8,128)(2,1)} async-done(((bf16[4,128,2048]{2,1,0:T(8,128)(2,1)}), bf16[4,128,2048]{2,1,0:T(8,128)(2,1)}, u32[]{:S(2)}, u32[]{:S(2)}) %all-to-all-start.3) | async-done | bytes 2097184 | tf_op jit(solution)/shard_map/all_to_all | solution.py:235
  139.5 6.3 %all-to-all-start.4 = ((bf16[4,128,2048]{2,1,0:T(8,128)(2,1)}), bf16[4,128,2048]{2,1,0:T(8,128)(2,1)}, u32[]{:S(2)}, u32[]{:S(2)}) async-start(bf16[4,128,2048]{2,1,0:T(8,128)(2,1)} %bitcast.26), calls=%async_computation.6 | async-start | bytes 4194304 | tf_op jit(solution)/shard_map/all_to_all | solution.py:235
  146.5 3.3 %weight_grad_body.4 = bf16[256,2048]{1,0:T(8,128)(2,1)} custom-call(s32[3]{0:T(128)S(1)} %pad_add_fusion.place, bf16[512,512]{1,0:T(8,128)(2,1)S(1)} %arrange_body.1.hid_ref, bf16[512,2048]{1,0:T(8,128)(2,1)} %bitcast.11.grad_ref), custom_call_target="tpu_custom_call" | custom-call | tf_op jit(solution)/shard_map/weight_grad_body/pallas_call | solution.py:28
  150.8 2.3 %weight_grad_body.5.refs_0_ = bf16[256,2048]{1,0:T(8,128)(2,1)S(1)} custom-call(s32[3]{0:T(128)S(1)} %pad_add_fusion.place, bf16[512,512]{1,0:T(8,128)(2,1)S(1)} %arrange_body.1.hid_ref, bf16[512,2048]{1,0:T(8,128)(2,1)} %bitcast.11.grad_ref), custom_call_target="tpu_custom_call" | custom-call | tf_op jit(solution)/shard_map/weight_grad_body/pallas_call | solution.py:28
  154.1 3.1 %backward_first_body.1.first_ref = f32[512,512]{1,0:T(8,128)S(1)} custom-call(s32[3]{0:T(128)S(1)} %pad_add_fusion.place, bf16[512,2048]{1,0:T(8,128)(2,1)} %bitcast.11.grad_ref, bf16[256,4096]{1,0:T(8,128)(2,1)S(1)} %bitcast.23, bf16[256,2048]{1,0:T(8,128)(2,1)} %collective-permute-done.refs_1_), custom_call_target="tpu_custom_call" | custom-call | tf_op jit(solution)/shard_map/backward_first_body/pallas_call | solution.py:28
  158.2 11.5 %all-to-all-done.4 = bf16[4,128,2048]{2,1,0:T(8,128)(2,1)} async-done(((bf16[4,128,2048]{2,1,0:T(8,128)(2,1)}), bf16[4,128,2048]{2,1,0:T(8,128)(2,1)}, u32[]{:S(2)}, u32[]{:S(2)}) %all-to-all-start.4) | async-done | bytes 2097184 | tf_op jit(solution)/shard_map/all_to_all | solution.py:235
  169.7 3.4 %weight_grad_body.6 = bf16[256,2048]{1,0:T(8,128)(2,1)} custom-call(s32[3]{0:T(128)S(1)} %pad_add_fusion.place, bf16[512,512]{1,0:T(8,128)(2,1)S(1)} %arrange_body.1.hid_ref, bf16[512,2048]{1,0:T(8,128)(2,1)} %bitcast.13.grad_ref), custom_call_target="tpu_custom_call" | custom-call | tf_op jit(solution)/shard_map/weight_grad_body/pallas_call | solution.py:28
  174.1 4.0 %backward_last_body.1 = bf16[512,512]{1,0:T(8,128)(2,1)} custom-call(s32[3]{0:T(128)S(1)} %pad_add_fusion.place, f32[512,512]{1,0:T(8,128)S(1)} %copy-done.6, bf16[512,2048]{1,0:T(8,128)(2,1)} %bitcast.13.grad_ref, bf16[256,4096]{1,0:T(8,128)(2,1)S(1)} %bitcast.24, bf16[256,2048]{1,0:T(8,128)(2,1)} %collective-permute-done.1.refs_1_), custom_call_target="tpu_custom_call" | custom-call | tf_op jit(solution)/shard_map/backward_last_body/pallas_call | solution.py:28
  178.0 9.9 %all-to-all-start.5 = ((bf16[16,32,512]{2,1,0:T(8,128)(2,1)}), bf16[16,32,512]{2,1,0:T(8,128)(2,1)}, u32[]{:S(2)}, u32[]{:S(2)}) async-start(bf16[16,32,512]{2,1,0:T(8,128)(2,1)} %bitcast.14), calls=%async_computation.7 | async-start | bytes 1048576 | tf_op jit(solution)/shard_map/all_to_all | solution.py:235
  188.0 2.4 %weight_grad_body.7.refs_1_ = bf16[256,2048]{1,0:T(8,128)(2,1)S(1)} custom-call(s32[3]{0:T(128)S(1)} %pad_add_fusion.place, bf16[512,512]{1,0:T(8,128)(2,1)S(1)} %arrange_body.1.hid_ref, bf16[512,2048]{1,0:T(8,128)(2,1)} %bitcast.13.grad_ref), custom_call_target="tpu_custom_call" | custom-call | flops 274877906944 | tf_op jit(solution)/shard_map/weight_grad_body/pallas_call | solution.py:28
  191.3 6.2 %collective-permute-done.6.refs_3_ = bf16[256,2048]{1,0:T(8,128)(2,1)} collective-permute-done((bf16[256,2048]{1,0:T(8,128)(2,1)}, bf16[256,2048]{1,0:T(8,128)(2,1)}, u32[]{:S(2)}, u32[]{:S(2)}) %collective-permute-start.6) | collective-permute-done | bytes 1048608 | tf_op jit(solution)/shard_map/ppermute | solution.py:260
  200.0 3.5 %average_body.1 = bf16[256,4096]{1,0:T(8,128)(2,1)} custom-call(s32[3]{0:T(128)S(1)} %pad_add_fusion.place, bf16[256,2048]{1,0:T(8,128)(2,1)S(1)} %copy-done.4, bf16[256,2048]{1,0:T(8,128)(2,1)S(1)} %copy-done.12, bf16[256,2048]{1,0:T(8,128)(2,1)} %collective-permute-done.5.refs_2_, bf16[256,2048]{1,0:T(8,128)(2,1)} %collective-permute-done.6.refs_3_), custom_call_target="tpu_custom_call" | custom-call | tf_op jit(solution)/shard_map/average_body/pallas_call | solution.py:28
  203.5 5.1 %all-to-all-done.5 = bf16[16,32,512]{2,1,0:T(8,128)(2,1)} async-done(((bf16[16,32,512]{2,1,0:T(8,128)(2,1)}), bf16[16,32,512]{2,1,0:T(8,128)(2,1)}, u32[]{:S(2)}, u32[]{:S(2)}) %all-to-all-start.5) | async-done | bytes 524320 | tf_op jit(solution)/shard_map/all_to_all | solution.py:235
  (74 shorter events, 31.0 us)
Async XLA Ops:
  7.2 3.7 %copy-start.21 = (s32[128,2]{0,1:T(2,128)S(1)}, s32[128,2]{0,1:T(2,128)}, u32[]{:S(2)}) copy-start(s32[128,2]{0,1:T(2,128)} %param.7) | copy-start | bytes 3076
  7.2 3.8 %copy-start.22 = (s32[128,2]{0,1:T(2,128)S(1)}, s32[128,2]{0,1:T(2,128)}, u32[]{:S(2)}) copy-start(s32[128,2]{0,1:T(2,128)} %param.8) | copy-start | bytes 3076
  7.2 4.0 %copy-start.20 = (bf16[128,2,512]{2,1,0:T(2,128)(2,1)S(1)}, bf16[128,2,512]{2,1,0:T(2,128)(2,1)}, u32[]{:S(2)}) copy-start(bf16[128,2,512]{2,1,0:T(2,128)(2,1)} %param.5) | copy-start | bytes 786436
  7.2 13.1 %copy-start = (bf16[1,256,4096]{2,1,0:T(8,128)(2,1)S(1)}, bf16[1,256,4096]{2,1,0:T(8,128)(2,1)}, u32[]{:S(2)}) copy-start(bf16[1,256,4096]{2,1,0:T(8,128)(2,1)} %param.9) | copy-start | bytes 6291460
  9.7 25.2 %collective-permute-start = (bf16[256,2048]{1,0:T(8,128)(2,1)}, bf16[256,2048]{1,0:T(8,128)(2,1)}, u32[]{:S(2)}, u32[]{:S(2)}) collective-permute-start(bf16[256,2048]{1,0:T(8,128)(2,1)} %slice.8), channel_id=1, source_target_pairs={{0,16},{16,0},{1,17},{17,1},{2,18},{18,2},{3,19},{19,3},{4,20},{20... | collective-permute-start | bytes 3145736 | tf_op jit(solution)/shard_map/ppermute | solution.py:260
  11.0 2.4 %copy-start.15 = (s32[128,2]{1,0:T(8,128)}, s32[128,2]{1,0:T(8,128)S(1)}, u32[]{:S(2)}) copy-start(s32[128,2]{1,0:T(8,128)S(1)} %copy.8.ids_ref.refs_0_) | copy-start | bytes 3076
  11.1 2.3 %copy-start.13 = (s32[128,2]{1,0:T(8,128)}, s32[128,2]{1,0:T(8,128)S(1)}, u32[]{:S(2)}) copy-start(s32[128,2]{1,0:T(8,128)S(1)} %copy.9.num_ref) | copy-start | bytes 3076
  13.4 20.8 %all-to-all-start = ((bf16[16,32,512]{2,1,0:T(8,128)(2,1)}), bf16[16,32,512]{2,1,0:T(8,128)(2,1)S(1)}, u32[]{:S(2)}, u32[]{:S(2)}) async-start(bf16[16,32,512]{2,1,0:T(8,128)(2,1)} %bitcast.3), calls=%async_computation | async-start | bytes 1048576 | tf_op jit(solution)/shard_map/all_to_all | solution.py:235
  20.3 85.4 %all-gather.2.cloned.1.call-start = ((), (), s32[]{:S(2)}) async-start(), calls=%async_computation.10 | async-start | bytes 5242880 | tf_op jit(solution)/shard_map/all_gather | solution.py:275
  21.4 35.1 %collective-permute-start.1 = (bf16[256,2048]{1,0:T(8,128)(2,1)}, bf16[256,2048]{1,0:T(8,128)(2,1)}, u32[]{:S(2)}, u32[]{:S(2)}) collective-permute-start(bf16[256,2048]{1,0:T(8,128)(2,1)} %slice.7), channel_id=1, source_target_pairs={{0,16},{16,0},{1,17},{17,1},{2,18},{18,2},{3,19},{19,3},{4,20},{20... | collective-permute-start | bytes 3145736 | tf_op jit(solution)/shard_map/ppermute | solution.py:260
  37.4 1.4 copy-start.10
  38.8 30.5 %all-to-all-start.1 = ((bf16[4,128,2048]{2,1,0:T(8,128)(2,1)}), bf16[4,128,2048]{2,1,0:T(8,128)(2,1)}, u32[]{:S(2)}, u32[]{:S(2)}) async-start(bf16[4,128,2048]{2,1,0:T(8,128)(2,1)} %bitcast.28), calls=%async_computation.1 | async-start | bytes 4194304 | tf_op jit(solution)/shard_map/all_to_all | solution.py:235
  69.3 6.5 %copy-start.16 = (s32[128,2]{1,0:T(8,128)S(1)}, s32[128,2]{1,0:T(8,128)}, u32[]{:S(2)}) copy-start(s32[128,2]{1,0:T(8,128)} %copy-done.15) | copy-start | bytes 3076
  69.3 30.4 %all-to-all-start.2 = ((bf16[4,128,2048]{2,1,0:T(8,128)(2,1)}), bf16[4,128,2048]{2,1,0:T(8,128)(2,1)}, u32[]{:S(2)}, u32[]{:S(2)}) async-start(bf16[4,128,2048]{2,1,0:T(8,128)(2,1)} %bitcast.25), calls=%async_computation.2 | async-start | bytes 4194304 | tf_op jit(solution)/shard_map/all_to_all | solution.py:235
  75.8 115.5 %reduce-scatter.3.cloned.1.call-start = ((), (), s32[]{:S(2)}) async-start(), calls=%async_computation.8 | async-start | bytes 2621440 | tf_op jit(solution)/shard_map/reduce_scatter | solution.py:295
  75.8 6.9 %collective-permute-start.2 = (s32[128,2]{1,0:T(8,128)S(1)}, s32[128,2]{1,0:T(8,128)S(1)}, u32[]{:S(2)}, u32[]{:S(2)}) collective-permute-start(s32[128,2]{1,0:T(8,128)S(1)} %copy-done.16), channel_id=1, source_target_pairs={{0,4},{4,0},{8,12},{12,8},{1,5},{5,1},{9,13},{13,9},{2,6},{6,2},{1... | collective-permute-start | bytes 3080 | tf_op jit(solution)/shard_map/ppermute | solution.py:281
  75.8 10.1 %collective-permute-start.3 = (s32[128,2]{1,0:T(8,128)S(1)}, s32[128,2]{1,0:T(8,128)S(1)}, u32[]{:S(2)}, u32[]{:S(2)}) collective-permute-start(s32[128,2]{1,0:T(8,128)S(1)} %copy-done.16), channel_id=1, source_target_pairs={{0,8},{4,12},{8,0},{12,4},{1,9},{5,13},{9,1},{13,5},{2,10},{6,14},... | collective-permute-start | bytes 3080 | tf_op jit(solution)/shard_map/ppermute | solution.py:281
  79.3 14.3 %collective-permute-start.4 = (s32[128,2]{1,0:T(8,128)S(1)}, s32[128,2]{1,0:T(8,128)S(1)}, u32[]{:S(2)}, u32[]{:S(2)}) collective-permute-start(s32[128,2]{1,0:T(8,128)S(1)} %copy-done.16), channel_id=1, source_target_pairs={{0,12},{4,8},{8,4},{12,0},{1,13},{5,9},{9,5},{13,1},{2,14},{6,10},... | collective-permute-start | bytes 3080 | tf_op jit(solution)/shard_map/ppermute | solution.py:281
  97.6 1.4 copy-start.2
  102.0 1.4 copy-start.1
  105.7 2.2 copy-start.17
  110.5 29.0 %all-to-all-start.3 = ((bf16[4,128,2048]{2,1,0:T(8,128)(2,1)}), bf16[4,128,2048]{2,1,0:T(8,128)(2,1)}, u32[]{:S(2)}, u32[]{:S(2)}) async-start(bf16[4,128,2048]{2,1,0:T(8,128)(2,1)} %bitcast.27), calls=%async_computation.5 | async-start | bytes 4194304 | tf_op jit(solution)/shard_map/all_to_all | solution.py:235
  115.6 2.5 %copy-start.18 = (bf16[512,4096]{1,0:T(8,128)(2,1)S(1)}, bf16[512,4096]{1,0:T(8,128)(2,1)}, u32[]{:S(2)}) copy-start(bf16[512,4096]{1,0:T(8,128)(2,1)} %all-gather.2.cloned.1.call-done.refs_4_) | copy-start | bytes 12582916
  119.4 1.3 copy-start.8
  139.5 30.2 %all-to-all-start.4 = ((bf16[4,128,2048]{2,1,0:T(8,128)(2,1)}), bf16[4,128,2048]{2,1,0:T(8,128)(2,1)}, u32[]{:S(2)}, u32[]{:S(2)}) async-start(bf16[4,128,2048]{2,1,0:T(8,128)(2,1)} %bitcast.26), calls=%async_computation.6 | async-start | bytes 4194304 | tf_op jit(solution)/shard_map/all_to_all | solution.py:235
  145.8 65.2 %reduce-scatter.5.cloned.1.call-start = ((), (), s32[]{:S(2)}) async-start(), calls=%async_computation.9 | async-start | bytes 2621440 | tf_op jit(solution)/shard_map/reduce_scatter | solution.py:295
  149.8 41.5 %collective-permute-start.5 = (bf16[256,2048]{1,0:T(8,128)(2,1)}, bf16[256,2048]{1,0:T(8,128)(2,1)}, u32[]{:S(2)}, u32[]{:S(2)}) collective-permute-start(bf16[256,2048]{1,0:T(8,128)(2,1)} %weight_grad_body.4), channel_id=1, source_target_pairs={{0,16},{16,0},{1,17},{17,1},{2,18},{18,2},{3,19},{19,3},{4,20},{20... | collective-permute-start | bytes 3145736 | tf_op jit(solution)/shard_map/ppermute | solution.py:260
  169.7 4.4 %copy-start.6 = (f32[512,512]{1,0:T(8,128)S(1)}, f32[512,512]{1,0:T(8,128)}, u32[]{:S(2)}) copy-start(f32[512,512]{1,0:T(8,128)} %copy-done.5) | copy-start | bytes 3145732
  173.1 24.4 %collective-permute-start.6 = (bf16[256,2048]{1,0:T(8,128)(2,1)}, bf16[256,2048]{1,0:T(8,128)(2,1)}, u32[]{:S(2)}, u32[]{:S(2)}) collective-permute-start(bf16[256,2048]{1,0:T(8,128)(2,1)} %weight_grad_body.6), channel_id=1, source_target_pairs={{0,16},{16,0},{1,17},{17,1},{2,18},{18,2},{3,19},{19,3},{4,20},{20... | collective-permute-start | bytes 3145736 | tf_op jit(solution)/shard_map/ppermute | solution.py:260
  178.0 30.6 %all-to-all-start.5 = ((bf16[16,32,512]{2,1,0:T(8,128)(2,1)}), bf16[16,32,512]{2,1,0:T(8,128)(2,1)}, u32[]{:S(2)}, u32[]{:S(2)}) async-start(bf16[16,32,512]{2,1,0:T(8,128)(2,1)} %bitcast.14), calls=%async_computation.7 | async-start | bytes 1048576 | tf_op jit(solution)/shard_map/all_to_all | solution.py:235
  200.0 8.7 %copy-start.14 = (s32[128,2]{1,0:T(8,128)S(1)}, s32[128,2]{1,0:T(8,128)}, u32[]{:S(2)}) copy-start(s32[128,2]{1,0:T(8,128)} %copy-done.13) | copy-start | bytes 3076
  200.0 11.0 %copy-start.19 = (bf16[128,2048]{1,0:T(8,128)(2,1)S(1)}, bf16[128,2048]{1,0:T(8,128)(2,1)}, u32[]{:S(2)}) copy-start(bf16[128,2048]{1,0:T(8,128)(2,1)} %reduce-scatter.3.cloned.1.call-done) | copy-start | bytes 1572868
  (7 other events, 8.0 us)
Sparse Core Ops, SparseCore 0:
  22.7 82.9 all-gather.1
  108.0 43.1 reduce-scatter.2
  153.6 51.7 reduce-scatter.4

commit v5 on v4

--- a/solution.py
+++ b/solution.py
@@ -181,17 +181,6 @@
         out_ref[:, at] = dot(hid_ref[:, lo:hi], grad_ref[:, at], 0, 0).astype(BF16)
 
 
-def average_body(replicas, place, *refs):
-    *pieces, out_ref = refs
-    n = len(pieces) // 2
-    c = 0
-    for a, b in zip(pieces[:n], pieces[n:]):
-        for at in steps(a.shape[1]):
-            total = a[:, at].astype(F32) + b[:, at].astype(F32)
-            out_ref[:, c + at.start : c + at.stop] = (total / replicas).astype(BF16)
-        c += a.shape[1]
-
-
 def back_dots(grad_ref, weights, offset):
     w = weights[0][:, offset : offset + grad_ref.shape[1]]
     return [dot(grad_ref[...], w, 1, 1)] + [dot(grad_ref[...], x[...], 1, 1) for x in weights[1:]]
@@ -344,8 +333,12 @@
             lax.psum_scatter(g, "dp", scatter_dimension=0, tiled=True) for g in other_grads
         ]
 
-    down_grad = call(
-        part(average_body, replicas), shaped((share, width)), after(place, own_b, layer_a), *own_grads, *other_grads
+    down_grad = jnp.concatenate(
+        [
+            ((own.astype(F32) + after(other, own_b, layer_a).astype(F32)) / replicas).astype(BF16)
+            for own, other in zip(own_grads, other_grads)
+        ],
+        1,
     )
     hidden_grad = call(
         part(hidden_grad_body, top, pair), shaped((tokens, top * units)), after(place, down_grad), col_own, gate_num, back_rows

time: 223 us -> 222 us (level)
  other arithmetic: 2.17 us -> 7.26 us
  Pallas kernels: 40.1 us -> 36 us
  local copies, waits for them, and re-layouts: 22.9 us -> 20.4 us
    pallas_call x17 -> x16, Pallas kernels: 40.1 us -> 36 us  [call(): pl.pallas_call(body, out_shape=outs, in_specs=[SMEM] + [VMEM] * (len(args...]
    convert_element_type x0 -> x2, other arithmetic: none -> 3.55 us  [on_device(): ((own.astype(F32) + after(other, own_b, layer_a).astype(F32)) / replicas)...]
    all_to_all x6, waiting for transfers between devices: 57.6 us -> 60.3 us  [exchange(): return lax.all_to_all(x, axes, split_axis=0, concat_axis=0, tiled=True)]
    unnamed x49 -> x47, local copies, waits for them, and re-layouts: 18.5 us -> 16 us
  transfers between devices with their start and end apart: 16 -> 16, of which waited for: 12 -> 12; matrix products, arithmetic and copies ran while one was open for 1% -> 3% of each run, Pallas kernels for 18% -> 16%
where the time goes in v5:
time: 222 us; the launch traced here: 219 us
  waiting for transfers between devices  93.5 us (42%)
  starting transfers between devices  47.8 us (22%)
  Pallas kernels  36 us (16%)
  local copies, waits for them, and re-layouts  20.4 us (9%)
  between operations  14 us (6%)
  other arithmetic  7.26 us (3%)
    all_to_all x6, waiting for transfers between devices, exchange(): return lax.all_to_all(x, axes, split_axis=0, concat_axis=0, tiled=True)  60.3 us
    all_to_all x6, starting transfers between devices, exchange(): return lax.all_to_all(x, axes, split_axis=0, concat_axis=0, tiled=True)  40.9 us
    pallas_call x16, Pallas kernels, call(): pl.pallas_call(body, out_shape=outs, in_specs=[SMEM] + [VMEM] * (len(args...  36 us
    unnamed x47, local copies, waits for them, and re-layouts  16 us
    ppermute x4, waiting for transfers between devices, to_replica(): return lax.ppermute(x, 'dp', [(0, 1), (1, 0)])  15.9 us
    ppermute x3, waiting for transfers between devices, on_device(): lax.ppermute(expert_ids, 'z', [(i, i ^ j) for i in range(PLANES)])  14.3 us
  transfers between devices with their start and end apart: 16, of which 12 were waited for; matrix products, arithmetic and copies ran while one was open for 3% of the time, Pallas kernels for 16%

profile of v5, /device:TPU:11, one launch (start us, length us, event | category | flops | bytes accessed | tf_op | source)
XLA Modules:
  0.0 219.0 jit_solution(16231438301043670294)
XLA Ops:
  7.2 2.5 %slice.8 = bf16[256,2048]{1,0:T(8,128)(2,1)} slice(bf16[256,4096]{1,0:T(8,128)(2,1)} %bitcast.20), slice={[0:256], [0:2048]} | slice | bytes 2097152 | tf_op jit(solution)/shard_map/slice | solution.py:229
  11.3 2.2 prepare_body.1
  13.4 6.8 %all-to-all-start = ((bf16[16,32,512]{2,1,0:T(8,128)(2,1)}), bf16[16,32,512]{2,1,0:T(8,128)(2,1)S(1)}, u32[]{:S(2)}, u32[]{:S(2)}) async-start(bf16[16,32,512]{2,1,0:T(8,128)(2,1)} %bitcast.3), calls=%async_computation | async-start | bytes 1048576 | tf_op jit(solution)/shard_map/all_to_all | solution.py:224
  21.7 12.6 %all-to-all-done = bf16[16,32,512]{2,1,0:T(8,128)(2,1)S(1)} async-done(((bf16[16,32,512]{2,1,0:T(8,128)(2,1)}), bf16[16,32,512]{2,1,0:T(8,128)(2,1)S(1)}, u32[]{:S(2)}, u32[]{:S(2)}) %all-to-all-start) | async-done | bytes 524320 | tf_op jit(solution)/shard_map/all_to_all | solution.py:224
  34.9 2.5 %forward_body.2 = bf16[512,2048]{1,0:T(8,128)(2,1)S(1)} custom-call(s32[3]{0:T(128)S(1)} %pad_add_fusion.place, bf16[512,512]{1,0:T(8,128)(2,1)S(1)} %arrange_body.1.hid_ref, bf16[256,4096]{1,0:T(8,128)(2,1)S(1)} %bitcast.22, bf16[256,2048]{1,0:T(8,128)(2,1)} %collective-permute-done.refs_1_), custom_call_target="tpu_custom_call" | custom-call | flops 274877906944 | tf_op jit(solution)/shard_map/forward_body/pallas_call | solution.py:28
  38.8 6.6 %all-to-all-start.1 = ((bf16[4,128,2048]{2,1,0:T(8,128)(2,1)}), bf16[4,128,2048]{2,1,0:T(8,128)(2,1)}, u32[]{:S(2)}, u32[]{:S(2)}) async-start(bf16[4,128,2048]{2,1,0:T(8,128)(2,1)} %bitcast.29), calls=%async_computation.1 | async-start | bytes 4194304 | tf_op jit(solution)/shard_map/all_to_all | solution.py:224
  45.4 11.1 %collective-permute-done.1.refs_1_ = bf16[256,2048]{1,0:T(8,128)(2,1)} collective-permute-done((bf16[256,2048]{1,0:T(8,128)(2,1)}, bf16[256,2048]{1,0:T(8,128)(2,1)}, u32[]{:S(2)}, u32[]{:S(2)}) %collective-permute-start.1) | collective-permute-done | bytes 1048608 | tf_op jit(solution)/shard_map/ppermute | solution.py:249
  56.5 2.5 %forward_body.3 = bf16[512,2048]{1,0:T(8,128)(2,1)S(1)} custom-call(s32[3]{0:T(128)S(1)} %pad_add_fusion.place, bf16[512,512]{1,0:T(8,128)(2,1)S(1)} %arrange_body.1.hid_ref, bf16[256,4096]{1,0:T(8,128)(2,1)S(1)} %bitcast.23, bf16[256,2048]{1,0:T(8,128)(2,1)} %collective-permute-done.1.refs_1_), custom_call_target="tpu_custom_call" | custom-call | flops 274877906944 | tf_op jit(solution)/shard_map/forward_body/pallas_call | solution.py:28
  60.3 9.0 %all-to-all-done.1 = bf16[4,128,2048]{2,1,0:T(8,128)(2,1)} async-done(((bf16[4,128,2048]{2,1,0:T(8,128)(2,1)}), bf16[4,128,2048]{2,1,0:T(8,128)(2,1)}, u32[]{:S(2)}, u32[]{:S(2)}) %all-to-all-start.1) | async-done | bytes 2097184 | tf_op jit(solution)/shard_map/all_to_all | solution.py:224
  69.3 6.5 %all-to-all-start.2 = ((bf16[4,128,2048]{2,1,0:T(8,128)(2,1)}), bf16[4,128,2048]{2,1,0:T(8,128)(2,1)}, u32[]{:S(2)}, u32[]{:S(2)}) async-start(bf16[4,128,2048]{2,1,0:T(8,128)(2,1)} %bitcast.26), calls=%async_computation.2 | async-start | bytes 4194304 | tf_op jit(solution)/shard_map/all_to_all | solution.py:224
  75.8 3.5 %collective-permute-start.3 = (s32[128,2]{1,0:T(8,128)S(1)}, s32[128,2]{1,0:T(8,128)S(1)}, u32[]{:S(2)}, u32[]{:S(2)}) collective-permute-start(s32[128,2]{1,0:T(8,128)S(1)} %copy-done.15), channel_id=1, source_target_pairs={{0,8},{4,12},{8,0},{12,4},{1,9},{5,13},{9,1},{13,5},{2,10},{6,14},... | collective-permute-start | bytes 3080 | tf_op jit(solution)/shard_map/ppermute | solution.py:270
  79.3 3.4 %collective-permute-done.2.refs_1_ = s32[128,2]{1,0:T(8,128)S(1)} collective-permute-done((s32[128,2]{1,0:T(8,128)S(1)}, s32[128,2]{1,0:T(8,128)S(1)}, u32[]{:S(2)}, u32[]{:S(2)}) %collective-permute-start.2) | collective-permute-done | bytes 1056 | tf_op jit(solution)/shard_map/ppermute | solution.py:270
  82.7 3.1 %collective-permute-done.3.refs_2_ = s32[128,2]{1,0:T(8,128)S(1)} collective-permute-done((s32[128,2]{1,0:T(8,128)S(1)}, s32[128,2]{1,0:T(8,128)S(1)}, u32[]{:S(2)}, u32[]{:S(2)}) %collective-permute-start.3) | collective-permute-done | bytes 1056 | tf_op jit(solution)/shard_map/ppermute | solution.py:270
  85.9 7.7 %collective-permute-done.4.refs_3_ = s32[128,2]{1,0:T(8,128)S(1)} collective-permute-done((s32[128,2]{1,0:T(8,128)S(1)}, s32[128,2]{1,0:T(8,128)S(1)}, u32[]{:S(2)}, u32[]{:S(2)}) %collective-permute-start.4) | collective-permute-done | bytes 1056 | tf_op jit(solution)/shard_map/ppermute | solution.py:270
  95.2 2.4 %combine_body.2 = bf16[512,2048]{1,0:T(8,128)(2,1)S(1)} custom-call(s32[3]{0:T(128)S(1)} %pad_add_fusion.place, s32[2,128]{1,0:T(2,128)S(1)} %get-tuple-element.30.refs_0_, s32[2,128]{1,0:T(2,128)S(1)} %get-tuple-element.31.refs_1_, s32[2,128]{1,0:T(2,128)S(1)} %get-tuple-element.32.refs_2_, s32[2,128]{1,0:T(2,128)S(1)} %get-tuple-element.33.refs_3_, ...), custom_call_target="tpu_custom_call" | custom-call | tf_op jit(solution)/shard_map/combine_body/pallas_call | solution.py:28
  99.7 2.4 %combine_body.3 = bf16[512,2048]{1,0:T(8,128)(2,1)S(1)} custom-call(s32[3]{0:T(128)S(1)} %pad_add_fusion.place, s32[2,128]{1,0:T(2,128)S(1)} %get-tuple-element.30.refs_0_, s32[2,128]{1,0:T(2,128)S(1)} %get-tuple-element.31.refs_1_, s32[2,128]{1,0:T(2,128)S(1)} %get-tuple-element.32.refs_2_, s32[2,128]{1,0:T(2,128)S(1)} %get-tuple-element.33.refs_3_, ...), custom_call_target="tpu_custom_call" | custom-call | tf_op jit(solution)/shard_map/combine_body/pallas_call | solution.py:28
  103.4 2.3 %all-gather.2.cloned.1.call-done.refs_4_ = bf16[512,4096]{1,0:T(8,128)(2,1)} async-done(((bf16[128,4096]{1,0:T(8,128)(2,1)}), bf16[512,4096]{1,0:T(8,128)(2,1)}) %all-gather.2.cloned.1.call-update) | async-done | bytes 4194320 | tf_op jit(solution)/shard_map/all_gather | solution.py:264
  105.7 2.2 copy-done.16
  110.5 5.1 %all-to-all-start.3 = ((bf16[4,128,2048]{2,1,0:T(8,128)(2,1)}), bf16[4,128,2048]{2,1,0:T(8,128)(2,1)}, u32[]{:S(2)}, u32[]{:S(2)}) async-start(bf16[4,128,2048]{2,1,0:T(8,128)(2,1)} %bitcast.28), calls=%async_computation.5 | async-start | bytes 4194304 | tf_op jit(solution)/shard_map/all_to_all | solution.py:224
  115.6 2.5 %copy-done.17 = bf16[512,4096]{1,0:T(8,128)(2,1)S(1)} copy-done((bf16[512,4096]{1,0:T(8,128)(2,1)S(1)}, bf16[512,4096]{1,0:T(8,128)(2,1)}, u32[]{:S(2)}) %copy-start.17) | copy-done | bytes 4194328
  120.7 18.8 %all-to-all-done.3 = bf16[4,128,2048]{2,1,0:T(8,128)(2,1)} async-done(((bf16[4,128,2048]{2,1,0:T(8,128)(2,1)}), bf16[4,128,2048]{2,1,0:T(8,128)(2,1)}, u32[]{:S(2)}, u32[]{:S(2)}) %all-to-all-start.3) | async-done | bytes 2097184 | tf_op jit(solution)/shard_map/all_to_all | solution.py:224
  139.5 6.3 %all-to-all-start.4 = ((bf16[4,128,2048]{2,1,0:T(8,128)(2,1)}), bf16[4,128,2048]{2,1,0:T(8,128)(2,1)}, u32[]{:S(2)}, u32[]{:S(2)}) async-start(bf16[4,128,2048]{2,1,0:T(8,128)(2,1)} %bitcast.27), calls=%async_computation.6 | async-start | bytes 4194304 | tf_op jit(solution)/shard_map/all_to_all | solution.py:224
  146.6 3.3 %weight_grad_body.4 = bf16[256,2048]{1,0:T(8,128)(2,1)} custom-call(s32[3]{0:T(128)S(1)} %pad_add_fusion.place, bf16[512,512]{1,0:T(8,128)(2,1)S(1)} %arrange_body.1.hid_ref, bf16[512,2048]{1,0:T(8,128)(2,1)} %bitcast.11.grad_ref), custom_call_target="tpu_custom_call" | custom-call | tf_op jit(solution)/shard_map/weight_grad_body/pallas_call | solution.py:28
  150.8 2.3 %weight_grad_body.5 = bf16[256,2048]{1,0:T(8,128)(2,1)S(1)} custom-call(s32[3]{0:T(128)S(1)} %pad_add_fusion.place, bf16[512,512]{1,0:T(8,128)(2,1)S(1)} %arrange_body.1.hid_ref, bf16[512,2048]{1,0:T(8,128)(2,1)} %bitcast.11.grad_ref), custom_call_target="tpu_custom_call" | custom-call | tf_op jit(solution)/shard_map/weight_grad_body/pallas_call | solution.py:28
  154.2 3.1 %backward_first_body.1.first_ref = f32[512,512]{1,0:T(8,128)S(1)} custom-call(s32[3]{0:T(128)S(1)} %pad_add_fusion.place, bf16[512,2048]{1,0:T(8,128)(2,1)} %bitcast.11.grad_ref, bf16[256,4096]{1,0:T(8,128)(2,1)S(1)} %bitcast.24, bf16[256,2048]{1,0:T(8,128)(2,1)} %collective-permute-done.refs_1_), custom_call_target="tpu_custom_call" | custom-call | tf_op jit(solution)/shard_map/backward_first_body/pallas_call | solution.py:28
  158.3 11.4 %all-to-all-done.4 = bf16[4,128,2048]{2,1,0:T(8,128)(2,1)} async-done(((bf16[4,128,2048]{2,1,0:T(8,128)(2,1)}), bf16[4,128,2048]{2,1,0:T(8,128)(2,1)}, u32[]{:S(2)}, u32[]{:S(2)}) %all-to-all-start.4) | async-done | bytes 2097184 | tf_op jit(solution)/shard_map/all_to_all | solution.py:224
  169.7 3.4 %weight_grad_body.6 = bf16[256,2048]{1,0:T(8,128)(2,1)} custom-call(s32[3]{0:T(128)S(1)} %pad_add_fusion.place, bf16[512,512]{1,0:T(8,128)(2,1)S(1)} %arrange_body.1.hid_ref, bf16[512,2048]{1,0:T(8,128)(2,1)} %bitcast.13.grad_ref), custom_call_target="tpu_custom_call" | custom-call | tf_op jit(solution)/shard_map/weight_grad_body/pallas_call | solution.py:28
  174.1 4.0 %backward_last_body.1 = bf16[512,512]{1,0:T(8,128)(2,1)} custom-call(s32[3]{0:T(128)S(1)} %pad_add_fusion.place, f32[512,512]{1,0:T(8,128)S(1)} %copy-done.5, bf16[512,2048]{1,0:T(8,128)(2,1)} %bitcast.13.grad_ref, bf16[256,4096]{1,0:T(8,128)(2,1)S(1)} %bitcast.25, bf16[256,2048]{1,0:T(8,128)(2,1)} %collective-permute-done.1.refs_1_), custom_call_target="tpu_custom_call" | custom-call | tf_op jit(solution)/shard_map/backward_last_body/pallas_call | solution.py:28
  178.1 2.3 %weight_grad_body.7 = bf16[256,2048]{1,0:T(8,128)(2,1)S(1)} custom-call(s32[3]{0:T(128)S(1)} %pad_add_fusion.place, bf16[512,512]{1,0:T(8,128)(2,1)S(1)} %arrange_body.1.hid_ref, bf16[512,2048]{1,0:T(8,128)(2,1)} %bitcast.13.grad_ref), custom_call_target="tpu_custom_call" | custom-call | flops 274877906944 | tf_op jit(solution)/shard_map/weight_grad_body/pallas_call | solution.py:28
  181.4 9.4 %all-to-all-start.5 = ((bf16[16,32,512]{2,1,0:T(8,128)(2,1)}), bf16[16,32,512]{2,1,0:T(8,128)(2,1)S(1)}, u32[]{:S(2)}, u32[]{:S(2)}) async-start(bf16[16,32,512]{2,1,0:T(8,128)(2,1)} %bitcast.14), calls=%async_computation.7 | async-start | bytes 1048576 | tf_op jit(solution)/shard_map/all_to_all | solution.py:224
  192.8 4.8 %collective-permute-done.6 = bf16[256,2048]{1,0:T(8,128)(2,1)} collective-permute-done((bf16[256,2048]{1,0:T(8,128)(2,1)}, bf16[256,2048]{1,0:T(8,128)(2,1)}, u32[]{:S(2)}, u32[]{:S(2)}) %collective-permute-start.6) | collective-permute-done | bytes 1048608 | tf_op jit(solution)/shard_map/ppermute | solution.py:249
  200.7 7.9 %all-to-all-done.5 = bf16[16,32,512]{2,1,0:T(8,128)(2,1)S(1)} async-done(((bf16[16,32,512]{2,1,0:T(8,128)(2,1)}), bf16[16,32,512]{2,1,0:T(8,128)(2,1)S(1)}, u32[]{:S(2)}, u32[]{:S(2)}) %all-to-all-start.5) | async-done | bytes 524320 | tf_op jit(solution)/shard_map/all_to_all | solution.py:224
  (74 shorter events, 31.0 us)
Async XLA Ops:
  7.2 3.7 %copy-start.20 = (s32[128,2]{0,1:T(2,128)S(1)}, s32[128,2]{0,1:T(2,128)}, u32[]{:S(2)}) copy-start(s32[128,2]{0,1:T(2,128)} %param.7) | copy-start | bytes 3076
  7.2 3.8 %copy-start.21 = (s32[128,2]{0,1:T(2,128)S(1)}, s32[128,2]{0,1:T(2,128)}, u32[]{:S(2)}) copy-start(s32[128,2]{0,1:T(2,128)} %param.8) | copy-start | bytes 3076
  7.2 4.0 %copy-start.19 = (bf16[128,2,512]{2,1,0:T(2,128)(2,1)S(1)}, bf16[128,2,512]{2,1,0:T(2,128)(2,1)}, u32[]{:S(2)}) copy-start(bf16[128,2,512]{2,1,0:T(2,128)(2,1)} %param.5) | copy-start | bytes 786436
  7.2 13.1 %copy-start = (bf16[1,256,4096]{2,1,0:T(8,128)(2,1)S(1)}, bf16[1,256,4096]{2,1,0:T(8,128)(2,1)}, u32[]{:S(2)}) copy-start(bf16[1,256,4096]{2,1,0:T(8,128)(2,1)} %param.9) | copy-start | bytes 6291460
  9.7 25.2 %collective-permute-start = (bf16[256,2048]{1,0:T(8,128)(2,1)}, bf16[256,2048]{1,0:T(8,128)(2,1)}, u32[]{:S(2)}, u32[]{:S(2)}) collective-permute-start(bf16[256,2048]{1,0:T(8,128)(2,1)} %slice.8), channel_id=1, source_target_pairs={{0,16},{16,0},{1,17},{17,1},{2,18},{18,2},{3,19},{19,3},{4,20},{20... | collective-permute-start | bytes 3145736 | tf_op jit(solution)/shard_map/ppermute | solution.py:249
  11.0 2.4 %copy-start.14 = (s32[128,2]{1,0:T(8,128)}, s32[128,2]{1,0:T(8,128)S(1)}, u32[]{:S(2)}) copy-start(s32[128,2]{1,0:T(8,128)S(1)} %copy.8.ids_ref.refs_0_) | copy-start | bytes 3076
  11.1 2.3 %copy-start.12 = (s32[128,2]{1,0:T(8,128)}, s32[128,2]{1,0:T(8,128)S(1)}, u32[]{:S(2)}) copy-start(s32[128,2]{1,0:T(8,128)S(1)} %copy.9.num_ref) | copy-start | bytes 3076
  13.4 20.8 %all-to-all-start = ((bf16[16,32,512]{2,1,0:T(8,128)(2,1)}), bf16[16,32,512]{2,1,0:T(8,128)(2,1)S(1)}, u32[]{:S(2)}, u32[]{:S(2)}) async-start(bf16[16,32,512]{2,1,0:T(8,128)(2,1)} %bitcast.3), calls=%async_computation | async-start | bytes 1048576 | tf_op jit(solution)/shard_map/all_to_all | solution.py:224
  20.3 85.4 %all-gather.2.cloned.1.call-start = ((), (), s32[]{:S(2)}) async-start(), calls=%async_computation.10 | async-start | bytes 5242880 | tf_op jit(solution)/shard_map/all_gather | solution.py:264
  21.4 35.1 %collective-permute-start.1 = (bf16[256,2048]{1,0:T(8,128)(2,1)}, bf16[256,2048]{1,0:T(8,128)(2,1)}, u32[]{:S(2)}, u32[]{:S(2)}) collective-permute-start(bf16[256,2048]{1,0:T(8,128)(2,1)} %slice.7), channel_id=1, source_target_pairs={{0,16},{16,0},{1,17},{17,1},{2,18},{18,2},{3,19},{19,3},{4,20},{20... | collective-permute-start | bytes 3145736 | tf_op jit(solution)/shard_map/ppermute | solution.py:249
  37.4 1.4 copy-start.9
  38.8 30.5 %all-to-all-start.1 = ((bf16[4,128,2048]{2,1,0:T(8,128)(2,1)}), bf16[4,128,2048]{2,1,0:T(8,128)(2,1)}, u32[]{:S(2)}, u32[]{:S(2)}) async-start(bf16[4,128,2048]{2,1,0:T(8,128)(2,1)} %bitcast.29), calls=%async_computation.1 | async-start | bytes 4194304 | tf_op jit(solution)/shard_map/all_to_all | solution.py:224
  69.3 6.5 %copy-start.15 = (s32[128,2]{1,0:T(8,128)S(1)}, s32[128,2]{1,0:T(8,128)}, u32[]{:S(2)}) copy-start(s32[128,2]{1,0:T(8,128)} %copy-done.14) | copy-start | bytes 3076
  69.3 30.4 %all-to-all-start.2 = ((bf16[4,128,2048]{2,1,0:T(8,128)(2,1)}), bf16[4,128,2048]{2,1,0:T(8,128)(2,1)}, u32[]{:S(2)}, u32[]{:S(2)}) async-start(bf16[4,128,2048]{2,1,0:T(8,128)(2,1)} %bitcast.26), calls=%async_computation.2 | async-start | bytes 4194304 | tf_op jit(solution)/shard_map/all_to_all | solution.py:224
  75.8 105.6 %reduce-scatter.3.cloned.1.call-start = ((), (), s32[]{:S(2)}) async-start(), calls=%async_computation.8 | async-start | bytes 2621440 | tf_op jit(solution)/shard_map/reduce_scatter | solution.py:284
  75.8 7.0 %collective-permute-start.2 = (s32[128,2]{1,0:T(8,128)S(1)}, s32[128,2]{1,0:T(8,128)S(1)}, u32[]{:S(2)}, u32[]{:S(2)}) collective-permute-start(s32[128,2]{1,0:T(8,128)S(1)} %copy-done.15), channel_id=1, source_target_pairs={{0,4},{4,0},{8,12},{12,8},{1,5},{5,1},{9,13},{13,9},{2,6},{6,2},{1... | collective-permute-start | bytes 3080 | tf_op jit(solution)/shard_map/ppermute | solution.py:270
  75.8 10.1 %collective-permute-start.3 = (s32[128,2]{1,0:T(8,128)S(1)}, s32[128,2]{1,0:T(8,128)S(1)}, u32[]{:S(2)}, u32[]{:S(2)}) collective-permute-start(s32[128,2]{1,0:T(8,128)S(1)} %copy-done.15), channel_id=1, source_target_pairs={{0,8},{4,12},{8,0},{12,4},{1,9},{5,13},{9,1},{13,5},{2,10},{6,14},... | collective-permute-start | bytes 3080 | tf_op jit(solution)/shard_map/ppermute | solution.py:270
  79.3 14.3 %collective-permute-start.4 = (s32[128,2]{1,0:T(8,128)S(1)}, s32[128,2]{1,0:T(8,128)S(1)}, u32[]{:S(2)}, u32[]{:S(2)}) collective-permute-start(s32[128,2]{1,0:T(8,128)S(1)} %copy-done.15), channel_id=1, source_target_pairs={{0,12},{4,8},{8,4},{12,0},{1,13},{5,9},{9,5},{13,1},{2,14},{6,10},... | collective-permute-start | bytes 3080 | tf_op jit(solution)/shard_map/ppermute | solution.py:270
  97.6 1.4 copy-start.2
  102.0 1.4 copy-start.1
  105.7 2.2 copy-start.16
  110.5 29.0 %all-to-all-start.3 = ((bf16[4,128,2048]{2,1,0:T(8,128)(2,1)}), bf16[4,128,2048]{2,1,0:T(8,128)(2,1)}, u32[]{:S(2)}, u32[]{:S(2)}) async-start(bf16[4,128,2048]{2,1,0:T(8,128)(2,1)} %bitcast.28), calls=%async_computation.5 | async-start | bytes 4194304 | tf_op jit(solution)/shard_map/all_to_all | solution.py:224
  115.6 2.5 %copy-start.17 = (bf16[512,4096]{1,0:T(8,128)(2,1)S(1)}, bf16[512,4096]{1,0:T(8,128)(2,1)}, u32[]{:S(2)}) copy-start(bf16[512,4096]{1,0:T(8,128)(2,1)} %all-gather.2.cloned.1.call-done.refs_4_) | copy-start | bytes 12582916
  139.5 30.2 %all-to-all-start.4 = ((bf16[4,128,2048]{2,1,0:T(8,128)(2,1)}), bf16[4,128,2048]{2,1,0:T(8,128)(2,1)}, u32[]{:S(2)}, u32[]{:S(2)}) async-start(bf16[4,128,2048]{2,1,0:T(8,128)(2,1)} %bitcast.27), calls=%async_computation.6 | async-start | bytes 4194304 | tf_op jit(solution)/shard_map/all_to_all | solution.py:224
  145.8 64.5 %reduce-scatter.5.cloned.1.call-start = ((), (), s32[]{:S(2)}) async-start(), calls=%async_computation.9 | async-start | bytes 2621440 | tf_op jit(solution)/shard_map/reduce_scatter | solution.py:284
  149.9 31.5 %collective-permute-start.5 = (bf16[256,2048]{1,0:T(8,128)(2,1)}, bf16[256,2048]{1,0:T(8,128)(2,1)}, u32[]{:S(2)}, u32[]{:S(2)}) collective-permute-start(bf16[256,2048]{1,0:T(8,128)(2,1)} %weight_grad_body.4), channel_id=1, source_target_pairs={{0,16},{16,0},{1,17},{17,1},{2,18},{18,2},{3,19},{19,3},{4,20},{20... | collective-permute-start | bytes 3145736 | tf_op jit(solution)/shard_map/ppermute | solution.py:249
  169.7 4.4 %copy-start.5 = (f32[512,512]{1,0:T(8,128)S(1)}, f32[512,512]{1,0:T(8,128)}, u32[]{:S(2)}) copy-start(f32[512,512]{1,0:T(8,128)} %copy-done.4) | copy-start | bytes 3145732
  173.1 24.4 %collective-permute-start.6 = (bf16[256,2048]{1,0:T(8,128)(2,1)}, bf16[256,2048]{1,0:T(8,128)(2,1)}, u32[]{:S(2)}, u32[]{:S(2)}) collective-permute-start(bf16[256,2048]{1,0:T(8,128)(2,1)} %weight_grad_body.6), channel_id=1, source_target_pairs={{0,16},{16,0},{1,17},{17,1},{2,18},{18,2},{3,19},{19,3},{4,20},{20... | collective-permute-start | bytes 3145736 | tf_op jit(solution)/shard_map/ppermute | solution.py:249
  181.4 16.2 %copy-start.11 = (bf16[256,2048]{1,0:T(8,128)(2,1)S(1)}, bf16[256,2048]{1,0:T(8,128)(2,1)}, u32[]{:S(2)}) copy-start(bf16[256,2048]{1,0:T(8,128)(2,1)} %copy-done.10) | copy-start | bytes 3145732
  181.4 27.2 %all-to-all-start.5 = ((bf16[16,32,512]{2,1,0:T(8,128)(2,1)}), bf16[16,32,512]{2,1,0:T(8,128)(2,1)S(1)}, u32[]{:S(2)}, u32[]{:S(2)}) async-start(bf16[16,32,512]{2,1,0:T(8,128)(2,1)} %bitcast.14), calls=%async_computation.7 | async-start | bytes 1048576 | tf_op jit(solution)/shard_map/all_to_all | solution.py:224
  199.2 9.4 %copy-start.13 = (s32[128,2]{1,0:T(8,128)S(1)}, s32[128,2]{1,0:T(8,128)}, u32[]{:S(2)}) copy-start(s32[128,2]{1,0:T(8,128)} %copy-done.12) | copy-start | bytes 3076
  199.2 11.2 %copy-start.18 = (bf16[128,2048]{1,0:T(8,128)(2,1)S(1)}, bf16[128,2048]{1,0:T(8,128)(2,1)}, u32[]{:S(2)}) copy-start(bf16[128,2048]{1,0:T(8,128)(2,1)} %reduce-scatter.3.cloned.1.call-done) | copy-start | bytes 1572868
  (6 other events, 6.9 us)
Sparse Core Ops, SparseCore 0:
  22.7 82.9 all-gather.1
  108.0 43.1 reduce-scatter.2
  153.6 47.6 reduce-scatter.4

commit v6 on v5

--- a/solution.py
+++ b/solution.py
@@ -33,7 +33,7 @@
         scratch_shapes=scratch,
         name=(body.func if isinstance(body, functools.partial) else body).__name__,
         cost_estimate=pl.CostEstimate(flops=cost, bytes_accessed=0, transcendentals=0),
-        compiler_params=pltpu.CompilerParams(vmem_limit_bytes=16 * 1024 * 1024),
+        compiler_params=pltpu.CompilerParams(vmem_limit_bytes=8 * 1024 * 1024),
     )(*args)
 
 

time: 222 us -> 222 us (level)
  no operation moved by 1% of the time
where the time goes in v6:
time: 222 us; the launch traced here: 219 us
  waiting for transfers between devices  93.5 us (42%)
  starting transfers between devices  47.8 us (22%)
  Pallas kernels  36 us (16%)
  local copies, waits for them, and re-layouts  20.4 us (9%)
  between operations  14 us (6%)
  other arithmetic  7.26 us (3%)
    all_to_all x6, waiting for transfers between devices, exchange(): return lax.all_to_all(x, axes, split_axis=0, concat_axis=0, tiled=True)  60.3 us
    all_to_all x6, starting transfers between devices, exchange(): return lax.all_to_all(x, axes, split_axis=0, concat_axis=0, tiled=True)  40.9 us
    pallas_call x16, Pallas kernels, call(): pl.pallas_call(body, out_shape=outs, in_specs=[SMEM] + [VMEM] * (len(args...  36 us
    unnamed x47, local copies, waits for them, and re-layouts  16 us
    ppermute x4, waiting for transfers between devices, to_replica(): return lax.ppermute(x, 'dp', [(0, 1), (1, 0)])  15.9 us
    ppermute x3, waiting for transfers between devices, on_device(): lax.ppermute(expert_ids, 'z', [(i, i ^ j) for i in range(PLANES)])  14.3 us
  transfers between devices with their start and end apart: 16, of which 12 were waited for; matrix products, arithmetic and copies ran while one was open for 3% of the time, Pallas kernels for 16%

profile of v6, /device:TPU:11, one launch (start us, length us, event | category | flops | bytes accessed | tf_op | source)
XLA Modules:
  0.0 219.0 jit_solution(934772202899515395)
XLA Ops:
  7.2 2.5 %slice.8 = bf16[256,2048]{1,0:T(8,128)(2,1)} slice(bf16[256,4096]{1,0:T(8,128)(2,1)} %bitcast.20), slice={[0:256], [0:2048]} | slice | bytes 2097152 | tf_op jit(solution)/shard_map/slice | solution.py:229
  11.3 2.2 prepare_body.1
  13.4 6.8 %all-to-all-start = ((bf16[16,32,512]{2,1,0:T(8,128)(2,1)}), bf16[16,32,512]{2,1,0:T(8,128)(2,1)S(1)}, u32[]{:S(2)}, u32[]{:S(2)}) async-start(bf16[16,32,512]{2,1,0:T(8,128)(2,1)} %bitcast.3), calls=%async_computation | async-start | bytes 1048576 | tf_op jit(solution)/shard_map/all_to_all | solution.py:224
  21.7 12.6 %all-to-all-done = bf16[16,32,512]{2,1,0:T(8,128)(2,1)S(1)} async-done(((bf16[16,32,512]{2,1,0:T(8,128)(2,1)}), bf16[16,32,512]{2,1,0:T(8,128)(2,1)S(1)}, u32[]{:S(2)}, u32[]{:S(2)}) %all-to-all-start) | async-done | bytes 524320 | tf_op jit(solution)/shard_map/all_to_all | solution.py:224
  34.9 2.5 %forward_body.2 = bf16[512,2048]{1,0:T(8,128)(2,1)S(1)} custom-call(s32[3]{0:T(128)S(1)} %pad_add_fusion.place, bf16[512,512]{1,0:T(8,128)(2,1)S(1)} %arrange_body.1.hid_ref, bf16[256,4096]{1,0:T(8,128)(2,1)S(1)} %bitcast.22, bf16[256,2048]{1,0:T(8,128)(2,1)} %collective-permute-done.refs_1_), custom_call_target="tpu_custom_call" | custom-call | flops 274877906944 | tf_op jit(solution)/shard_map/forward_body/pallas_call | solution.py:28
  38.8 6.6 %all-to-all-start.1 = ((bf16[4,128,2048]{2,1,0:T(8,128)(2,1)}), bf16[4,128,2048]{2,1,0:T(8,128)(2,1)}, u32[]{:S(2)}, u32[]{:S(2)}) async-start(bf16[4,128,2048]{2,1,0:T(8,128)(2,1)} %bitcast.29), calls=%async_computation.1 | async-start | bytes 4194304 | tf_op jit(solution)/shard_map/all_to_all | solution.py:224
  45.4 11.1 %collective-permute-done.1.refs_1_ = bf16[256,2048]{1,0:T(8,128)(2,1)} collective-permute-done((bf16[256,2048]{1,0:T(8,128)(2,1)}, bf16[256,2048]{1,0:T(8,128)(2,1)}, u32[]{:S(2)}, u32[]{:S(2)}) %collective-permute-start.1) | collective-permute-done | bytes 1048608 | tf_op jit(solution)/shard_map/ppermute | solution.py:249
  56.5 2.5 %forward_body.3 = bf16[512,2048]{1,0:T(8,128)(2,1)S(1)} custom-call(s32[3]{0:T(128)S(1)} %pad_add_fusion.place, bf16[512,512]{1,0:T(8,128)(2,1)S(1)} %arrange_body.1.hid_ref, bf16[256,4096]{1,0:T(8,128)(2,1)S(1)} %bitcast.23, bf16[256,2048]{1,0:T(8,128)(2,1)} %collective-permute-done.1.refs_1_), custom_call_target="tpu_custom_call" | custom-call | flops 274877906944 | tf_op jit(solution)/shard_map/forward_body/pallas_call | solution.py:28
  60.3 9.0 %all-to-all-done.1 = bf16[4,128,2048]{2,1,0:T(8,128)(2,1)} async-done(((bf16[4,128,2048]{2,1,0:T(8,128)(2,1)}), bf16[4,128,2048]{2,1,0:T(8,128)(2,1)}, u32[]{:S(2)}, u32[]{:S(2)}) %all-to-all-start.1) | async-done | bytes 2097184 | tf_op jit(solution)/shard_map/all_to_all | solution.py:224
  69.3 6.5 %all-to-all-start.2 = ((bf16[4,128,2048]{2,1,0:T(8,128)(2,1)}), bf16[4,128,2048]{2,1,0:T(8,128)(2,1)}, u32[]{:S(2)}, u32[]{:S(2)}) async-start(bf16[4,128,2048]{2,1,0:T(8,128)(2,1)} %bitcast.26), calls=%async_computation.2 | async-start | bytes 4194304 | tf_op jit(solution)/shard_map/all_to_all | solution.py:224
  75.8 3.5 %collective-permute-start.3 = (s32[128,2]{1,0:T(8,128)S(1)}, s32[128,2]{1,0:T(8,128)S(1)}, u32[]{:S(2)}, u32[]{:S(2)}) collective-permute-start(s32[128,2]{1,0:T(8,128)S(1)} %copy-done.15), channel_id=1, source_target_pairs={{0,8},{4,12},{8,0},{12,4},{1,9},{5,13},{9,1},{13,5},{2,10},{6,14},... | collective-permute-start | bytes 3080 | tf_op jit(solution)/shard_map/ppermute | solution.py:270
  79.3 3.4 %collective-permute-done.2.refs_1_ = s32[128,2]{1,0:T(8,128)S(1)} collective-permute-done((s32[128,2]{1,0:T(8,128)S(1)}, s32[128,2]{1,0:T(8,128)S(1)}, u32[]{:S(2)}, u32[]{:S(2)}) %collective-permute-start.2) | collective-permute-done | bytes 1056 | tf_op jit(solution)/shard_map/ppermute | solution.py:270
  82.7 3.1 %collective-permute-done.3.refs_2_ = s32[128,2]{1,0:T(8,128)S(1)} collective-permute-done((s32[128,2]{1,0:T(8,128)S(1)}, s32[128,2]{1,0:T(8,128)S(1)}, u32[]{:S(2)}, u32[]{:S(2)}) %collective-permute-start.3) | collective-permute-done | bytes 1056 | tf_op jit(solution)/shard_map/ppermute | solution.py:270
  85.9 7.7 %collective-permute-done.4.refs_3_ = s32[128,2]{1,0:T(8,128)S(1)} collective-permute-done((s32[128,2]{1,0:T(8,128)S(1)}, s32[128,2]{1,0:T(8,128)S(1)}, u32[]{:S(2)}, u32[]{:S(2)}) %collective-permute-start.4) | collective-permute-done | bytes 1056 | tf_op jit(solution)/shard_map/ppermute | solution.py:270
  95.2 2.4 %combine_body.2 = bf16[512,2048]{1,0:T(8,128)(2,1)S(1)} custom-call(s32[3]{0:T(128)S(1)} %pad_add_fusion.place, s32[2,128]{1,0:T(2,128)S(1)} %get-tuple-element.30.refs_0_, s32[2,128]{1,0:T(2,128)S(1)} %get-tuple-element.31.refs_1_, s32[2,128]{1,0:T(2,128)S(1)} %get-tuple-element.32.refs_2_, s32[2,128]{1,0:T(2,128)S(1)} %get-tuple-element.33.refs_3_, ...), custom_call_target="tpu_custom_call" | custom-call | tf_op jit(solution)/shard_map/combine_body/pallas_call | solution.py:28
  99.7 2.4 %combine_body.3 = bf16[512,2048]{1,0:T(8,128)(2,1)S(1)} custom-call(s32[3]{0:T(128)S(1)} %pad_add_fusion.place, s32[2,128]{1,0:T(2,128)S(1)} %get-tuple-element.30.refs_0_, s32[2,128]{1,0:T(2,128)S(1)} %get-tuple-element.31.refs_1_, s32[2,128]{1,0:T(2,128)S(1)} %get-tuple-element.32.refs_2_, s32[2,128]{1,0:T(2,128)S(1)} %get-tuple-element.33.refs_3_, ...), custom_call_target="tpu_custom_call" | custom-call | tf_op jit(solution)/shard_map/combine_body/pallas_call | solution.py:28
  103.4 2.3 %all-gather.2.cloned.1.call-done.refs_4_ = bf16[512,4096]{1,0:T(8,128)(2,1)} async-done(((bf16[128,4096]{1,0:T(8,128)(2,1)}), bf16[512,4096]{1,0:T(8,128)(2,1)}) %all-gather.2.cloned.1.call-update) | async-done | bytes 4194320 | tf_op jit(solution)/shard_map/all_gather | solution.py:264
  105.7 2.2 copy-done.16
  110.5 5.1 %all-to-all-start.3 = ((bf16[4,128,2048]{2,1,0:T(8,128)(2,1)}), bf16[4,128,2048]{2,1,0:T(8,128)(2,1)}, u32[]{:S(2)}, u32[]{:S(2)}) async-start(bf16[4,128,2048]{2,1,0:T(8,128)(2,1)} %bitcast.28), calls=%async_computation.5 | async-start | bytes 4194304 | tf_op jit(solution)/shard_map/all_to_all | solution.py:224
  115.6 2.5 %copy-done.17 = bf16[512,4096]{1,0:T(8,128)(2,1)S(1)} copy-done((bf16[512,4096]{1,0:T(8,128)(2,1)S(1)}, bf16[512,4096]{1,0:T(8,128)(2,1)}, u32[]{:S(2)}) %copy-start.17) | copy-done | bytes 4194328
  120.7 18.8 %all-to-all-done.3 = bf16[4,128,2048]{2,1,0:T(8,128)(2,1)} async-done(((bf16[4,128,2048]{2,1,0:T(8,128)(2,1)}), bf16[4,128,2048]{2,1,0:T(8,128)(2,1)}, u32[]{:S(2)}, u32[]{:S(2)}) %all-to-all-start.3) | async-done | bytes 2097184 | tf_op jit(solution)/shard_map/all_to_all | solution.py:224
  139.5 6.3 %all-to-all-start.4 = ((bf16[4,128,2048]{2,1,0:T(8,128)(2,1)}), bf16[4,128,2048]{2,1,0:T(8,128)(2,1)}, u32[]{:S(2)}, u32[]{:S(2)}) async-start(bf16[4,128,2048]{2,1,0:T(8,128)(2,1)} %bitcast.27), calls=%async_computation.6 | async-start | bytes 4194304 | tf_op jit(solution)/shard_map/all_to_all | solution.py:224
  146.6 3.3 %weight_grad_body.4 = bf16[256,2048]{1,0:T(8,128)(2,1)} custom-call(s32[3]{0:T(128)S(1)} %pad_add_fusion.place, bf16[512,512]{1,0:T(8,128)(2,1)S(1)} %arrange_body.1.hid_ref, bf16[512,2048]{1,0:T(8,128)(2,1)} %bitcast.11.grad_ref), custom_call_target="tpu_custom_call" | custom-call | tf_op jit(solution)/shard_map/weight_grad_body/pallas_call | solution.py:28
  150.8 2.3 %weight_grad_body.5 = bf16[256,2048]{1,0:T(8,128)(2,1)S(1)} custom-call(s32[3]{0:T(128)S(1)} %pad_add_fusion.place, bf16[512,512]{1,0:T(8,128)(2,1)S(1)} %arrange_body.1.hid_ref, bf16[512,2048]{1,0:T(8,128)(2,1)} %bitcast.11.grad_ref), custom_call_target="tpu_custom_call" | custom-call | tf_op jit(solution)/shard_map/weight_grad_body/pallas_call | solution.py:28
  154.2 3.1 %backward_first_body.1.first_ref = f32[512,512]{1,0:T(8,128)S(1)} custom-call(s32[3]{0:T(128)S(1)} %pad_add_fusion.place, bf16[512,2048]{1,0:T(8,128)(2,1)} %bitcast.11.grad_ref, bf16[256,4096]{1,0:T(8,128)(2,1)S(1)} %bitcast.24, bf16[256,2048]{1,0:T(8,128)(2,1)} %collective-permute-done.refs_1_), custom_call_target="tpu_custom_call" | custom-call | tf_op jit(solution)/shard_map/backward_first_body/pallas_call | solution.py:28
  158.3 11.4 %all-to-all-done.4 = bf16[4,128,2048]{2,1,0:T(8,128)(2,1)} async-done(((bf16[4,128,2048]{2,1,0:T(8,128)(2,1)}), bf16[4,128,2048]{2,1,0:T(8,128)(2,1)}, u32[]{:S(2)}, u32[]{:S(2)}) %all-to-all-start.4) | async-done | bytes 2097184 | tf_op jit(solution)/shard_map/all_to_all | solution.py:224
  169.7 3.4 %weight_grad_body.6 = bf16[256,2048]{1,0:T(8,128)(2,1)} custom-call(s32[3]{0:T(128)S(1)} %pad_add_fusion.place, bf16[512,512]{1,0:T(8,128)(2,1)S(1)} %arrange_body.1.hid_ref, bf16[512,2048]{1,0:T(8,128)(2,1)} %bitcast.13.grad_ref), custom_call_target="tpu_custom_call" | custom-call | tf_op jit(solution)/shard_map/weight_grad_body/pallas_call | solution.py:28
  174.1 4.0 %backward_last_body.1 = bf16[512,512]{1,0:T(8,128)(2,1)} custom-call(s32[3]{0:T(128)S(1)} %pad_add_fusion.place, f32[512,512]{1,0:T(8,128)S(1)} %copy-done.5, bf16[512,2048]{1,0:T(8,128)(2,1)} %bitcast.13.grad_ref, bf16[256,4096]{1,0:T(8,128)(2,1)S(1)} %bitcast.25, bf16[256,2048]{1,0:T(8,128)(2,1)} %collective-permute-done.1.refs_1_), custom_call_target="tpu_custom_call" | custom-call | tf_op jit(solution)/shard_map/backward_last_body/pallas_call | solution.py:28
  178.1 2.3 %weight_grad_body.7 = bf16[256,2048]{1,0:T(8,128)(2,1)S(1)} custom-call(s32[3]{0:T(128)S(1)} %pad_add_fusion.place, bf16[512,512]{1,0:T(8,128)(2,1)S(1)} %arrange_body.1.hid_ref, bf16[512,2048]{1,0:T(8,128)(2,1)} %bitcast.13.grad_ref), custom_call_target="tpu_custom_call" | custom-call | flops 274877906944 | tf_op jit(solution)/shard_map/weight_grad_body/pallas_call | solution.py:28
  181.4 9.4 %all-to-all-start.5 = ((bf16[16,32,512]{2,1,0:T(8,128)(2,1)}), bf16[16,32,512]{2,1,0:T(8,128)(2,1)S(1)}, u32[]{:S(2)}, u32[]{:S(2)}) async-start(bf16[16,32,512]{2,1,0:T(8,128)(2,1)} %bitcast.14), calls=%async_computation.7 | async-start | bytes 1048576 | tf_op jit(solution)/shard_map/all_to_all | solution.py:224
  192.8 4.8 %collective-permute-done.6 = bf16[256,2048]{1,0:T(8,128)(2,1)} collective-permute-done((bf16[256,2048]{1,0:T(8,128)(2,1)}, bf16[256,2048]{1,0:T(8,128)(2,1)}, u32[]{:S(2)}, u32[]{:S(2)}) %collective-permute-start.6) | collective-permute-done | bytes 1048608 | tf_op jit(solution)/shard_map/ppermute | solution.py:249
  200.7 7.9 %all-to-all-done.5 = bf16[16,32,512]{2,1,0:T(8,128)(2,1)S(1)} async-done(((bf16[16,32,512]{2,1,0:T(8,128)(2,1)}), bf16[16,32,512]{2,1,0:T(8,128)(2,1)S(1)}, u32[]{:S(2)}, u32[]{:S(2)}) %all-to-all-start.5) | async-done | bytes 524320 | tf_op jit(solution)/shard_map/all_to_all | solution.py:224
  (74 shorter events, 31.0 us)
Async XLA Ops:
  7.2 3.7 %copy-start.20 = (s32[128,2]{0,1:T(2,128)S(1)}, s32[128,2]{0,1:T(2,128)}, u32[]{:S(2)}) copy-start(s32[128,2]{0,1:T(2,128)} %param.7) | copy-start | bytes 3076
  7.2 3.8 %copy-start.21 = (s32[128,2]{0,1:T(2,128)S(1)}, s32[128,2]{0,1:T(2,128)}, u32[]{:S(2)}) copy-start(s32[128,2]{0,1:T(2,128)} %param.8) | copy-start | bytes 3076
  7.2 4.0 %copy-start.19 = (bf16[128,2,512]{2,1,0:T(2,128)(2,1)S(1)}, bf16[128,2,512]{2,1,0:T(2,128)(2,1)}, u32[]{:S(2)}) copy-start(bf16[128,2,512]{2,1,0:T(2,128)(2,1)} %param.5) | copy-start | bytes 786436
  7.2 13.1 %copy-start = (bf16[1,256,4096]{2,1,0:T(8,128)(2,1)S(1)}, bf16[1,256,4096]{2,1,0:T(8,128)(2,1)}, u32[]{:S(2)}) copy-start(bf16[1,256,4096]{2,1,0:T(8,128)(2,1)} %param.9) | copy-start | bytes 6291460
  9.7 25.2 %collective-permute-start = (bf16[256,2048]{1,0:T(8,128)(2,1)}, bf16[256,2048]{1,0:T(8,128)(2,1)}, u32[]{:S(2)}, u32[]{:S(2)}) collective-permute-start(bf16[256,2048]{1,0:T(8,128)(2,1)} %slice.8), channel_id=1, source_target_pairs={{0,16},{16,0},{1,17},{17,1},{2,18},{18,2},{3,19},{19,3},{4,20},{20... | collective-permute-start | bytes 3145736 | tf_op jit(solution)/shard_map/ppermute | solution.py:249
  11.0 2.4 %copy-start.14 = (s32[128,2]{1,0:T(8,128)}, s32[128,2]{1,0:T(8,128)S(1)}, u32[]{:S(2)}) copy-start(s32[128,2]{1,0:T(8,128)S(1)} %copy.8.ids_ref.refs_0_) | copy-start | bytes 3076
  11.1 2.3 %copy-start.12 = (s32[128,2]{1,0:T(8,128)}, s32[128,2]{1,0:T(8,128)S(1)}, u32[]{:S(2)}) copy-start(s32[128,2]{1,0:T(8,128)S(1)} %copy.9.num_ref) | copy-start | bytes 3076
  13.4 20.8 %all-to-all-start = ((bf16[16,32,512]{2,1,0:T(8,128)(2,1)}), bf16[16,32,512]{2,1,0:T(8,128)(2,1)S(1)}, u32[]{:S(2)}, u32[]{:S(2)}) async-start(bf16[16,32,512]{2,1,0:T(8,128)(2,1)} %bitcast.3), calls=%async_computation | async-start | bytes 1048576 | tf_op jit(solution)/shard_map/all_to_all | solution.py:224
  20.3 85.4 %all-gather.2.cloned.1.call-start = ((), (), s32[]{:S(2)}) async-start(), calls=%async_computation.10 | async-start | bytes 5242880 | tf_op jit(solution)/shard_map/all_gather | solution.py:264
  21.4 35.1 %collective-permute-start.1 = (bf16[256,2048]{1,0:T(8,128)(2,1)}, bf16[256,2048]{1,0:T(8,128)(2,1)}, u32[]{:S(2)}, u32[]{:S(2)}) collective-permute-start(bf16[256,2048]{1,0:T(8,128)(2,1)} %slice.7), channel_id=1, source_target_pairs={{0,16},{16,0},{1,17},{17,1},{2,18},{18,2},{3,19},{19,3},{4,20},{20... | collective-permute-start | bytes 3145736 | tf_op jit(solution)/shard_map/ppermute | solution.py:249
  37.4 1.4 copy-start.9
  38.8 30.5 %all-to-all-start.1 = ((bf16[4,128,2048]{2,1,0:T(8,128)(2,1)}), bf16[4,128,2048]{2,1,0:T(8,128)(2,1)}, u32[]{:S(2)}, u32[]{:S(2)}) async-start(bf16[4,128,2048]{2,1,0:T(8,128)(2,1)} %bitcast.29), calls=%async_computation.1 | async-start | bytes 4194304 | tf_op jit(solution)/shard_map/all_to_all | solution.py:224
  69.3 6.5 %copy-start.15 = (s32[128,2]{1,0:T(8,128)S(1)}, s32[128,2]{1,0:T(8,128)}, u32[]{:S(2)}) copy-start(s32[128,2]{1,0:T(8,128)} %copy-done.14) | copy-start | bytes 3076
  69.3 30.4 %all-to-all-start.2 = ((bf16[4,128,2048]{2,1,0:T(8,128)(2,1)}), bf16[4,128,2048]{2,1,0:T(8,128)(2,1)}, u32[]{:S(2)}, u32[]{:S(2)}) async-start(bf16[4,128,2048]{2,1,0:T(8,128)(2,1)} %bitcast.26), calls=%async_computation.2 | async-start | bytes 4194304 | tf_op jit(solution)/shard_map/all_to_all | solution.py:224
  75.8 105.6 %reduce-scatter.3.cloned.1.call-start = ((), (), s32[]{:S(2)}) async-start(), calls=%async_computation.8 | async-start | bytes 2621440 | tf_op jit(solution)/shard_map/reduce_scatter | solution.py:284
  75.8 7.0 %collective-permute-start.2 = (s32[128,2]{1,0:T(8,128)S(1)}, s32[128,2]{1,0:T(8,128)S(1)}, u32[]{:S(2)}, u32[]{:S(2)}) collective-permute-start(s32[128,2]{1,0:T(8,128)S(1)} %copy-done.15), channel_id=1, source_target_pairs={{0,4},{4,0},{8,12},{12,8},{1,5},{5,1},{9,13},{13,9},{2,6},{6,2},{1... | collective-permute-start | bytes 3080 | tf_op jit(solution)/shard_map/ppermute | solution.py:270
  75.8 10.1 %collective-permute-start.3 = (s32[128,2]{1,0:T(8,128)S(1)}, s32[128,2]{1,0:T(8,128)S(1)}, u32[]{:S(2)}, u32[]{:S(2)}) collective-permute-start(s32[128,2]{1,0:T(8,128)S(1)} %copy-done.15), channel_id=1, source_target_pairs={{0,8},{4,12},{8,0},{12,4},{1,9},{5,13},{9,1},{13,5},{2,10},{6,14},... | collective-permute-start | bytes 3080 | tf_op jit(solution)/shard_map/ppermute | solution.py:270
  79.3 14.3 %collective-permute-start.4 = (s32[128,2]{1,0:T(8,128)S(1)}, s32[128,2]{1,0:T(8,128)S(1)}, u32[]{:S(2)}, u32[]{:S(2)}) collective-permute-start(s32[128,2]{1,0:T(8,128)S(1)} %copy-done.15), channel_id=1, source_target_pairs={{0,12},{4,8},{8,4},{12,0},{1,13},{5,9},{9,5},{13,1},{2,14},{6,10},... | collective-permute-start | bytes 3080 | tf_op jit(solution)/shard_map/ppermute | solution.py:270
  97.6 1.4 copy-start.2
  102.0 1.4 copy-start.1
  105.7 2.2 copy-start.16
  110.5 29.0 %all-to-all-start.3 = ((bf16[4,128,2048]{2,1,0:T(8,128)(2,1)}), bf16[4,128,2048]{2,1,0:T(8,128)(2,1)}, u32[]{:S(2)}, u32[]{:S(2)}) async-start(bf16[4,128,2048]{2,1,0:T(8,128)(2,1)} %bitcast.28), calls=%async_computation.5 | async-start | bytes 4194304 | tf_op jit(solution)/shard_map/all_to_all | solution.py:224
  115.6 2.5 %copy-start.17 = (bf16[512,4096]{1,0:T(8,128)(2,1)S(1)}, bf16[512,4096]{1,0:T(8,128)(2,1)}, u32[]{:S(2)}) copy-start(bf16[512,4096]{1,0:T(8,128)(2,1)} %all-gather.2.cloned.1.call-done.refs_4_) | copy-start | bytes 12582916
  139.5 30.2 %all-to-all-start.4 = ((bf16[4,128,2048]{2,1,0:T(8,128)(2,1)}), bf16[4,128,2048]{2,1,0:T(8,128)(2,1)}, u32[]{:S(2)}, u32[]{:S(2)}) async-start(bf16[4,128,2048]{2,1,0:T(8,128)(2,1)} %bitcast.27), calls=%async_computation.6 | async-start | bytes 4194304 | tf_op jit(solution)/shard_map/all_to_all | solution.py:224
  145.8 64.5 %reduce-scatter.5.cloned.1.call-start = ((), (), s32[]{:S(2)}) async-start(), calls=%async_computation.9 | async-start | bytes 2621440 | tf_op jit(solution)/shard_map/reduce_scatter | solution.py:284
  149.9 31.5 %collective-permute-start.5 = (bf16[256,2048]{1,0:T(8,128)(2,1)}, bf16[256,2048]{1,0:T(8,128)(2,1)}, u32[]{:S(2)}, u32[]{:S(2)}) collective-permute-start(bf16[256,2048]{1,0:T(8,128)(2,1)} %weight_grad_body.4), channel_id=1, source_target_pairs={{0,16},{16,0},{1,17},{17,1},{2,18},{18,2},{3,19},{19,3},{4,20},{20... | collective-permute-start | bytes 3145736 | tf_op jit(solution)/shard_map/ppermute | solution.py:249
  169.7 4.4 %copy-start.5 = (f32[512,512]{1,0:T(8,128)S(1)}, f32[512,512]{1,0:T(8,128)}, u32[]{:S(2)}) copy-start(f32[512,512]{1,0:T(8,128)} %copy-done.4) | copy-start | bytes 3145732
  173.1 24.4 %collective-permute-start.6 = (bf16[256,2048]{1,0:T(8,128)(2,1)}, bf16[256,2048]{1,0:T(8,128)(2,1)}, u32[]{:S(2)}, u32[]{:S(2)}) collective-permute-start(bf16[256,2048]{1,0:T(8,128)(2,1)} %weight_grad_body.6), channel_id=1, source_target_pairs={{0,16},{16,0},{1,17},{17,1},{2,18},{18,2},{3,19},{19,3},{4,20},{20... | collective-permute-start | bytes 3145736 | tf_op jit(solution)/shard_map/ppermute | solution.py:249
  181.4 16.2 %copy-start.11 = (bf16[256,2048]{1,0:T(8,128)(2,1)S(1)}, bf16[256,2048]{1,0:T(8,128)(2,1)}, u32[]{:S(2)}) copy-start(bf16[256,2048]{1,0:T(8,128)(2,1)} %copy-done.10) | copy-start | bytes 3145732
  181.4 27.2 %all-to-all-start.5 = ((bf16[16,32,512]{2,1,0:T(8,128)(2,1)}), bf16[16,32,512]{2,1,0:T(8,128)(2,1)S(1)}, u32[]{:S(2)}, u32[]{:S(2)}) async-start(bf16[16,32,512]{2,1,0:T(8,128)(2,1)} %bitcast.14), calls=%async_computation.7 | async-start | bytes 1048576 | tf_op jit(solution)/shard_map/all_to_all | solution.py:224
  199.2 9.4 %copy-start.13 = (s32[128,2]{1,0:T(8,128)S(1)}, s32[128,2]{1,0:T(8,128)}, u32[]{:S(2)}) copy-start(s32[128,2]{1,0:T(8,128)} %copy-done.12) | copy-start | bytes 3076
  199.2 11.2 %copy-start.18 = (bf16[128,2048]{1,0:T(8,128)(2,1)S(1)}, bf16[128,2048]{1,0:T(8,128)(2,1)}, u32[]{:S(2)}) copy-start(bf16[128,2048]{1,0:T(8,128)(2,1)} %reduce-scatter.3.cloned.1.call-done) | copy-start | bytes 1572868
  (6 other events, 6.9 us)
Sparse Core Ops, SparseCore 0:
  22.7 82.9 all-gather.1
  108.0 43.1 reduce-scatter.2
  153.6 47.6 reduce-scatter.4
